TPU v7x, 32 devices: a whole 2x2x4 slice. The times are simulated.
32 devices in a mesh: groups: 2 (over y), dp: 4 (over z), tm: 2 (over core), rows: 2 (over x).
Axes of the slice: x: 2, y: 2, z: 4, core: 2. Of those that a mesh axis runs over, the one named last changes fastest.
Arguments:
- spikes: bfloat16 [8, 6, 16, 64, 320], P(('groups', 'dp'), 'tm', 'rows'), parts along dimension 0, may hold values from 0 to 1, as said below
- cotangent: bfloat16 [8, 6, 16, 64, 320], P(('groups', 'dp'), 'tm', 'rows'), parts along dimension 0, may hold values from -6 to 6
- weight_codes: int32 [3, 3, 320, 320], P(None, None, None, 'dp'), may hold values from -127 to 127
- block_exponents: int32 [3, 3, 10, 320], P(None, None, None, 'dp'), may hold values from -13 to -11
- current_bias: float32 [320], replicated, may hold values from -3 to 3
- threshold: float32 [320], replicated, may hold values from 0.5 to 1.5
Outputs:
- residual_output: bfloat16 [8, 6, 16, 64, 320], P(('groups', 'dp'), 'tm', 'rows'), parts along dimension 0
- input_grad: float32 [8, 6, 16, 64, 320], P(('groups', 'dp'), 'tm', 'rows'), parts along dimension 0
There are 2 independent parts, one for each index of `groups`. A program takes and returns all parts, laid end to end along the dimension named above; an argument that names none is the same for every part. Nothing has to cross between parts.
Inputs may be any that keep to these rules, and one draw needn't show every extreme that they name: `spikes`: every entry is 0 or 1.
All inputs are finite; a program needn't handle non-finite values.
Results may differ from a plain program's by a relative error of at most 0.002.
Values may be sent and summed in bfloat16 or wider, within the bound.
No kernel may reach another device: no remote copies, remote signals or barrier semaphores. Data moves between devices by JAX's collectives and lax.ppermute only.
A program may use at most 64 MiB of HBM per device.

v0:
```python
import jax
import jax.numpy as jnp
from jax import lax
from jax.sharding import PartitionSpec as P

MX_BLOCK = 32


surrogate_steepness = 2.0


def padded_2(cells, sides, width):
    for axis, dim in sides:
        count = lax.axis_size(axis)
        ends = count - 1
        head = lax.slice_in_dim(cells, 0, width, axis=dim)
        tail = lax.slice_in_dim(cells, cells.shape[dim] - width, cells.shape[dim], axis=dim)
        cells = jnp.concatenate(
            [
                lax.ppermute(tail, axis, [(i, (i + 1) % count) for i in range(ends)]),
                cells,
                lax.ppermute(head, axis, [((i + 1) % count, i) for i in range(ends)]),
            ],
            axis=dim,
        )
    return cells


def from_behind(value, axis, steps):
    count = lax.axis_size(axis)
    initial, last = (max(0, -steps), min(count, count - steps))
    return lax.ppermute(value, axis, [(source, source + steps) for source in range(initial, last)])


def dequantize(weight_codes, block_exponents):
    scales = 1.0 / (2 ** (-block_exponents)).astype(jnp.float32)
    scales = jnp.repeat(scales, MX_BLOCK, axis=2)
    return (weight_codes.astype(jnp.float32) * scales).astype(jnp.bfloat16)


def column_taps(array, columns, reverse_taps):
    padded = jnp.pad(array, ((0, 0), (0, 0), (0, 0), (1, 1), (0, 0)))
    if reverse_taps:
        return jnp.stack(
            [padded[:, :, :, 2 - offset : 2 - offset + columns] for offset in range(3)], axis=4
        )
    return jnp.stack([padded[:, :, :, offset : offset + columns] for offset in range(3)], axis=4)


def accumulate_charge(input_current, start_state, threshold):
    membrane_voltage = start_state
    collected = []
    for moment in range(input_current.shape[1]):
        potential = membrane_voltage + input_current[:, moment]
        spiking = jax.nn.sigmoid(surrogate_steepness * (potential - threshold))
        membrane_voltage = potential - threshold * spiking
        collected.append(spiking)
    return (jnp.stack(collected, axis=1), membrane_voltage)


def retreat(drive_term, carry_gain, adjoint_end):
    adjoint_now = adjoint_end
    step_count = drive_term.shape[1]
    collected = [None] * step_count
    for moment in reversed(range(step_count)):
        adjoint_now = drive_term[:, moment] + carry_gain[:, moment] * adjoint_now
        collected[moment] = adjoint_now
    return (jnp.stack(collected, axis=1), adjoint_now)


def on_device(spikes, cotangent, weight_codes, block_exponents, current_bias, threshold):
    weights = dequantize(weight_codes, block_exponents)
    rows_here = spikes.shape[2]
    columns = spikes.shape[3]
    rows_in = padded_2(spikes, (("rows", 2),), 1)
    shifted = column_taps(rows_in, columns, False)
    weight_piece = lax.all_gather(weights, "dp", axis=3, tiled=True)
    total = jnp.einsum(
        "btrwxi,xik->btrwk",
        shifted[:, :, 0:rows_here],
        weight_piece[0],
        preferred_element_type=jnp.float32,
    )
    for row_tap in range(1, 3):
        total = total + jnp.einsum(
            "btrwxi,xik->btrwk",
            shifted[:, :, row_tap : row_tap + rows_here],
            weight_piece[row_tap],
            preferred_element_type=jnp.float32,
        )
    input_current = total + current_bias
    blank_state = jnp.zeros(input_current.shape[:1] + input_current.shape[2:], jnp.float32)
    membrane_voltage = blank_state
    unused_value, final_state = accumulate_charge(input_current, membrane_voltage, threshold)
    membrane_voltage = from_behind(final_state.astype(jnp.bfloat16), "tm", 1).astype(
        final_state.dtype
    )
    fired_spikes, unused_value = accumulate_charge(input_current, membrane_voltage, threshold)
    residual_output = (fired_spikes + spikes.astype(jnp.float32)).astype(jnp.bfloat16)
    upstream = cotangent.astype(jnp.float32)
    surrogate_slopes = surrogate_steepness * fired_spikes * (1.0 - fired_spikes)
    drive_term = upstream * surrogate_slopes
    carry_gain = 1.0 - threshold * surrogate_slopes
    incoming = blank_state
    unused_value, adjoint_start = retreat(drive_term, carry_gain, incoming)
    incoming = from_behind(adjoint_start.astype(jnp.bfloat16), "tm", -1).astype(adjoint_start.dtype)
    current_grad, unused_value = retreat(drive_term, carry_gain, incoming)
    grad_rounded = current_grad.astype(jnp.bfloat16)
    grad_rows = padded_2(grad_rounded, (("rows", 2),), 1)
    grad_shifted = column_taps(grad_rows, columns, True)
    blank_grad = jnp.zeros(upstream.shape, jnp.float32)
    running = blank_grad
    weight_piece = lax.all_gather(weights, "dp", axis=3, tiled=True)
    for row_tap in range(3):
        running = running + jnp.einsum(
            "btrwxk,xik->btrwi",
            grad_shifted[:, :, 2 - row_tap : 2 - row_tap + rows_here],
            weight_piece[row_tap],
            preferred_element_type=jnp.float32,
        )
    input_grad = upstream + running
    return (residual_output, input_grad)


def solution(mesh):
    return jax.shard_map(
        on_device,
        mesh=mesh,
        in_specs=(
            P(("groups", "dp"), "tm", "rows", None, None),
            P(("groups", "dp"), "tm", "rows", None, None),
            P(None, None, None, "dp"),
            P(None, None, None, "dp"),
            P(),
            P(),
        ),
        out_specs=(
            P(("groups", "dp"), "tm", "rows", None, None),
            P(("groups", "dp"), "tm", "rows", None, None),
        ),
        check_vma=False,
    )
```

profile of v0, /device:TPU:0, one launch (start us, length us, event | category | flops | bytes accessed | tf_op | source)
XLA Modules:
  0.0 113.3 jit_solution(15283733149829473557)
XLA Ops:
  8.2 1.5 %copy.41 = f32[3,3,320,80]{2,3,1,0:T(8,128)} copy(f32[3,3,320,80]{3,2,1,0:T(8,128)S(1)} %bitcast.198) | data formatting | bytes 1843200 | tf_op jit(solution)/shard_map/reshape | solution.py:37
  9.8 2.5 %multiply_convert_fusion = bf16[3,3,320,80]{2,3,1,0:T(8,128)(2,1)} fusion(f32[3,3,320,80]{2,3,1,0:T(8,128)} %copy.41, s32[3,3,320,80]{2,3,1,0:T(8,128)} %param.8), kind=kLoop, calls=%fused_computation.38 | loop fusion | flops 691200 | bytes 2304000 | tf_op jit(solution)/shard_map/convert_element_type | solution.py:38
  12.3 4.9 %collective-permute-start = (bf16[1,3,1,64,320]{4,3,2,1,0:T(8,128)(2,1)S(1)}, bf16[1,3,1,64,320]{4,3,2,1,0:T(8,128)(2,1)S(1)}, u32[]{:S(2)}, u32[]{:S(2)}) collective-permute-start(bf16[1,3,1,64,320]{4,3,2,1,0:T(8,128)(2,1)S(1)} %get-tuple-element.21), channel_id=1, source_target_pairs={{0,1},{2,3},{4,5},{6,7},{8,9},{10,11},{12,13},{14,15},{16,17},{18,... | collective-permute-start | bytes 368648 | tf_op jit(solution)/shard_map/ppermute | solution.py:20
  17.2 1.3 %collective-permute-start.1 = (bf16[1,3,1,64,320]{4,3,2,1,0:T(8,128)(2,1)S(1)}, bf16[1,3,1,64,320]{4,3,2,1,0:T(8,128)(2,1)S(1)}, u32[]{:S(2)}, u32[]{:S(2)}) collective-permute-start(bf16[1,3,1,64,320]{4,3,2,1,0:T(8,128)(2,1)S(1)} %get-tuple-element.20), channel_id=1, source_target_pairs={{1,0},{3,2},{5,4},{7,6},{9,8},{11,10},{13,12},{15,14},{17,16},{19,... | collective-permute-start | bytes 368648 | tf_op jit(solution)/shard_map/ppermute | solution.py:22
  18.5 1.8 %collective-permute-done = bf16[1,3,1,64,320]{4,3,2,1,0:T(8,128)(2,1)S(1)} collective-permute-done((bf16[1,3,1,64,320]{4,3,2,1,0:T(8,128)(2,1)S(1)}, bf16[1,3,1,64,320]{4,3,2,1,0:T(8,128)(2,1)S(1)}, u32[]{:S(2)}, u32[]{:S(2)}) %collective-permute-start) | collective-permute-done | bytes 122912 | tf_op jit(solution)/shard_map/ppermute | solution.py:20
  20.6 3.8 %collective-permute-done.1 = bf16[1,3,1,64,320]{4,3,2,1,0:T(8,128)(2,1)S(1)} collective-permute-done((bf16[1,3,1,64,320]{4,3,2,1,0:T(8,128)(2,1)S(1)}, bf16[1,3,1,64,320]{4,3,2,1,0:T(8,128)(2,1)S(1)}, u32[]{:S(2)}, u32[]{:S(2)}) %collective-permute-start.1) | collective-permute-done | bytes 122912 | tf_op jit(solution)/shard_map/ppermute | solution.py:22
  25.4 2.5 %pad_maximum_fusion = bf16[1,3,10,64,3,320]{5,3,4,2,1,0:T(8,128)(2,1)} fusion(bf16[1,3,10,64,1,320]{5,3,4,2,1,0:T(8,128)(2,1)S(1)} %get-tuple-element.17, bf16[1,3,10,64,1,320]{5,3,4,2,1,0:T(8,128)(2,1)S(1)} %bitcast.194, bf16[1,3,10,64,1,320]{5,3,4,2,1,0:T(8,128)(2,1)S(1)} %get-tuple-element.16), kind=kLoop, calls=%fused_computation | loop fusion | flops 3686400 | bytes 7372800 | tf_op jit(solution)/shard_map/stack | solution.py:47
  27.9 35.2 %all-gather.2.cloned.1.call-done = bf16[3,3,320,320]{2,3,1,0:T(8,128)(2,1)} async-done(((bf16[3,3,320,80]{2,3,1,0:T(8,128)(2,1)}), bf16[3,3,320,320]{2,3,1,0:T(8,128)(2,1)}) %all-gather.2.cloned.1.call-update) | async-done | bytes 1843216 | tf_op jit(solution)/shard_map/all_gather | solution.py:77
  63.1 4.5 %fusion.1 = f32[3,8,64,320,1]{3,2,4,1,0:T(8,128)S(1)} fusion(bf16[1,3,10,64,3,320]{5,3,4,2,1,0:T(8,128)(2,1)} %pad_maximum_fusion, bf16[3,3,320,320]{2,3,1,0:T(8,128)(2,1)} %all-gather.2.cloned.1.call-done), kind=kOutput, calls=%fused_computation.8 | convolution fusion | flops 943718400 | bytes 6242304 | tf_op jit(solution)/shard_map/btrwxi,xik->btrwk/dot_general | solution.py:85
  67.6 2.1 %fusion.2 = f32[3,8,64,320,1]{3,2,4,1,0:T(8,128)S(1)} fusion(bf16[1,3,10,64,3,320]{5,3,4,2,1,0:T(8,128)(2,1)S(1)} %copy-done.2, bf16[3,3,320,320]{2,3,1,0:T(8,128)(2,1)S(1)} %copy-done.4), kind=kOutput, calls=%fused_computation.10 | convolution fusion | flops 943718400 | bytes 6242304 | tf_op jit(solution)/shard_map/btrwxi,xik->btrwk/dot_general | solution.py:78
  69.8 2.3 %fusion.10 = f32[1,3,8,64,320]{4,3,2,1,0:T(8,128)S(1)} fusion(f32[3,8,64,320,1]{3,2,4,1,0:T(8,128)S(1)} %fusion.1, f32[3,8,64,320,1]{3,2,4,1,0:T(8,128)S(1)} %fusion.2, bf16[1,3,10,64,3,320]{5,3,4,2,1,0:T(8,128)(2,1)S(1)} %copy-done.2, f32[320]{0:T(512)S(1)} %copy-done.5, bf16[3,3,320,320]{2,3,1,0:T(8,128)(2,1)S(1)} %copy-done.4), kind=kOutput, calls=%fused_computation.24 | convolution fusion | flops 945192960 | bytes 10962944 | tf_op jit(solution)/shard_map/btrwxi,xik->btrwk/dot_general | solution.py:85
  72.9 2.1 %collective-permute-start.2 = (bf16[1,8,64,320]{3,2,1,0:T(8,128)(2,1)S(1)}, bf16[1,8,64,320]{3,2,1,0:T(8,128)(2,1)S(1)}, u32[]{:S(2)}, u32[]{:S(2)}) collective-permute-start(bf16[1,8,64,320]{3,2,1,0:T(8,128)(2,1)S(1)} %subtract_convert_fusion), channel_id=1, source_target_pairs={{0,2},{1,3},{4,6},{5,7},{8,10},{9,11},{12,14},{13,15},{16,18},{17,... | collective-permute-start | bytes 983048 | tf_op jit(solution)/shard_map/ppermute | solution.py:32
  77.1 1.8 %multiply_subtract_fusion = (f32[1,3,8,64,320]{4,3,2,1,0:T(8,128)S(1)}, f32[1,3,8,64,320]{4,3,2,1,0:T(8,128)S(1)}, bf16[1,3,8,64,320]{4,3,2,1,0:T(8,128)(2,1)}) fusion(f32[320]{0:T(512)S(1)} %copy-done.3, f32[1,1,8,64,320]{4,3,2,1,0:T(8,128)S(1)} %divide_bitcast_fusion, f32[1,1,8,64,320]{4,3,2,1,0:T(8,128)S(1)} %get-tuple-element.4, ...), kind=kLoop, calls=%fused_computation.26 | loop fusion | flops 5898240 | bytes 8848640 | tf_op jit(solution)/shard_map/sub | solution.py:103
  79.3 1.3 %collective-permute-start.3 = (bf16[1,8,64,320]{3,2,1,0:T(8,128)(2,1)S(1)}, bf16[1,8,64,320]{3,2,1,0:T(8,128)(2,1)S(1)}, u32[]{:S(2)}, u32[]{:S(2)}) collective-permute-start(bf16[1,8,64,320]{3,2,1,0:T(8,128)(2,1)S(1)} %add_convert_fusion.2), channel_id=1, source_target_pairs={{2,0},{3,1},{6,4},{7,5},{10,8},{11,9},{14,12},{15,13},{18,16},{19,... | collective-permute-start | bytes 983048 | tf_op jit(solution)/shard_map/ppermute | solution.py:32
  80.6 2.3 %collective-permute-done.3 = bf16[1,8,64,320]{3,2,1,0:T(8,128)(2,1)S(1)} collective-permute-done((bf16[1,8,64,320]{3,2,1,0:T(8,128)(2,1)S(1)}, bf16[1,8,64,320]{3,2,1,0:T(8,128)(2,1)S(1)}, u32[]{:S(2)}, u32[]{:S(2)}) %collective-permute-start.3) | collective-permute-done | bytes 327712 | tf_op jit(solution)/shard_map/ppermute | solution.py:32
  83.4 3.4 %collective-permute-start.4 = (bf16[1,3,1,64,320]{4,3,2,1,0:T(8,128)(2,1)S(1)}, bf16[1,3,1,64,320]{4,3,2,1,0:T(8,128)(2,1)S(1)}, u32[]{:S(2)}, u32[]{:S(2)}) collective-permute-start(bf16[1,3,1,64,320]{4,3,2,1,0:T(8,128)(2,1)S(1)} %get-tuple-element.18), channel_id=1, source_target_pairs={{0,1},{2,3},{4,5},{6,7},{8,9},{10,11},{12,13},{14,15},{16,17},{18,... | collective-permute-start | bytes 368648 | tf_op jit(solution)/shard_map/ppermute | solution.py:20
  86.8 1.3 %collective-permute-start.5 = (bf16[1,3,1,64,320]{4,3,2,1,0:T(8,128)(2,1)S(1)}, bf16[1,3,1,64,320]{4,3,2,1,0:T(8,128)(2,1)S(1)}, u32[]{:S(2)}, u32[]{:S(2)}) collective-permute-start(bf16[1,3,1,64,320]{4,3,2,1,0:T(8,128)(2,1)S(1)} %get-tuple-element.19), channel_id=1, source_target_pairs={{1,0},{3,2},{5,4},{7,6},{9,8},{11,10},{13,12},{15,14},{17,16},{19,... | collective-permute-start | bytes 368648 | tf_op jit(solution)/shard_map/ppermute | solution.py:22
  88.1 2.1 %collective-permute-done.4 = bf16[1,3,1,64,320]{4,3,2,1,0:T(8,128)(2,1)S(1)} collective-permute-done((bf16[1,3,1,64,320]{4,3,2,1,0:T(8,128)(2,1)S(1)}, bf16[1,3,1,64,320]{4,3,2,1,0:T(8,128)(2,1)S(1)}, u32[]{:S(2)}, u32[]{:S(2)}) %collective-permute-start.4) | collective-permute-done | bytes 122912 | tf_op jit(solution)/shard_map/ppermute | solution.py:20
  90.2 4.1 %collective-permute-done.5 = bf16[1,3,1,64,320]{4,3,2,1,0:T(8,128)(2,1)S(1)} collective-permute-done((bf16[1,3,1,64,320]{4,3,2,1,0:T(8,128)(2,1)S(1)}, bf16[1,3,1,64,320]{4,3,2,1,0:T(8,128)(2,1)S(1)}, u32[]{:S(2)}, u32[]{:S(2)}) %collective-permute-start.5) | collective-permute-done | bytes 122912 | tf_op jit(solution)/shard_map/ppermute | solution.py:22
  97.1 1.7 %slice_bitcast_fusion.2 = (bf16[3,8,64,3,320]{4,2,1,0,3:T(8,128)(2,1)S(1)}, bf16[3,8,64,3,320]{4,2,1,0,3:T(8,128)(2,1)S(1)}, bf16[3,8,64,3,320]{4,2,1,0,3:T(8,128)(2,1)S(1)}) fusion(bf16[1,3,10,64,3,320]{5,3,2,1,4,0:T(8,128)(2,1)S(1)} %pad_maximum_fusion.1), kind=kLoop, calls=%fused_computation.4 | loop fusion | bytes 17694720 | tf_op jit(solution)/shard_map/reshape.13
  98.8 1.8 %fusion.7 = f32[3,8,64,320,1]{3,2,0,1,4:T(8,128)S(1)} fusion(bf16[3,8,64,3,320]{4,2,1,0,3:T(8,128)(2,1)S(1)} %get-tuple-element.7, bf16[3,3,320,320]{2,3,1,0:T(8,128)(2,1)S(1)} %copy-done.4), kind=kOutput, calls=%fused_computation.15 | convolution fusion | flops 943718400 | bytes 6242304 | tf_op jit(solution)/shard_map/btrwxk,xik->btrwi/dot_general | solution.py:115
  100.6 1.8 %fusion.3 = f32[3,8,64,320,1]{3,2,0,1,4:T(8,128)S(1)} fusion(bf16[3,8,64,3,320]{4,2,1,0,3:T(8,128)(2,1)S(1)} %get-tuple-element.8, bf16[3,3,320,320]{2,3,1,0:T(8,128)(2,1)S(1)} %copy-done.4), kind=kOutput, calls=%fused_computation.11 | convolution fusion | flops 943718400 | bytes 6242304 | tf_op jit(solution)/shard_map/btrwxk,xik->btrwi/dot_general | solution.py:115
  102.4 1.8 %fusion.5 = f32[3,8,64,320,1]{3,2,0,1,4:T(8,128)S(1)} fusion(bf16[3,8,64,3,320]{4,2,1,0,3:T(8,128)(2,1)S(1)} %get-tuple-element.9, bf16[3,3,320,320]{2,3,1,0:T(8,128)(2,1)S(1)} %copy-done.4), kind=kOutput, calls=%fused_computation.13 | convolution fusion | flops 943718400 | bytes 6242304 | tf_op jit(solution)/shard_map/btrwxk,xik->btrwi/dot_general | solution.py:115
  104.2 2.2 %convert_add_fusion = f32[1,3,8,64,320]{4,3,2,1,0:T(8,128)} fusion(bf16[1,3,8,64,320]{4,3,2,1,0:T(8,128)(2,1)S(1)} %copy-done.1, f32[3,8,64,320,1]{3,2,0,1,4:T(8,128)S(1)} %fusion.3, f32[3,8,64,320,1]{3,2,0,1,4:T(8,128)S(1)} %fusion.5, f32[3,8,64,320,1]{3,2,0,1,4:T(8,128)S(1)} %fusion.7), kind=kLoop, calls=%fused_computation.17 | loop fusion | flops 1966080 | bytes 8847360 | tf_op jit(solution)/shard_map/add | solution.py:121
  (32 shorter events, 8.8 us)
Async XLA Ops:
  7.2 56.0 %all-gather.2.cloned.1.call-start = ((), (), s32[]{:S(2)}) async-start(), calls=%async_computation | async-start | bytes 2764800 | tf_op jit(solution)/shard_map/all_gather | solution.py:77
  8.2 4.0 %copy-start = (bf16[1,3,8,64,320]{4,3,2,1,0:T(8,128)(2,1)S(1)}, bf16[1,3,8,64,320]{4,3,2,1,0:T(8,128)(2,1)}, u32[]{:S(2)}) copy-start(bf16[1,3,8,64,320]{4,3,2,1,0:T(8,128)(2,1)} %param.6) | copy-start | bytes 2949124
  12.3 8.0 %collective-permute-start = (bf16[1,3,1,64,320]{4,3,2,1,0:T(8,128)(2,1)S(1)}, bf16[1,3,1,64,320]{4,3,2,1,0:T(8,128)(2,1)S(1)}, u32[]{:S(2)}, u32[]{:S(2)}) collective-permute-start(bf16[1,3,1,64,320]{4,3,2,1,0:T(8,128)(2,1)S(1)} %get-tuple-element.21), channel_id=1, source_target_pairs={{0,1},{2,3},{4,5},{6,7},{8,9},{10,11},{12,13},{14,15},{16,17},{18,... | collective-permute-start | bytes 368648 | tf_op jit(solution)/shard_map/ppermute | solution.py:20
  17.2 7.2 %collective-permute-start.1 = (bf16[1,3,1,64,320]{4,3,2,1,0:T(8,128)(2,1)S(1)}, bf16[1,3,1,64,320]{4,3,2,1,0:T(8,128)(2,1)S(1)}, u32[]{:S(2)}, u32[]{:S(2)}) collective-permute-start(bf16[1,3,1,64,320]{4,3,2,1,0:T(8,128)(2,1)S(1)} %get-tuple-element.20), channel_id=1, source_target_pairs={{1,0},{3,2},{5,4},{7,6},{9,8},{11,10},{13,12},{15,14},{17,16},{19,... | collective-permute-start | bytes 368648 | tf_op jit(solution)/shard_map/ppermute | solution.py:22
  63.1 4.5 %copy-start.2 = (bf16[1,3,10,64,3,320]{5,3,4,2,1,0:T(8,128)(2,1)S(1)}, bf16[1,3,10,64,3,320]{5,3,4,2,1,0:T(8,128)(2,1)}, u32[]{:S(2)}) copy-start(bf16[1,3,10,64,3,320]{5,3,4,2,1,0:T(8,128)(2,1)} %pad_maximum_fusion) | copy-start | bytes 11059204
  63.1 4.5 %copy-start.4 = (bf16[3,3,320,320]{2,3,1,0:T(8,128)(2,1)S(1)}, bf16[3,3,320,320]{2,3,1,0:T(8,128)(2,1)}, u32[]{:S(2)}) copy-start(bf16[3,3,320,320]{2,3,1,0:T(8,128)(2,1)} %all-gather.2.cloned.1.call-done) | copy-start | bytes 5529604
  67.6 2.2 %copy-start.5 = (f32[320]{0:T(512)S(1)}, f32[320]{0:T(512)}, u32[]{:S(2)}) copy-start(f32[320]{0:T(512)} %param.10) | copy-start | bytes 3844
  69.8 2.4 %copy-start.3 = (f32[320]{0:T(512)S(1)}, f32[320]{0:T(512)}, u32[]{:S(2)}) copy-start(f32[320]{0:T(512)} %param.11) | copy-start | bytes 3844
  72.9 4.2 %copy-start.1 = (bf16[1,3,8,64,320]{4,3,2,1,0:T(8,128)(2,1)S(1)}, bf16[1,3,8,64,320]{4,3,2,1,0:T(8,128)(2,1)}, u32[]{:S(2)}) copy-start(bf16[1,3,8,64,320]{4,3,2,1,0:T(8,128)(2,1)} %param.7) | copy-start | bytes 2949124
  72.9 3.2 %collective-permute-start.2 = (bf16[1,8,64,320]{3,2,1,0:T(8,128)(2,1)S(1)}, bf16[1,8,64,320]{3,2,1,0:T(8,128)(2,1)S(1)}, u32[]{:S(2)}, u32[]{:S(2)}) collective-permute-start(bf16[1,8,64,320]{3,2,1,0:T(8,128)(2,1)S(1)} %subtract_convert_fusion), channel_id=1, source_target_pairs={{0,2},{1,3},{4,6},{5,7},{8,10},{9,11},{12,14},{13,15},{16,18},{17,... | collective-permute-start | bytes 983048 | tf_op jit(solution)/shard_map/ppermute | solution.py:32
  79.3 3.6 %collective-permute-start.3 = (bf16[1,8,64,320]{3,2,1,0:T(8,128)(2,1)S(1)}, bf16[1,8,64,320]{3,2,1,0:T(8,128)(2,1)S(1)}, u32[]{:S(2)}, u32[]{:S(2)}) collective-permute-start(bf16[1,8,64,320]{3,2,1,0:T(8,128)(2,1)S(1)} %add_convert_fusion.2), channel_id=1, source_target_pairs={{2,0},{3,1},{6,4},{7,5},{10,8},{11,9},{14,12},{15,13},{18,16},{19,... | collective-permute-start | bytes 983048 | tf_op jit(solution)/shard_map/ppermute | solution.py:32
  83.4 6.8 %collective-permute-start.4 = (bf16[1,3,1,64,320]{4,3,2,1,0:T(8,128)(2,1)S(1)}, bf16[1,3,1,64,320]{4,3,2,1,0:T(8,128)(2,1)S(1)}, u32[]{:S(2)}, u32[]{:S(2)}) collective-permute-start(bf16[1,3,1,64,320]{4,3,2,1,0:T(8,128)(2,1)S(1)} %get-tuple-element.18), channel_id=1, source_target_pairs={{0,1},{2,3},{4,5},{6,7},{8,9},{10,11},{12,13},{14,15},{16,17},{18,... | collective-permute-start | bytes 368648 | tf_op jit(solution)/shard_map/ppermute | solution.py:20
  86.8 7.5 %collective-permute-start.5 = (bf16[1,3,1,64,320]{4,3,2,1,0:T(8,128)(2,1)S(1)}, bf16[1,3,1,64,320]{4,3,2,1,0:T(8,128)(2,1)S(1)}, u32[]{:S(2)}, u32[]{:S(2)}) collective-permute-start(bf16[1,3,1,64,320]{4,3,2,1,0:T(8,128)(2,1)S(1)} %get-tuple-element.19), channel_id=1, source_target_pairs={{1,0},{3,2},{5,4},{7,6},{9,8},{11,10},{13,12},{15,14},{17,16},{19,... | collective-permute-start | bytes 368648 | tf_op jit(solution)/shard_map/ppermute | solution.py:22
Sparse Core Ops, SparseCore 0:
  12.4 50.7 all-gather.1
where the time goes:
time: 114 us; the launch traced here: 113 us
  waiting for transfers between devices  50.5 us (44%)
  matrix products  14.4 us (13%)
  other arithmetic  14.3 us (13%)
  between operations  14.3 us (13%)
  starting transfers between devices  14.2 us (12%)
  local copies, waits for them, and re-layouts  5.57 us (5%)
    all_gather x1, waiting for transfers between devices, on_device(): weight_piece = lax.all_gather(weights, 'dp', axis=3, tiled=True)  35.2 us
    ppermute x2, starting transfers between devices, padded_2(): lax.ppermute(tail, axis, [(i, (i + 1) % count) for i in range(ends)])  8.24 us
    ppermute x2, waiting for transfers between devices, padded_2(): lax.ppermute(head, axis, [((i + 1) % count, i) for i in range(ends)])  7.97 us
    dot_general x2, matrix products, on_device(): jnp.einsum('btrwxi,xik->btrwk', shifted[:, :, row_tap:row_tap + rows_here...  6.8 us
    dot_general x3, matrix products, on_device(): jnp.einsum('btrwxk,xik->btrwi', grad_shifted[:, :, 2 - row_tap:2 - row_ta...  5.42 us
    ppermute x2, waiting for transfers between devices, padded_2(): lax.ppermute(tail, axis, [(i, (i + 1) % count) for i in range(ends)])  3.89 us
    ppermute x2, waiting for transfers between devices, from_behind(): lax.ppermute(value, axis, [(source, source + steps) for source in range(i...  3.44 us
    ppermute x2, starting transfers between devices, from_behind(): lax.ppermute(value, axis, [(source, source + steps) for source in range(i...  3.37 us
  transfers between devices with their start and end apart: 7, of which 7 were waited for; matrix products, arithmetic and copies ran while one was open for 3% of the time, Pallas kernels for 0%

commit v1 on v0

v1 whole, which is shorter than its diff:
```python
import functools

import jax
import jax.numpy as jnp
from jax import lax
from jax.experimental import pallas as pl
from jax.experimental.pallas import tpu as pltpu
from jax.sharding import PartitionSpec as P

MX_BLOCK = 32
TAPS = 3
F32 = jnp.float32
BF16 = jnp.bfloat16
VMEM_SPEC = pl.BlockSpec(memory_space=pltpu.VMEM)
ANY_SPEC = pl.BlockSpec(memory_space=pl.ANY)


def params(mib):
    return pltpu.CompilerParams(vmem_limit_bytes=mib << 20)


def dot(a, b, dims):
    return lax.dot_general(a, b, (dims, ((), ())), preferred_element_type=F32)


def dequant_kernel(codes_ref, exps_ref, out_ref):
    outs, ins = codes_ref.shape[2:]
    blocks = exps_ref.shape[1]
    spread = lax.broadcasted_iota(jnp.int32, (blocks, ins), 1) // MX_BLOCK
    spread = (spread == lax.broadcasted_iota(jnp.int32, (blocks, ins), 0)).astype(F32).astype(BF16)
    for dy in range(TAPS):
        parts = []
        for dx in range(TAPS):
            scale = 1.0 / lax.shift_left(jnp.int32(1), -exps_ref[dy, :, dx, :]).astype(F32)
            scale = dot(scale.astype(BF16), spread, ((0,), (0,)))
            parts.append(codes_ref[dy, dx].astype(F32) * scale)
        parts.append(jnp.zeros((outs, out_ref.shape[1] - TAPS * ins), F32))
        out_ref[dy * outs : (dy + 1) * outs, :] = jnp.concatenate(parts, axis=1).astype(BF16)


def dequantize(weight_codes, block_exponents, lanes):
    outs = weight_codes.shape[3]
    return pl.pallas_call(
        dequant_kernel,
        out_shape=jax.ShapeDtypeStruct((TAPS * outs, lanes), BF16),
        in_specs=[VMEM_SPEC] * 2,
        out_specs=VMEM_SPEC,
        compiler_params=params(16),
        name="dequant",
    )(weight_codes.transpose(0, 1, 3, 2), block_exponents.transpose(0, 2, 1, 3))


def strip_offsets(two, row):
    if two:
        return 1 + row, ((1 - row) * 0, row)
    return 2, None


def taps_kernel(two, spikes_ref, spikes2_ref, cot_ref, cot2_ref, *refs):
    n_halo = 1 if two else 2
    halos, halos2 = refs[:n_halo], refs[n_halo : 2 * n_halo]
    x_ref, s_ref, c_ref = refs[2 * n_halo :]
    core, row = lax.axis_index("tm"), lax.axis_index("rows")
    steps, rows, cols, ch = spikes_ref.shape
    half = ch // 2
    lanes = x_ref.shape[2]
    strip = x_ref.shape[0]
    edge = lax.broadcasted_iota(jnp.int32, (cols, 1), 0)

    def half_of(x):
        return jnp.where(core == 0, x[:, :half], x[:, half:])

    def put_taps(x, s, t):
        before = jnp.where(edge == 0, 0.0, pltpu.roll(x, 1, 0))
        after = jnp.where(edge == cols - 1, 0.0, pltpu.roll(x, cols - 1, 0))
        pad = jnp.zeros((cols, lanes - TAPS * ch), F32)
        x_ref[s, pl.ds(pl.multiple_of(t * cols, cols), cols), :] = jnp.concatenate([before, x, after, pad], axis=1).astype(BF16)

    own = 1 + row if two else 2
    first = own - 1
    for which, (s_in, c_in, h_in) in enumerate(((spikes_ref, cot_ref, halos), (spikes2_ref, cot2_ref, halos2))):

        def body(n, carry, s_in=s_in, c_in=c_in, which=which):
            t, h = n // rows, n % rows
            x = s_in[t, h].astype(F32)
            put_taps(x, own + h, which * steps + t)
            s_ref[first + h, which * steps + t] = half_of(x).astype(BF16)
            c_ref[first + h, which * steps + t] = half_of(c_in[t, h].astype(F32)).astype(BF16)
            return carry

        lax.fori_loop(0, steps * rows, body, 0)
        for side, halo in enumerate(h_in):
            if two:
                s0 = jnp.where(row == 0, rows + 1, 0)
                u0 = jnp.where(row == 0, rows, 0)
            else:
                s0, u0 = (0, 0) if side == 0 else (rows + 2, rows + 1)

            def halo_body(t, carry, halo=halo, s0=s0, u0=u0, which=which):
                for k in range(2):
                    put_taps(halo[t, k].astype(F32), s0 + k, which * steps + t)
                c_ref[u0, which * steps + t] = half_of(halo[t, 2].astype(F32)).astype(BF16)
                s_ref[u0, which * steps + t] = jnp.zeros((cols, half), BF16)
                return carry

            lax.fori_loop(0, steps, halo_body, 0)
    if two:
        x_ref[jnp.where(row == 0, 0, strip - 1)] = jnp.zeros(x_ref.shape[1:], BF16)


def build_taps(two, own, other, lanes):
    spikes, cot, halos = own
    steps, rows, cols, ch = spikes.shape
    n_cur = rows + 1 if two else rows + 2
    outs = (
        jax.ShapeDtypeStruct((n_cur + 2, 2 * steps * cols, lanes), BF16),
        jax.ShapeDtypeStruct((n_cur, 2 * steps, cols, ch // 2), BF16),
        jax.ShapeDtypeStruct((n_cur, 2 * steps, cols, ch // 2), BF16),
    )
    args = (spikes, other[0], cot, other[1], *halos, *other[2])
    return pl.pallas_call(
        functools.partial(taps_kernel, two),
        out_shape=outs,
        in_specs=[VMEM_SPEC] * len(args),
        out_specs=(VMEM_SPEC,) * 3,
        compiler_params=params(40),
        name="taps",
    )(*args)


def assemble(wh_ref, parts, place):
    outs = parts[0].shape[0] // TAPS
    half = wh_ref.shape[0] // TAPS
    for k, part in enumerate(parts):
        at = lax.rem(place + k, len(parts)) * outs if len(parts) > 1 else 0
        for dy in range(TAPS):
            start = dy * half + at
            if len(parts) > 1:
                start = pl.multiple_of(start, 16)
            wh_ref[pl.ds(start, outs), :] = part[dy * outs : (dy + 1) * outs, :]


def forward_kernel(two, n_parts, *refs):
    parts = refs[:n_parts]
    x_hbm, s_ref, c_ref, bias_ref, thr_ref, gk_ref, gs_ref, rk_ref, rs_ref, wh_ref, xs, cur_ref, sems = refs[n_parts:]
    core, row = lax.axis_index("tm"), lax.axis_index("rows")
    place = lax.rem(lax.axis_index("dp"), n_parts)
    strip = xs.shape[0]
    n_cur, times, cols, half = s_ref.shape
    steps = times // 2

    def copy(s):
        return pltpu.make_async_copy(x_hbm.at[s], xs.at[s], sems.at[s])

    for s in range(strip):
        copy(s).start()
    assemble(wh_ref, parts, place)
    bias = jnp.where(core == 0, bias_ref[:, :half], bias_ref[:, half:])
    thr = jnp.where(core == 0, thr_ref[:, :half], thr_ref[:, half:])

    def currents(u):
        total = None
        for dy in range(TAPS):
            term = dot(xs[u + dy], wh_ref[dy * half : (dy + 1) * half, :], ((1,), (1,)))
            total = term if total is None else total + term
        cur_ref[lax.rem(u, 2)] = total + bias

    chunk = 16

    def scan(u):
        slot = lax.rem(u, 2)
        g = u + 1 - row if two else u
        inside = None
        if not two:
            last = lax.axis_size("rows") - 1
            inside = jnp.where(((u == 0) & (row == 0)) | ((u == n_cur - 1) & (row == last)), 0.0, 1.0)
        for w0 in range(0, cols, chunk):
            state = jnp.zeros((chunk, half), F32)
            fired, where_t = [], []
            for t in range(times):
                part, tl = divmod(t, steps)
                at = lax.rem(core + part, 2) * steps + tl
                where_t.append(at)
                now = cur_ref[slot, pl.ds(pl.multiple_of(at * cols + w0, chunk), chunk), :]
                potential = state + now
                spiking = 0.5 + 0.5 * jnp.tanh(potential - thr)
                state = potential - thr * spiking
                fired.append(spiking)
            res = [(f + s_ref[u, at, w0 : w0 + chunk, :].astype(F32)).astype(BF16) for f, at in zip(fired, where_t)]
            adjoint = jnp.zeros((chunk, half), F32)
            grads = [None] * times
            for t in reversed(range(times)):
                slope = 2.0 * fired[t] * (1.0 - fired[t])
                drive = c_ref[u, where_t[t], w0 : w0 + chunk, :].astype(F32) * slope
                adjoint = drive + (1.0 - thr * slope) * adjoint
                out = adjoint if inside is None else adjoint * inside
                grads[t] = out.astype(BF16)
            mine = core == 0
            for tl in range(steps):
                a, b = grads[tl], grads[steps + tl]
                gk_ref[tl, g, w0 : w0 + chunk, :] = jnp.where(mine, a, b)
                gs_ref[tl, g, w0 : w0 + chunk, :] = jnp.where(mine, b, a)
                a, b = res[tl], res[steps + tl]
                rk_ref[tl, u, w0 : w0 + chunk, :] = jnp.where(mine, a, b)
                rs_ref[tl, u, w0 : w0 + chunk, :] = jnp.where(mine, b, a)

    if two:
        edge = jnp.where(row == 0, 0, gk_ref.shape[1] - 1)
        for ref in (gk_ref, gs_ref):
            for tl in range(steps):
                ref[tl, edge] = jnp.zeros((cols, half), BF16)
    for s in range(TAPS):
        copy(s).wait()
    currents(jnp.int32(0))

    def body(u, carry):
        copy(u + TAPS).wait()
        currents(u + 1)
        scan(u)
        return carry

    lax.fori_loop(0, n_cur - 1, body, 0)
    scan(jnp.int32(n_cur - 1))


def forward(two, parts, taps, bias, thr):
    x, s, c = taps
    strip, positions, lanes = x.shape
    n_cur, times, cols, half = s.shape
    steps = times // 2
    rows = n_cur - 1 if two else n_cur - 2
    grad = jax.ShapeDtypeStruct((steps, rows + 2, cols, half), BF16)
    res = jax.ShapeDtypeStruct((steps, n_cur, cols, half), BF16)
    return pl.pallas_call(
        functools.partial(forward_kernel, two, len(parts)),
        out_shape=(grad, grad, res, res),
        in_specs=[VMEM_SPEC] * len(parts) + [ANY_SPEC] + [VMEM_SPEC] * 4,
        out_specs=(VMEM_SPEC,) * 4,
        scratch_shapes=[
            pltpu.VMEM((TAPS * half, lanes), BF16),
            pltpu.VMEM((strip, positions, lanes), BF16),
            pltpu.VMEM((2, positions, half), F32),
            pltpu.SemaphoreType.DMA((strip,)),
        ],
        compiler_params=params(40),
        name="forward",
    )(*parts, x, s, c, bias, thr)


def backward_kernel(n_parts, with_res, two, *refs):
    parts = refs[:n_parts]
    if with_res:
        g_ref, base_ref, rk_ref, rs_ref, out_ref, res_ref, wh_ref = refs[n_parts:]
    else:
        g_ref, base_ref, out_ref, wh_ref = refs[n_parts:]
    steps, rows2, cols, half = g_ref.shape
    rows, ch = rows2 - 2, base_ref.shape[3]
    core, row = lax.axis_index("tm"), lax.axis_index("rows")
    assemble(wh_ref, parts, lax.rem(lax.axis_index("dp"), n_parts))
    edge = lax.broadcasted_iota(jnp.int32, (1, cols, 1), 1)
    block = 4

    def body(n, carry):
        t, h0 = n // (rows // block), n % (rows // block) * block
        total = None
        for dy in range(TAPS):
            grads = g_ref[t, pl.ds(h0 + 2 - dy, block)].reshape(block * cols, half)
            term = dot(grads, wh_ref[dy * half : (dy + 1) * half, :], ((1,), (0,)))
            total = term if total is None else total + term
        total = total.reshape(block, cols, -1)
        left, mid, right = (total[:, :, k * ch : (k + 1) * ch] for k in range(TAPS))
        left = jnp.where(edge == cols - 1, 0.0, pltpu.roll(left, cols - 1, 1))
        right = jnp.where(edge == 0, 0.0, pltpu.roll(right, 1, 1))
        out_ref[t, pl.ds(h0, block)] = base_ref[t, pl.ds(h0, block)].astype(F32) + (left + mid + right)
        if with_res:
            first = row if two else 1
            a = rk_ref[t, pl.ds(h0 + first, block)].astype(F32)
            b = rs_ref[t, pl.ds(h0 + first, block)].astype(F32)
            both = jnp.concatenate([jnp.where(core == 0, a, b), jnp.where(core == 0, b, a)], axis=2)
            res_ref[t, pl.ds(h0, block)] = both.astype(BF16)
        return carry

    lax.fori_loop(0, steps * (rows // block), body, 0)


def backward(two, parts, grads, base, res=()):
    steps, rows, cols, ch = base.shape
    half = grads.shape[3]
    out = [jax.ShapeDtypeStruct(base.shape, F32)]
    if res:
        out.append(jax.ShapeDtypeStruct(base.shape, BF16))
    return pl.pallas_call(
        functools.partial(backward_kernel, len(parts), bool(res), two),
        out_shape=tuple(out),
        in_specs=[VMEM_SPEC] * (len(parts) + 2 + len(res)),
        out_specs=(VMEM_SPEC,) * len(out),
        scratch_shapes=[pltpu.VMEM((TAPS * half, parts[0].shape[1]), BF16)],
        compiler_params=params(40),
        name="backward_own" if not res else "backward_other",
    )(*parts, grads, base, *res)


def swap_cores(x):
    return lax.ppermute(x, "tm", [(0, 1), (1, 0)])


def fetch_halos(spikes, cot):
    count = lax.axis_size("rows")
    rows = spikes.shape[1]
    row = lax.axis_index("rows")
    if count == 2:
        s = lax.dynamic_slice_in_dim(spikes, (1 - row) * (rows - 2), 2, axis=1)
        c = lax.dynamic_slice_in_dim(cot, (1 - row) * (rows - 1), 1, axis=1)
        return [lax.ppermute(jnp.concatenate([s, c], axis=1), "rows", [(0, 1), (1, 0)])]
    tail = jnp.concatenate([spikes[:, rows - 2 :], cot[:, rows - 1 :]], axis=1)
    head = jnp.concatenate([spikes[:, :2], cot[:, :1]], axis=1)
    return [
        lax.ppermute(tail, "rows", [(i, i + 1) for i in range(count - 1)]),
        lax.ppermute(head, "rows", [(i + 1, i) for i in range(count - 1)]),
    ]


def fetch_weights(shard):
    count = lax.axis_size("dp")
    h = count // 2
    rounds = []
    for k in range(h):
        pairs = []
        for z in range(count):
            for c in range(2):
                s = c * h + (z + k) % h
                pairs.append((s * 2 + z // h, z * 2 + c))
        rounds.append(lax.ppermute(shard, ("dp", "tm"), pairs))
    return rounds


def in_order(rounds):
    h = len(rounds)
    outs = rounds[0].shape[0] // TAPS
    lanes = rounds[0].shape[1]
    if outs % 16 == 0:
        return rounds
    stack = jnp.stack([r.reshape(TAPS, outs, lanes) for r in rounds], axis=1)
    stack = jnp.roll(stack, lax.axis_index("dp") % h, axis=1)
    return [stack.reshape(TAPS * h * outs, lanes)]


def on_device(spikes, cotangent, weight_codes, block_exponents, current_bias, threshold):
    ch = spikes.shape[-1]
    lanes = -(-TAPS * ch // 256) * 256
    two = lax.axis_size("rows") == 2
    spikes, cot = spikes[0], cotangent[0]
    halos = fetch_halos(spikes, cot)
    shard = dequantize(weight_codes, block_exponents, lanes)
    own = (spikes, cot, halos)
    other = (swap_cores(spikes), swap_cores(cot), [swap_cores(x) for x in halos])
    rounds = in_order(fetch_weights(shard))
    taps = build_taps(two, own, other, lanes)
    rounds2 = [swap_cores(r) for r in rounds]
    keep, send, res_keep, res_send = forward(two, rounds, taps, current_bias[None], threshold[None])
    arrived = swap_cores(send)
    res_arrived = swap_cores(res_send)
    (partial,) = backward(two, rounds, keep, cot)
    input_grad, residual = backward(two, rounds2, arrived, partial, (res_keep, res_arrived))
    return residual[None], input_grad[None]


def solution(mesh):
    return jax.shard_map(
        on_device,
        mesh=mesh,
        in_specs=(
            P(("groups", "dp"), "tm", "rows", None, None),
            P(("groups", "dp"), "tm", "rows", None, None),
            P(None, None, None, "dp"),
            P(None, None, None, "dp"),
            P(),
            P(),
        ),
        out_specs=(
            P(("groups", "dp"), "tm", "rows", None, None),
            P(("groups", "dp"), "tm", "rows", None, None),
        ),
        check_vma=False,
    )
```

time: 114 us -> 57.7 us (0.51)
  the two profiles are of different devices: /device:TPU:0 before, /device:TPU:21 now
where the time goes in v1:
time: 57.7 us; the launch traced here: 57.4 us
  Pallas kernels  30.6 us (53%)
  starting transfers between devices  13 us (23%)
  waiting for transfers between devices  7.21 us (12%)
  local copies, waits for them, and re-layouts  4.79 us (8%)
  other arithmetic  1.15 us (2%)
  between operations  0.72 us (1%)
    pallas_call x1, Pallas kernels, forward(): pl.pallas_call(functools.partial(forward_kernel, two, len(parts)), out_sh...  11.3 us
    ppermute x7, starting transfers between devices, swap_cores(): return lax.ppermute(x, 'tm', [(0, 1), (1, 0)])  9.63 us
    pallas_call x2, Pallas kernels, backward(): pl.pallas_call(functools.partial(backward_kernel, len(parts), bool(res),...  9.58 us
    pallas_call x1, Pallas kernels, build_taps(): pl.pallas_call(functools.partial(taps_kernel, two), out_shape=outs, in_sp...  9.23 us
    ppermute x1, waiting for transfers between devices, fetch_halos(): lax.ppermute(jnp.concatenate([s, c], axis=1), 'rows', [(0, 1), (1, 0)])  6.75 us
    ppermute x2, starting transfers between devices, fetch_weights(): rounds.append(lax.ppermute(shard, ('dp', 'tm'), pairs))  2.05 us
    dynamic_slice x1, local copies, waits for them, and re-layouts, fetch_halos(): c = lax.dynamic_slice_in_dim(cot, (1 - row) * (rows - 1), 1, axis=1)  1.59 us
    ppermute x1, starting transfers between devices, fetch_halos(): lax.ppermute(jnp.concatenate([s, c], axis=1), 'rows', [(0, 1), (1, 0)])  1.28 us
  transfers between devices with their start and end apart: 10, of which 3 were waited for; matrix products, arithmetic and copies ran while one was open for 9% of the time, Pallas kernels for 24%

profile of v1, /device:TPU:21, one launch (start us, length us, event | category | flops | bytes accessed | tf_op | source)
XLA Modules:
  0.0 57.4 jit_solution(18440861502186302970)
XLA Ops:
  0.6 0.7 %collective-permute-start.5 = (bf16[3,8,64,320]{3,2,1,0:T(8,128)(2,1)}, bf16[3,8,64,320]{3,2,1,0:T(8,128)(2,1)S(1)}, u32[]{:S(2)}, u32[]{:S(2)}) collective-permute-start(bf16[3,8,64,320]{3,2,1,0:T(8,128)(2,1)} %bitcast.10), channel_id=1, source_target_pairs={{0,2},{2,0},{1,3},{3,1},{4,6},{6,4},{5,7},{7,5},{8,10},{10,8},{9,1... | collective-permute-start | bytes 2949128 | tf_op jit(solution)/shard_map/ppermute | solution.py:304
  1.4 0.1 collective-permute-start.4
  1.5 1.6 %dynamic-slice_bitcast_fusion.1 = bf16[3,1,64,320]{3,2,1,0:T(8,128)(2,1)} fusion(bf16[1,3,8,64,320]{4,3,2,1,0:T(8,128)(2,1)} %param.7, s32[]{:T(128)S(6)} %select_n.7), kind=kLoop, calls=%fused_computation.2 | loop fusion | bytes 245764 | tf_op jit(solution)/shard_map/dynamic_slice | solution.py:313
  3.0 1.0 %dynamic-slice_bitcast_fusion = bf16[3,2,64,320]{3,2,1,0:T(8,128)(2,1)S(1)} fusion(bf16[1,3,8,64,320]{4,3,2,1,0:T(8,128)(2,1)} %param.6, s32[]{:T(128)S(6)} %select_n.6), kind=kLoop, calls=%fused_computation.1 | loop fusion | bytes 491524 | tf_op jit(solution)/shard_map/dynamic_slice | solution.py:312
  4.1 1.1 %pad_maximum_fusion = bf16[3,3,64,320]{3,2,1,0:T(8,128)(2,1)S(1)} fusion(bf16[3,1,64,320]{3,2,1,0:T(8,128)(2,1)} %dynamic-slice_bitcast_fusion.1, bf16[3,2,64,320]{3,2,1,0:T(8,128)(2,1)S(1)} %dynamic-slice_bitcast_fusion), kind=kLoop, calls=%fused_computation | loop fusion | flops 184320 | bytes 737280 | tf_op jit(solution)/shard_map/concatenate | solution.py:314
  5.2 1.3 %collective-permute-start.6 = (bf16[3,3,64,320]{3,2,1,0:T(8,128)(2,1)S(1)}, bf16[3,3,64,320]{3,2,1,0:T(8,128)(2,1)S(1)}, u32[]{:S(2)}, u32[]{:S(2)}) collective-permute-start(bf16[3,3,64,320]{3,2,1,0:T(8,128)(2,1)S(1)} %pad_maximum_fusion), channel_id=1, source_target_pairs={{0,1},{1,0},{2,3},{3,2},{4,5},{5,4},{6,7},{7,6},{8,9},{9,8},{10,11... | collective-permute-start | bytes 1105928 | tf_op jit(solution)/shard_map/ppermute | solution.py:314
  6.5 0.8 %copy-done.3 = s32[3,3,10,80]{3,1,2,0:T(4,128)S(1)} copy-done((s32[3,3,10,80]{3,1,2,0:T(4,128)S(1)}, s32[3,3,10,80]{3,1,2,0:T(4,128)}, u32[]{:S(2)}) %copy-start.3) | copy-done | bytes 28824
  7.3 0.4 dequant.1
  7.8 0.7 %collective-permute-start = (bf16[240,1024]{1,0:T(8,128)(2,1)S(1)}, bf16[240,1024]{1,0:T(8,128)(2,1)S(1)}, u32[]{:S(2)}, u32[]{:S(2)}) collective-permute-start(bf16[240,1024]{1,0:T(8,128)(2,1)S(1)} %dequant.1), channel_id=1, source_target_pairs={{0,0},{8,2},{4,4},{12,6},{2,8},{10,10},{6,12},{14,14},{1,1},{9,3},... | collective-permute-start | bytes 1474568 | tf_op jit(solution)/shard_map/ppermute | solution.py:333
  8.5 1.4 %collective-permute-start.2 = (bf16[240,1024]{1,0:T(8,128)(2,1)S(1)}, bf16[240,1024]{1,0:T(8,128)(2,1)S(1)}, u32[]{:S(2)}, u32[]{:S(2)}) collective-permute-start(bf16[240,1024]{1,0:T(8,128)(2,1)S(1)} %dequant.1), channel_id=1, source_target_pairs={{4,0},{12,2},{0,4},{8,6},{6,8},{14,10},{2,12},{10,14},{5,1},{13,3}... | collective-permute-start | bytes 1474568 | tf_op jit(solution)/shard_map/ppermute | solution.py:333
  9.8 6.7 %collective-permute-done.6.refs_0_ = bf16[3,3,64,320]{3,2,1,0:T(8,128)(2,1)S(1)} collective-permute-done((bf16[3,3,64,320]{3,2,1,0:T(8,128)(2,1)S(1)}, bf16[3,3,64,320]{3,2,1,0:T(8,128)(2,1)S(1)}, u32[]{:S(2)}, u32[]{:S(2)}) %collective-permute-start.6) | collective-permute-done | bytes 368672 | tf_op jit(solution)/shard_map/ppermute | solution.py:314
  16.6 1.3 %collective-permute-start.7 = (bf16[3,3,64,320]{3,2,1,0:T(8,128)(2,1)S(1)}, bf16[3,3,64,320]{3,2,1,0:T(8,128)(2,1)S(1)}, u32[]{:S(2)}, u32[]{:S(2)}) collective-permute-start(bf16[3,3,64,320]{3,2,1,0:T(8,128)(2,1)S(1)} %collective-permute-done.6.refs_0_), channel_id=1, source_target_pairs={{0,2},{2,0},{1,3},{3,1},{4,6},{6,4},{5,7},{7,5},{8,10},{10,8},{9,1... | collective-permute-start | bytes 1105928 | tf_op jit(solution)/shard_map/ppermute | solution.py:304
  17.9 0.7 %broadcast_in_dim.12.refs_5_ = f32[1,320]{1,0:T(1,128)S(1)} reshape(f32[320]{0:T(512)} %param.10) | data formatting | bytes 2560 | tf_op jit(solution)/shard_map/broadcast_in_dim | solution.py:360
  18.5 0.7 %broadcast_in_dim.13.refs_6_ = f32[1,320]{1,0:T(1,128)S(1)} reshape(f32[320]{0:T(512)} %param.11) | data formatting | bytes 2560 | tf_op jit(solution)/shard_map/broadcast_in_dim | solution.py:360
  19.2 0.1 collective-permute-done.7.refs_1_
  19.3 9.2 %taps.1 = (bf16[11,384,1024]{2,1,0:T(8,128)(2,1)}, bf16[9,6,64,160]{3,2,1,0:T(8,128)(2,1)S(1)}, bf16[9,6,64,160]{3,2,1,0:T(8,128)(2,1)S(1)}) custom-call(bf16[3,8,64,320]{3,2,1,0:T(8,128)(2,1)S(1)} %bitcast.14, bf16[3,8,64,320]{3,2,1,0:T(8,128)(2,1)S(1)} %collective-permute-done.4.spikes2_ref, bf16[3,8,64,320]{3,2,1,0:T(8,128)(2,1)S(1)} %bitcast.11, ...), custom_call_target="tpu_custom_call" | custom-call | tf_op jit(solution)/shard_map/taps/pallas_call | solution.py:121
  28.5 11.3 %forward.1 = (bf16[3,10,64,160]{3,2,1,0:T(8,128)(2,1)S(1)}, bf16[3,10,64,160]{3,2,1,0:T(8,128)(2,1)S(1)}, bf16[3,9,64,160]{3,2,1,0:T(8,128)(2,1)S(1)}, bf16[3,9,64,160]{3,2,1,0:T(8,128)(2,1)S(1)}) custom-call(bf16[240,1024]{1,0:T(8,128)(2,1)S(1)} %collective-permute-done.refs_0_, bf16[240,1024]{1,0:T(8,128)(2,1)S(1)} %collective-permute-done.2.refs_1_, ...), custom_call_target="tpu_custom_call" | custom-call | tf_op jit(solution)/shard_map/forward/pallas_call | solution.py:234
  39.9 6.9 %collective-permute-start.8 = (bf16[3,10,64,160]{3,2,1,0:T(8,128)(2,1)S(1)}, bf16[3,10,64,160]{3,2,1,0:T(8,128)(2,1)S(1)}, u32[]{:S(2)}, u32[]{:S(2)}) collective-permute-start(bf16[3,10,64,160]{3,2,1,0:T(8,128)(2,1)S(1)} %get-tuple-element.14), channel_id=1, source_target_pairs={{0,2},{2,0},{1,3},{3,1},{4,6},{6,4},{5,7},{7,5},{8,10},{10,8},{9,1... | collective-permute-start | bytes 1843208 | tf_op jit(solution)/shard_map/ppermute | solution.py:304
  46.8 0.1 collective-permute-start.9
  46.9 0.4 collective-permute-start.1
  47.3 0.1 collective-permute-start.3
  47.4 3.9 %backward_own.1.refs_3_ = f32[3,8,64,320]{3,2,1,0:T(8,128)S(1)} custom-call(bf16[240,1024]{1,0:T(8,128)(2,1)S(1)} %collective-permute-done.refs_0_, bf16[240,1024]{1,0:T(8,128)(2,1)S(1)} %collective-permute-done.2.refs_1_, bf16[3,10,64,160]{3,2,1,0:T(8,128)(2,1)S(1)} %get-tuple-element.15.refs_2_, bf16[3,8,64,320]{3,2,1,0:T(8,128)(2,1)S(1)} %bitcast.12), custom_call_target="tpu_custom_call" | custom-call | tf_op jit(solution)/shard_map/backward_own/pallas_call | solution.py:292
  51.3 0.4 collective-permute-done.3.refs_1_
  51.7 5.7 %backward_other.1 = (f32[3,8,64,320]{3,2,1,0:T(8,128)}, bf16[3,8,64,320]{3,2,1,0:T(8,128)(2,1)}) custom-call(bf16[240,1024]{1,0:T(8,128)(2,1)S(1)} %collective-permute-done.1.refs_0_, bf16[240,1024]{1,0:T(8,128)(2,1)S(1)} %collective-permute-done.3.refs_1_, bf16[3,10,64,160]{3,2,1,0:T(8,128)(2,1)S(1)} %collective-permute-done.8.refs_2_, ...), custom_call_target="tpu_custom_call" | custom-call | tf_op jit(solution)/shard_map/backward_other/pallas_call | solution.py:292
  (14 shorter events, 0.0 us)
Async XLA Ops:
  0.6 5.9 %copy-start.2 = (s32[3,3,320,80]{2,3,1,0:T(8,128)S(1)}, s32[3,3,320,80]{2,3,1,0:T(8,128)}, u32[]{:S(2)}) copy-start(s32[3,3,320,80]{2,3,1,0:T(8,128)} %param.8) | copy-start | bytes 2764804
  0.6 18.6 %collective-permute-start.5 = (bf16[3,8,64,320]{3,2,1,0:T(8,128)(2,1)}, bf16[3,8,64,320]{3,2,1,0:T(8,128)(2,1)S(1)}, u32[]{:S(2)}, u32[]{:S(2)}) collective-permute-start(bf16[3,8,64,320]{3,2,1,0:T(8,128)(2,1)} %bitcast.10), channel_id=1, source_target_pairs={{0,2},{2,0},{1,3},{3,1},{4,6},{6,4},{5,7},{7,5},{8,10},{10,8},{9,1... | collective-permute-start | bytes 2949128 | tf_op jit(solution)/shard_map/ppermute | solution.py:304
  1.4 17.9 %collective-permute-start.4 = (bf16[3,8,64,320]{3,2,1,0:T(8,128)(2,1)}, bf16[3,8,64,320]{3,2,1,0:T(8,128)(2,1)S(1)}, u32[]{:S(2)}, u32[]{:S(2)}) collective-permute-start(bf16[3,8,64,320]{3,2,1,0:T(8,128)(2,1)} %bitcast.13), channel_id=1, source_target_pairs={{0,2},{2,0},{1,3},{3,1},{4,6},{6,4},{5,7},{7,5},{8,10},{10,8},{9,1... | collective-permute-start | bytes 2949128 | tf_op jit(solution)/shard_map/ppermute | solution.py:304
  4.0 15.3 %copy-start = (bf16[1,3,8,64,320]{4,3,2,1,0:T(8,128)(2,1)S(1)}, bf16[1,3,8,64,320]{4,3,2,1,0:T(8,128)(2,1)}, u32[]{:S(2)}) copy-start(bf16[1,3,8,64,320]{4,3,2,1,0:T(8,128)(2,1)} %param.7) | copy-start | bytes 2949124
  4.1 15.2 %copy-start.1 = (bf16[1,3,8,64,320]{4,3,2,1,0:T(8,128)(2,1)S(1)}, bf16[1,3,8,64,320]{4,3,2,1,0:T(8,128)(2,1)}, u32[]{:S(2)}) copy-start(bf16[1,3,8,64,320]{4,3,2,1,0:T(8,128)(2,1)} %param.6) | copy-start | bytes 2949124
  5.2 11.4 %collective-permute-start.6 = (bf16[3,3,64,320]{3,2,1,0:T(8,128)(2,1)S(1)}, bf16[3,3,64,320]{3,2,1,0:T(8,128)(2,1)S(1)}, u32[]{:S(2)}, u32[]{:S(2)}) collective-permute-start(bf16[3,3,64,320]{3,2,1,0:T(8,128)(2,1)S(1)} %pad_maximum_fusion), channel_id=1, source_target_pairs={{0,1},{1,0},{2,3},{3,2},{4,5},{5,4},{6,7},{7,6},{8,9},{9,8},{10,11... | collective-permute-start | bytes 1105928 | tf_op jit(solution)/shard_map/ppermute | solution.py:314
  6.5 0.8 %copy-start.3 = (s32[3,3,10,80]{3,1,2,0:T(4,128)S(1)}, s32[3,3,10,80]{3,1,2,0:T(4,128)}, u32[]{:S(2)}) copy-start(s32[3,3,10,80]{3,1,2,0:T(4,128)} %param.9) | copy-start | bytes 86404
  7.8 20.8 %collective-permute-start = (bf16[240,1024]{1,0:T(8,128)(2,1)S(1)}, bf16[240,1024]{1,0:T(8,128)(2,1)S(1)}, u32[]{:S(2)}, u32[]{:S(2)}) collective-permute-start(bf16[240,1024]{1,0:T(8,128)(2,1)S(1)} %dequant.1), channel_id=1, source_target_pairs={{0,0},{8,2},{4,4},{12,6},{2,8},{10,10},{6,12},{14,14},{1,1},{9,3},... | collective-permute-start | bytes 1474568 | tf_op jit(solution)/shard_map/ppermute | solution.py:333
  8.5 20.1 %collective-permute-start.2 = (bf16[240,1024]{1,0:T(8,128)(2,1)S(1)}, bf16[240,1024]{1,0:T(8,128)(2,1)S(1)}, u32[]{:S(2)}, u32[]{:S(2)}) collective-permute-start(bf16[240,1024]{1,0:T(8,128)(2,1)S(1)} %dequant.1), channel_id=1, source_target_pairs={{4,0},{12,2},{0,4},{8,6},{6,8},{14,10},{2,12},{10,14},{5,1},{13,3}... | collective-permute-start | bytes 1474568 | tf_op jit(solution)/shard_map/ppermute | solution.py:333
  16.6 2.7 %collective-permute-start.7 = (bf16[3,3,64,320]{3,2,1,0:T(8,128)(2,1)S(1)}, bf16[3,3,64,320]{3,2,1,0:T(8,128)(2,1)S(1)}, u32[]{:S(2)}, u32[]{:S(2)}) collective-permute-start(bf16[3,3,64,320]{3,2,1,0:T(8,128)(2,1)S(1)} %collective-permute-done.6.refs_0_), channel_id=1, source_target_pairs={{0,2},{2,0},{1,3},{3,1},{4,6},{6,4},{5,7},{7,5},{8,10},{10,8},{9,1... | collective-permute-start | bytes 1105928 | tf_op jit(solution)/shard_map/ppermute | solution.py:304
  39.9 11.8 %collective-permute-start.8 = (bf16[3,10,64,160]{3,2,1,0:T(8,128)(2,1)S(1)}, bf16[3,10,64,160]{3,2,1,0:T(8,128)(2,1)S(1)}, u32[]{:S(2)}, u32[]{:S(2)}) collective-permute-start(bf16[3,10,64,160]{3,2,1,0:T(8,128)(2,1)S(1)} %get-tuple-element.14), channel_id=1, source_target_pairs={{0,2},{2,0},{1,3},{3,1},{4,6},{6,4},{5,7},{7,5},{8,10},{10,8},{9,1... | collective-permute-start | bytes 1843208 | tf_op jit(solution)/shard_map/ppermute | solution.py:304
  46.8 4.9 %collective-permute-start.9 = (bf16[3,9,64,160]{3,2,1,0:T(8,128)(2,1)S(1)}, bf16[3,9,64,160]{3,2,1,0:T(8,128)(2,1)S(1)}, u32[]{:S(2)}, u32[]{:S(2)}) collective-permute-start(bf16[3,9,64,160]{3,2,1,0:T(8,128)(2,1)S(1)} %get-tuple-element.17), channel_id=1, source_target_pairs={{0,2},{2,0},{1,3},{3,1},{4,6},{6,4},{5,7},{7,5},{8,10},{10,8},{9,1... | collective-permute-start | bytes 1658888 | tf_op jit(solution)/shard_map/ppermute | solution.py:304
  46.9 4.4 %collective-permute-start.1 = (bf16[240,1024]{1,0:T(8,128)(2,1)S(1)}, bf16[240,1024]{1,0:T(8,128)(2,1)S(1)}, u32[]{:S(2)}, u32[]{:S(2)}) collective-permute-start(bf16[240,1024]{1,0:T(8,128)(2,1)S(1)} %collective-permute-done.refs_0_), channel_id=1, source_target_pairs={{0,2},{2,0},{1,3},{3,1},{4,6},{6,4},{5,7},{7,5},{8,10},{10,8},{9,1... | collective-permute-start | bytes 1474568 | tf_op jit(solution)/shard_map/ppermute | solution.py:304
  47.3 4.4 %collective-permute-start.3 = (bf16[240,1024]{1,0:T(8,128)(2,1)S(1)}, bf16[240,1024]{1,0:T(8,128)(2,1)S(1)}, u32[]{:S(2)}, u32[]{:S(2)}) collective-permute-start(bf16[240,1024]{1,0:T(8,128)(2,1)S(1)} %collective-permute-done.2.refs_1_), channel_id=1, source_target_pairs={{0,2},{2,0},{1,3},{3,1},{4,6},{6,4},{5,7},{7,5},{8,10},{10,8},{9,1... | collective-permute-start | bytes 1474568 | tf_op jit(solution)/shard_map/ppermute | solution.py:304

commit v2 on v0

v2 whole, which is shorter than its diff:
```python
import functools

import jax
import jax.numpy as jnp
from jax import lax
from jax.experimental import pallas as pl
from jax.experimental.pallas import tpu as pltpu
from jax.sharding import PartitionSpec as P

MX_BLOCK = 32
TAPS = 3
F32 = jnp.float32
BF16 = jnp.bfloat16
VMEM_SPEC = pl.BlockSpec(memory_space=pltpu.VMEM)
ANY_SPEC = pl.BlockSpec(memory_space=pl.ANY)
QUARTERS = 4


def call(body, out_shape, in_specs, mib, name, scratch=(), grid=(), out_specs=None):
    return pl.pallas_call(
        body,
        out_shape=out_shape,
        grid=grid,
        in_specs=in_specs,
        out_specs=out_specs or jax.tree.map(lambda _: VMEM_SPEC, out_shape),
        scratch_shapes=list(scratch),
        compiler_params=pltpu.CompilerParams(vmem_limit_bytes=mib << 20),
        name=name,
    )


def shape(dims, dtype=BF16):
    return jax.ShapeDtypeStruct(dims, dtype)


def dot(a, b, dims):
    return lax.dot_general(a, b, (dims, ((), ())), preferred_element_type=F32)


def quarter_here():
    return lax.axis_index("groups") * 2 + lax.rem(lax.axis_index("rows"), 2)


def prepare_kernel(two, codes_ref, exps_ref, spikes_ref, cot_ref, *refs):
    if two:
        w_ref, wq_ref, wd_ref, halo_ref, sems = refs
        halos = [(halo_ref, 1 - lax.axis_index("rows"))]
    else:
        w_ref, wq_ref, wd_ref, head_ref, tail_ref, sems = refs
        halos = [(head_ref, 0), (tail_ref, 1)]
    steps, rows = spikes_ref.shape[:2]
    copies = []
    for n, (ref, end) in enumerate(halos):
        for t in range(steps):
            s = spikes_ref.at[t, pl.ds(end * (rows - 2), 2)]
            c = cot_ref.at[t, pl.ds(end * (rows - 1), 1)]
            copies.append(pltpu.make_async_copy(s, ref.at[t, pl.ds(0, 2)], sems.at[len(copies)]))
            copies.append(pltpu.make_async_copy(c, ref.at[t, pl.ds(2, 1)], sems.at[len(copies)]))
    for copy in copies:
        copy.start()
    outs, ins = codes_ref.shape[2:]
    blocks = exps_ref.shape[1]
    width = w_ref.shape[2]
    spread = lax.broadcasted_iota(jnp.int32, (blocks, ins), 1) // MX_BLOCK
    spread = (spread == lax.broadcasted_iota(jnp.int32, (blocks, ins), 0)).astype(F32).astype(BF16)
    for dy in range(TAPS):
        parts = []
        for dx in range(TAPS):
            scale = 1.0 / lax.shift_left(jnp.int32(1), -exps_ref[dy, :, dx, :]).astype(F32)
            scale = dot(scale.astype(BF16), spread, ((0,), (0,)))
            parts.append(codes_ref[dy, dx].astype(F32) * scale)
        parts.append(jnp.zeros((outs, QUARTERS * width - TAPS * ins), F32))
        tap = jnp.concatenate(parts, axis=1).astype(BF16)
        for q in range(QUARTERS):
            w_ref[q, dy * outs : (dy + 1) * outs, :] = tap[:, q * width : (q + 1) * width]
    q = quarter_here()
    wq_ref[...] = w_ref[q]
    wd_ref[...] = w_ref[QUARTERS - 1 - q]
    for copy in copies:
        copy.wait()


def prepare(two, weight_codes, block_exponents, spikes, cot):
    outs = weight_codes.shape[3]
    steps, rows, cols, ch = spikes.shape
    width = -(-TAPS * ch // (QUARTERS * 128)) * 128
    n_halo = 1 if two else 2
    w = shape((TAPS * outs, width))
    out = (shape((QUARTERS, TAPS * outs, width)), w, w) + (shape((steps, 3, cols, ch)),) * n_halo
    return call(
        functools.partial(prepare_kernel, two),
        out,
        [VMEM_SPEC] * 2 + [ANY_SPEC] * 2,
        16,
        "prepare",
        [pltpu.SemaphoreType.DMA((2 * steps * n_halo,))],
    )(weight_codes.transpose(0, 1, 3, 2), block_exponents.transpose(0, 2, 1, 3), spikes, cot)


def put_taps(x_ref, x, s, t):
    cols, ch = x.shape
    edge = lax.broadcasted_iota(jnp.int32, (cols, 1), 0)
    before = jnp.where(edge == 0, 0.0, pltpu.roll(x, 1, 0))
    after = jnp.where(edge == cols - 1, 0.0, pltpu.roll(x, cols - 1, 0))
    pad = jnp.zeros((cols, x_ref.shape[2] - TAPS * ch), F32)
    taps = jnp.concatenate([before, x, after, pad], axis=1)
    x_ref[s, pl.ds(pl.multiple_of(t * cols, cols), cols), :] = taps.astype(BF16)


def half_of(x):
    half = x.shape[-1] // 2
    return jnp.where(lax.axis_index("tm") == 0, x[:, :half], x[:, half:])


def taps_kernel(spikes_ref, spikes2_ref, cot_ref, cot2_ref, x_ref, s_ref, c_ref):
    steps, rows = spikes_ref.shape[:2]
    for which, (s_in, c_in) in enumerate(((spikes_ref, cot_ref), (spikes2_ref, cot2_ref))):

        def body(n, carry, s_in=s_in, c_in=c_in, which=which):
            t, h = n // rows, n % rows
            x = s_in[t, h].astype(F32)
            put_taps(x_ref, x, h, which * steps + t)
            s_ref[h, which * steps + t] = half_of(x).astype(BF16)
            c_ref[h, which * steps + t] = half_of(c_in[t, h].astype(F32)).astype(BF16)
            return carry

        lax.fori_loop(0, steps * rows, body, 0)


def build_taps(spikes, cot, spikes2, cot2, lanes):
    steps, rows, cols, ch = spikes.shape
    half = shape((rows, 2 * steps, cols, ch // 2))
    out = (shape((rows, 2 * steps * cols, lanes)), half, half)
    return call(taps_kernel, out, [VMEM_SPEC] * 4, 16, "taps")(spikes, spikes2, cot, cot2)


def halo_taps_kernel(halo_ref, halo2_ref, x_ref, c_ref):
    steps = halo_ref.shape[0]
    for which, ref in enumerate((halo_ref, halo2_ref)):

        def body(t, carry, ref=ref, which=which):
            for k in range(2):
                put_taps(x_ref, ref[t, k].astype(F32), k, which * steps + t)
            c_ref[which * steps + t] = half_of(ref[t, 2].astype(F32)).astype(BF16)
            return carry

        lax.fori_loop(0, steps, body, 0)


def build_halo_taps(halo, halo2, lanes):
    steps, _, cols, ch = halo.shape
    out = (shape((2, 2 * steps * cols, lanes)), shape((2 * steps, cols, ch // 2)))
    return call(halo_taps_kernel, out, [VMEM_SPEC] * 2, 16, "halo_taps")(halo, halo2)


def split_half(half):
    main = half // 128 * 128
    return main, half - main, TAPS * main + -(-TAPS * (half - main) // 128) * 128


def join_kernel(w_ref, *refs):
    rounds, out_ref = (refs[:QUARTERS], refs[QUARTERS : 2 * QUARTERS]), refs[-1]
    outs = w_ref.shape[1] // TAPS
    width = w_ref.shape[2]
    main, tail, _ = split_half(2 * outs)
    z, core, q = lax.axis_index("dp"), lax.axis_index("tm"), quarter_here()
    place = lax.rem(z, 2)
    own = core == z // 2

    def put(part, lane, pos):
        at = pl.ds(pl.multiple_of(lane * width, width), width)
        for dy in range(TAPS):
            for o in range(0, outs, 16):
                c = pos * outs + o
                to = dy * main + c if c < main else TAPS * main + dy * tail + c - main
                out_ref[to : to + 16, at] = part[dy * outs + o : dy * outs + o + 16, :]

    def put_round(k, pos):
        lanes_of = (q, QUARTERS - 1 - q, jnp.bitwise_xor(q, 1), jnp.bitwise_xor(q, 2))
        if k == 1:
            for part, lane in zip(rounds[1], lanes_of):
                put(part, lane, pos)
            return

        @pl.when(own)
        def _():
            for n in range(QUARTERS):
                put(w_ref[n], n, pos)

        @pl.when(jnp.logical_not(own))
        def _():
            for part, lane in zip(rounds[0], lanes_of):
                put(part, lane, pos)

    for even in range(2):

        @pl.when(place == even)
        def _():
            put_round(0, even)
            put_round(1, 1 - even)

    rest = out_ref.shape[0] - TAPS * 2 * outs
    out_ref[TAPS * 2 * outs :, :] = jnp.zeros((rest, out_ref.shape[1]), BF16)


def fetch_weights(w, wq, wd):
    count = lax.axis_size("dp")
    n_rows = lax.axis_size("rows")
    h = count // 2
    outs = w.shape[1] // TAPS
    lanes = QUARTERS * w.shape[2]

    def pairs(k):
        todo = []
        for z in range(count):
            for c in range(2):
                s = c * h + (z + k) % h
                todo.append((s * 2 + z // h, z * 2 + c))
        return todo

    main, tail, padded = split_half(h * outs)
    if h == 2 and outs % 16 == 0 and n_rows % 2 == 0 and lax.axis_size("groups") == 2:
        moved = [[(a, b) for a, b in pairs(k) if a != b] for k in range(h)]
        first = [lax.ppermute(wq, ("dp", "tm"), moved[k]) for k in range(h)]
        last = [lax.ppermute(wd, ("dp", "tm"), moved[k]) for k in range(h)]
        args = []
        for k in range(h):
            takes = [b for _, b in moved[k]]
            rows = [(d * n_rows + r, d * n_rows + (r ^ 1)) for d in takes for r in range(n_rows)]
            groups = [(g * 2 * count + d, (1 - g) * 2 * count + d) for d in takes for g in range(2)]
            x = lax.ppermute(first[k], ("dp", "tm", "rows"), rows)
            y = lax.ppermute(first[k], ("groups", "dp", "tm"), groups)
            args += [first[k], last[k], x, y]
        return call(join_kernel, shape((padded, lanes)), [VMEM_SPEC] * 9, 8, "join")(w, *args)
    w = w.reshape(QUARTERS, TAPS, outs, -1).transpose(1, 2, 0, 3).reshape(TAPS, outs, lanes)
    stack = jnp.stack([lax.ppermute(w, ("dp", "tm"), pairs(k)) for k in range(h)], axis=1)
    stack = jnp.roll(stack, lax.axis_index("dp") % h, axis=1).reshape(TAPS, h * outs, lanes)
    rest = jnp.zeros((padded - TAPS * h * outs, lanes), BF16)
    return jnp.concatenate([stack[:, :main].reshape(-1, lanes), stack[:, main:].reshape(-1, lanes), rest])


def forward_kernel(two, w_ref, x_ref, s_ref, c_ref, *refs):
    if two:
        halos = [refs[:2]]
    else:
        halos = [refs[:2], refs[2:4]]
    bias_ref, thr_ref, gk_ref, gs_ref, rk_ref, rs_ref, p_ref = refs[2 * len(halos) :]
    core, row = lax.axis_index("tm"), lax.axis_index("rows")
    rows, times, cols, half = s_ref.shape
    lanes = x_ref.shape[2]
    steps = times // 2
    main, tail, _ = split_half(half)
    chunk = 16

    def half_row(ref):
        return jnp.where(core == 0, ref[:, :half], ref[:, half:])

    thr = half_row(thr_ref)
    shift = half_row(bias_ref) - thr
    at_of = [lax.rem(core + part, 2) * steps + tl for part in range(2) for tl in range(steps)]

    def currents(x, strip):
        p = dot(x.reshape(-1, lanes), w_ref[...], ((1,), (1,)))
        p_ref[pl.ds(strip, 2)] = p.reshape(2, times * cols, -1)

    def scan(strip, cot, spike, g, h, keep=None):
        for w0 in range(0, cols, chunk):
            for lo, width, first in ((0, main, 0), (main, tail, TAPS * main)):
                th = thr[:, lo : lo + width]
                half_th = 0.5 * th
                sh = shift[:, lo : lo + width]
                state = jnp.zeros((chunk, width), F32)
                tanhs = []
                for t in range(times):
                    at = pl.ds(pl.multiple_of(at_of[t] * cols + w0, chunk), chunk)
                    now = sh
                    for dy in range(TAPS):
                        now = now + p_ref[strip + dy, at, first + dy * width : first + (dy + 1) * width]
                    y = state + now
                    tanh = jnp.tanh(y)
                    state = (y + half_th) - half_th * tanh
                    tanhs.append(tanh)
                adjoint = jnp.zeros((chunk, width), F32)
                grads, res = [None] * times, [None] * times
                for t in reversed(range(times)):
                    here = slice(w0, w0 + chunk), slice(lo, lo + width)
                    slope = 0.5 - 0.5 * (tanhs[t] * tanhs[t])
                    up = cot(at_of[t], here).astype(F32)
                    adjoint = adjoint + slope * (up - th * adjoint)
                    out = adjoint if keep is None else adjoint * keep
                    grads[t] = out.astype(BF16)
                    if h is not None:
                        fired = 0.5 + 0.5 * tanhs[t]
                        res[t] = (fired + spike(at_of[t], here).astype(F32)).astype(BF16)
                mine = core == 0
                for tl in range(steps):
                    a, b = grads[tl], grads[steps + tl]
                    gk_ref[tl, g, w0 : w0 + chunk, lo : lo + width] = jnp.where(mine, a, b)
                    gs_ref[tl, g, w0 : w0 + chunk, lo : lo + width] = jnp.where(mine, b, a)
                    if h is not None:
                        a, b = res[tl], res[steps + tl]
                        rk_ref[tl, h, w0 : w0 + chunk, lo : lo + width] = jnp.where(mine, a, b)
                        rs_ref[tl, h, w0 : w0 + chunk, lo : lo + width] = jnp.where(mine, b, a)

    def scan_own(h, strip):
        scan(
            strip,
            lambda at, here: c_ref[h, at, here[0], here[1]],
            lambda at, here: s_ref[h, at, here[0], here[1]],
            h + 1,
            h,
        )

    def scan_halo(n, strip, g, keep=None):
        scan(strip, lambda at, here: halos[n][1][at, here[0], here[1]], None, g, None, keep)

    if two:
        flip = row == 1
        edge_strip = jnp.where(flip, rows + 2, 0)
        edge = jnp.where(flip, rows + 1, 0)
        p_ref[edge_strip] = jnp.zeros(p_ref.shape[1:], F32)
        for ref in (gk_ref, gs_ref):
            for tl in range(steps):
                ref[tl, edge] = jnp.zeros((cols, half), BF16)

        def scan_at(j):
            if j == rows:
                scan_halo(0, jnp.where(flip, 0, rows), jnp.where(flip, 0, rows + 1))
            elif 0 <= j < rows:
                h = jnp.where(flip, rows - 1 - j, j)
                scan_own(h, jnp.where(flip, h + 1, h))

        done = 0
        for i in range(rows // 2 + 1):
            if i < rows // 2:
                h = jnp.where(flip, rows - 2 - 2 * i, 2 * i)
                currents(x_ref[pl.ds(h, 2)], jnp.where(flip, h + 2, h + 1))
            else:
                currents(halos[0][0][...], jnp.where(flip, 0, rows + 1))
            while done <= 2 * i - 2:
                scan_at(done)
                done += 1
        while done <= rows:
            scan_at(done)
            done += 1
    else:
        last = lax.axis_size("rows") - 1
        currents(halos[0][0][...], 0)
        currents(halos[1][0][...], rows + 2)

        def pair(i, carry):
            currents(x_ref[pl.ds(2 * i, 2)], 2 * i + 2)
            return carry

        lax.fori_loop(0, rows // 2, pair, 0)

        def one(h, carry):
            scan_own(h, h + 1)
            return carry

        lax.fori_loop(0, rows, one, 0)
        scan_halo(0, 0, 0, jnp.where(row == 0, 0.0, 1.0))
        scan_halo(1, rows + 1, rows + 1, jnp.where(row == last, 0.0, 1.0))


def forward(two, weights, taps, halo_taps, bias, thr):
    x, s, c = taps
    rows, times, cols, half = s.shape
    steps = times // 2
    args = [weights, x, s, c] + [a for pair in halo_taps for a in pair] + [bias, thr]
    grad = shape((steps, rows + 2, cols, half))
    res = shape((steps, rows, cols, half))
    return call(
        functools.partial(forward_kernel, two),
        (grad, grad, res, res),
        [VMEM_SPEC] * len(args),
        16,
        "forward",
        [pltpu.VMEM((rows + (3 if two else 4), times * cols, weights.shape[0]), F32)],
    )(*args)


def rows_of_grads(g_ref, t, h0, count):
    cols, half = g_ref.shape[2:]
    main, tail, padded = split_half(half)
    taps = [g_ref[t, pl.ds(h0 + 2 - dy, count)].reshape(count * cols, half) for dy in range(TAPS)]
    rest = jnp.zeros((count * cols, padded - TAPS * half), BF16)
    return jnp.concatenate([x[:, :main] for x in taps] + [x[:, main:] for x in taps] + [rest], axis=1)


def backward_own_kernel(w_ref, g_ref, y_ref):
    steps, rows2 = g_ref.shape[:2]
    rows = rows2 - 2
    for t in range(steps):
        grads = rows_of_grads(g_ref, t, 0, rows)
        y_ref[t] = dot(grads, w_ref[...], ((1,), (0,)))


def backward_own(weights, grads):
    steps, rows2, cols, _ = grads.shape
    out = shape((steps, (rows2 - 2) * cols, weights.shape[1]), F32)
    return call(backward_own_kernel, out, [VMEM_SPEC] * 2, 12, "backward_own")(weights, grads)


def backward_kernel(w_ref, g_ref, y_ref, cot_ref, rk_ref, rs_ref, out_ref, res_ref):
    t = pl.program_id(0)
    _, rows, cols, ch = cot_ref.shape
    core = lax.axis_index("tm")
    edge = lax.broadcasted_iota(jnp.int32, (1, cols, 1), 1)
    block = 4
    for h0 in range(0, rows, block):
        total = dot(rows_of_grads(g_ref, t, h0, block), w_ref[...], ((1,), (0,)))
        total = (total + y_ref[t, h0 * cols : (h0 + block) * cols, :]).reshape(block, cols, -1)
        left, mid, right = (total[:, :, k * ch : (k + 1) * ch] for k in range(TAPS))
        left = jnp.where(edge == cols - 1, 0.0, pltpu.roll(left, cols - 1, 1))
        right = jnp.where(edge == 0, 0.0, pltpu.roll(right, 1, 1))
        out_ref[0, h0 : h0 + block] = cot_ref[t, h0 : h0 + block].astype(F32) + (left + mid + right)
        a = rk_ref[t, h0 : h0 + block].astype(F32)
        b = rs_ref[t, h0 : h0 + block].astype(F32)
        both = jnp.concatenate([jnp.where(core == 0, a, b), jnp.where(core == 0, b, a)], axis=2)
        res_ref[0, h0 : h0 + block] = both.astype(BF16)


def backward(weights, grads, y, cot, res_keep, res_arrived):
    block = pl.BlockSpec((1,) + cot.shape[1:], lambda t: (t, 0, 0, 0))
    return call(
        backward_kernel,
        (shape(cot.shape, F32), shape(cot.shape)),
        [VMEM_SPEC] * 6,
        16,
        "backward",
        grid=(cot.shape[0],),
        out_specs=(block, block),
    )(weights, grads, y, cot, res_keep, res_arrived)


def swap_cores(x):
    return lax.ppermute(x, "tm", [(0, 1), (1, 0)])


def fetch_halos(two, halos):
    if two:
        return [lax.ppermute(halos[0], "rows", [(0, 1), (1, 0)])]
    count = lax.axis_size("rows")
    head, tail = halos
    return [
        lax.ppermute(tail, "rows", [(i, i + 1) for i in range(count - 1)]),
        lax.ppermute(head, "rows", [(i + 1, i) for i in range(count - 1)]),
    ]


def on_device(spikes, cotangent, weight_codes, block_exponents, current_bias, threshold):
    two = lax.axis_size("rows") == 2
    spikes, cot = spikes[0], cotangent[0]
    w, wq, wd, *halos = prepare(two, weight_codes, block_exponents, spikes, cot)
    lanes = QUARTERS * w.shape[2]
    halos = fetch_halos(two, halos)
    weights = fetch_weights(w, wq, wd)
    taps = build_taps(spikes, cot, swap_cores(spikes), swap_cores(cot), lanes)
    halo_taps = [build_halo_taps(x, swap_cores(x), lanes) for x in halos]
    weights2 = swap_cores(weights)
    keep, send, res_keep, res_send = forward(two, weights, taps, halo_taps, current_bias[None], threshold[None])
    arrived = swap_cores(send)
    res_arrived = swap_cores(res_send)
    y = backward_own(weights, keep)
    input_grad, residual = backward(weights2, arrived, y, cot, res_keep, res_arrived)
    return residual[None], input_grad[None]


def solution(mesh):
    return jax.shard_map(
        on_device,
        mesh=mesh,
        in_specs=(
            P(("groups", "dp"), "tm", "rows", None, None),
            P(("groups", "dp"), "tm", "rows", None, None),
            P(None, None, None, "dp"),
            P(None, None, None, "dp"),
            P(),
            P(),
        ),
        out_specs=(
            P(("groups", "dp"), "tm", "rows", None, None),
            P(("groups", "dp"), "tm", "rows", None, None),
        ),
        check_vma=False,
    )
```

time: 114 us -> 60.5 us (0.53)
  the two profiles are of different devices: /device:TPU:0 before, /device:TPU:29 now
where the time goes in v2:
time: 60.5 us; the launch traced here: 60.1 us
  starting transfers between devices  24.3 us (40%)
  Pallas kernels  19.9 us (33%)
  waiting for transfers between devices  10.5 us (17%)
  local copies, waits for them, and re-layouts  4.64 us (8%)
  between operations  0.8 us (1%)
    ppermute x6, starting transfers between devices, swap_cores(): return lax.ppermute(x, 'tm', [(0, 1), (1, 0)])  17.4 us
    pallas_call x1, Pallas kernels, forward(): call(functools.partial(forward_kernel, two), (grad, grad, res, res), [VME...  7.05 us
    pallas_call x1, Pallas kernels, build_taps(): call(taps_kernel, out, [VMEM_SPEC] * 4, 16, 'taps')  5.17 us
    ppermute x2, waiting for transfers between devices, fetch_weights(): x = lax.ppermute(first[k], ('dp', 'tm', 'rows'), rows)  4.71 us
    unnamed x16, local copies, waits for them, and re-layouts  4.63 us
    ppermute x6, waiting for transfers between devices, swap_cores(): return lax.ppermute(x, 'tm', [(0, 1), (1, 0)])  4.21 us
    pallas_call x1, Pallas kernels, backward(): call(backward_kernel, (shape(cot.shape, F32), shape(cot.shape)), [VMEM_SP...  3.95 us
    ppermute x2, starting transfers between devices, fetch_weights(): last = [lax.ppermute(wd, ('dp', 'tm'), moved[k]) for k in range(h)]  2.02 us
  transfers between devices with their start and end apart: 15, of which 4 were waited for; matrix products, arithmetic and copies ran while one was open for 0% of the time, Pallas kernels for 26%

profile of v2, /device:TPU:29, one launch (start us, length us, event | category | flops | bytes accessed | tf_op | source)
XLA Modules:
  0.0 60.1 jit_solution(1296588996029301417)
XLA Ops:
  0.6 0.7 %collective-permute-start.10 = (bf16[3,8,64,320]{3,2,1,0:T(8,128)(2,1)}, bf16[3,8,64,320]{3,2,1,0:T(8,128)(2,1)S(1)}, u32[]{:S(2)}, u32[]{:S(2)}) collective-permute-start(bf16[3,8,64,320]{3,2,1,0:T(8,128)(2,1)} %bitcast.6), channel_id=1, source_target_pairs={{0,2},{2,0},{1,3},{3,1},{4,6},{6,4},{5,7},{7,5},{8,10},{10,8},{9,1... | collective-permute-start | bytes 2949128 | tf_op jit(solution)/shard_map/ppermute | solution.py:438
  1.5 1.3 %copy-done = bf16[1,3,8,64,320]{4,3,2,1,0:T(8,128)(2,1)S(1)} copy-done((bf16[1,3,8,64,320]{4,3,2,1,0:T(8,128)(2,1)S(1)}, bf16[1,3,8,64,320]{4,3,2,1,0:T(8,128)(2,1)}, u32[]{:S(2)}) %copy-start) | copy-done | bytes 983064
  2.7 1.3 %copy-done.2 = bf16[1,3,8,64,320]{4,3,2,1,0:T(8,128)(2,1)S(1)} copy-done((bf16[1,3,8,64,320]{4,3,2,1,0:T(8,128)(2,1)S(1)}, bf16[1,3,8,64,320]{4,3,2,1,0:T(8,128)(2,1)}, u32[]{:S(2)}) %copy-start.2) | copy-done | bytes 983064
  4.0 1.2 %copy-done.4 = s32[3,3,320,80]{2,3,1,0:T(8,128)S(1)} copy-done((s32[3,3,320,80]{2,3,1,0:T(8,128)S(1)}, s32[3,3,320,80]{2,3,1,0:T(8,128)}, u32[]{:S(2)}) %copy-start.4) | copy-done | bytes 921624
  5.2 0.8 %copy-done.5 = s32[3,3,10,80]{3,1,2,0:T(4,128)S(1)} copy-done((s32[3,3,10,80]{3,1,2,0:T(4,128)S(1)}, s32[3,3,10,80]{3,1,2,0:T(4,128)}, u32[]{:S(2)}) %copy-start.5) | copy-done | bytes 28824
  6.1 1.1 %prepare.1 = (bf16[4,240,256]{2,1,0:T(8,128)(2,1)S(1)}, bf16[240,256]{1,0:T(8,128)(2,1)S(1)}, bf16[240,256]{1,0:T(8,128)(2,1)S(1)}, bf16[3,3,64,320]{3,2,1,0:T(8,128)(2,1)S(1)}) custom-call(s32[3,3,80,320]{3,2,1,0:T(8,128)S(1)} %bitcast.13, s32[3,10,3,80]{3,2,1,0:T(4,128)S(1)} %bitcast.14, bf16[3,8,64,320]{3,2,1,0:T(8,128)(2,1)S(1)} %bitcast.11, ...), custom_call_target="tpu_custom_call" | custom-call | tf_op jit(solution)/shard_map/prepare/pallas_call | solution.py:90
  7.2 0.7 %collective-permute-start = (bf16[240,256]{1,0:T(8,128)(2,1)S(1)}, bf16[240,256]{1,0:T(8,128)(2,1)S(1)}, u32[]{:S(2)}, u32[]{:S(2)}) collective-permute-start(bf16[240,256]{1,0:T(8,128)(2,1)S(1)} %get-tuple-element.18), channel_id=1, source_target_pairs={{8,2},{12,6},{2,8},{6,12},{9,3},{13,7},{3,9},{7,13},{24,18},{28,22... | collective-permute-start | bytes 368648 | tf_op jit(solution)/shard_map/ppermute | solution.py:224
  8.1 0.7 %collective-permute-start.1 = (bf16[240,256]{1,0:T(8,128)(2,1)S(1)}, bf16[240,256]{1,0:T(8,128)(2,1)S(1)}, u32[]{:S(2)}, u32[]{:S(2)}) collective-permute-start(bf16[240,256]{1,0:T(8,128)(2,1)S(1)} %get-tuple-element.19), channel_id=1, source_target_pairs={{8,2},{12,6},{2,8},{6,12},{9,3},{13,7},{3,9},{7,13},{24,18},{28,22... | collective-permute-start | bytes 368648 | tf_op jit(solution)/shard_map/ppermute | solution.py:225
  8.8 1.4 %collective-permute-start.5 = (bf16[240,256]{1,0:T(8,128)(2,1)S(1)}, bf16[240,256]{1,0:T(8,128)(2,1)S(1)}, u32[]{:S(2)}, u32[]{:S(2)}) collective-permute-start(bf16[240,256]{1,0:T(8,128)(2,1)S(1)} %get-tuple-element.19), channel_id=1, source_target_pairs={{4,0},{12,2},{0,4},{8,6},{6,8},{14,10},{2,12},{10,14},{5,1},{13,3}... | collective-permute-start | bytes 368648 | tf_op jit(solution)/shard_map/ppermute | solution.py:225
  10.1 1.5 %collective-permute-done.4.refs_4_ = bf16[240,256]{1,0:T(8,128)(2,1)S(1)} collective-permute-done((bf16[240,256]{1,0:T(8,128)(2,1)S(1)}, bf16[240,256]{1,0:T(8,128)(2,1)S(1)}, u32[]{:S(2)}, u32[]{:S(2)}) %collective-permute-start.4) | collective-permute-done | bytes 122912 | tf_op jit(solution)/shard_map/ppermute | solution.py:224
  11.6 1.2 %collective-permute-start.11 = (bf16[3,3,64,320]{3,2,1,0:T(8,128)(2,1)S(1)}, bf16[3,3,64,320]{3,2,1,0:T(8,128)(2,1)S(1)}, u32[]{:S(2)}, u32[]{:S(2)}) collective-permute-start(bf16[3,3,64,320]{3,2,1,0:T(8,128)(2,1)S(1)} %get-tuple-element.23), channel_id=1, source_target_pairs={{0,1},{1,0},{2,3},{3,2},{4,5},{5,4},{6,7},{7,6},{8,9},{9,8},{10,11... | collective-permute-start | bytes 1105928 | tf_op jit(solution)/shard_map/ppermute | solution.py:443
  12.9 0.7 %collective-permute-start.2 = (bf16[240,256]{1,0:T(8,128)(2,1)S(1)}, bf16[240,256]{1,0:T(8,128)(2,1)S(1)}, u32[]{:S(2)}, u32[]{:S(2)}) collective-permute-start(bf16[240,256]{1,0:T(8,128)(2,1)S(1)} %collective-permute-done.refs_0_), channel_id=1, source_target_pairs={{2,3},{3,2},{6,7},{7,6},{8,9},{9,8},{12,13},{13,12},{18,19},{19,18... | collective-permute-start | bytes 368648 | tf_op jit(solution)/shard_map/ppermute | solution.py:231
  13.5 0.7 %collective-permute-start.3 = (bf16[240,256]{1,0:T(8,128)(2,1)S(1)}, bf16[240,256]{1,0:T(8,128)(2,1)S(1)}, u32[]{:S(2)}, u32[]{:S(2)}) collective-permute-start(bf16[240,256]{1,0:T(8,128)(2,1)S(1)} %collective-permute-done.refs_0_), channel_id=1, source_target_pairs={{2,18},{18,2},{6,22},{22,6},{8,24},{24,8},{12,28},{28,12},{3,19},{... | collective-permute-start | bytes 368648 | tf_op jit(solution)/shard_map/ppermute | solution.py:232
  14.2 1.2 %collective-permute-start.6 = (bf16[240,256]{1,0:T(8,128)(2,1)S(1)}, bf16[240,256]{1,0:T(8,128)(2,1)S(1)}, u32[]{:S(2)}, u32[]{:S(2)}) collective-permute-start(bf16[240,256]{1,0:T(8,128)(2,1)S(1)} %collective-permute-done.4.refs_4_), channel_id=1, source_target_pairs={{0,1},{1,0},{2,3},{3,2},{4,5},{5,4},{6,7},{7,6},{8,9},{9,8},{10,11... | collective-permute-start | bytes 368648 | tf_op jit(solution)/shard_map/ppermute | solution.py:231
  15.7 4.7 %collective-permute-done.6.refs_6_ = bf16[240,256]{1,0:T(8,128)(2,1)S(1)} collective-permute-done((bf16[240,256]{1,0:T(8,128)(2,1)S(1)}, bf16[240,256]{1,0:T(8,128)(2,1)S(1)}, u32[]{:S(2)}, u32[]{:S(2)}) %collective-permute-start.6) | collective-permute-done | bytes 122912 | tf_op jit(solution)/shard_map/ppermute | solution.py:231
  20.6 15.9 %collective-permute-start.8 = (bf16[512,1024]{1,0:T(8,128)(2,1)S(1)}, bf16[512,1024]{1,0:T(8,128)(2,1)S(1)}, u32[]{:S(2)}, u32[]{:S(2)}) collective-permute-start(bf16[512,1024]{1,0:T(8,128)(2,1)S(1)} %join.1.w_ref), channel_id=1, source_target_pairs={{0,2},{2,0},{1,3},{3,1},{4,6},{6,4},{5,7},{7,5},{8,10},{10,8},{9,1... | collective-permute-start | bytes 3145736 | tf_op jit(solution)/shard_map/ppermute | solution.py:438
  36.6 2.8 %collective-permute-done.12.halo2_ref = bf16[3,3,64,320]{3,2,1,0:T(8,128)(2,1)S(1)} collective-permute-done((bf16[3,3,64,320]{3,2,1,0:T(8,128)(2,1)S(1)}, bf16[3,3,64,320]{3,2,1,0:T(8,128)(2,1)S(1)}, u32[]{:S(2)}, u32[]{:S(2)}) %collective-permute-start.12) | collective-permute-done | bytes 368672 | tf_op jit(solution)/shard_map/ppermute | solution.py:438
  39.4 0.7 %halo_taps.1 = (bf16[2,384,1024]{2,1,0:T(8,128)(2,1)S(1)}, bf16[6,64,160]{2,1,0:T(8,128)(2,1)S(1)}) custom-call(bf16[3,3,64,320]{3,2,1,0:T(8,128)(2,1)S(1)} %collective-permute-done.11.halo_ref, bf16[3,3,64,320]{3,2,1,0:T(8,128)(2,1)S(1)} %collective-permute-done.12.halo2_ref), custom_call_target="tpu_custom_call" | custom-call | tf_op jit(solution)/shard_map/halo_taps/pallas_call | solution.py:153
  40.1 5.2 %taps.1 = (bf16[8,384,1024]{2,1,0:T(8,128)(2,1)S(1)}, bf16[8,6,64,160]{3,2,1,0:T(8,128)(2,1)S(1)}, bf16[8,6,64,160]{3,2,1,0:T(8,128)(2,1)S(1)}) custom-call(bf16[3,8,64,320]{3,2,1,0:T(8,128)(2,1)S(1)} %bitcast.12, bf16[3,8,64,320]{3,2,1,0:T(8,128)(2,1)S(1)} %collective-permute-done.9.spikes2_ref, bf16[3,8,64,320]{3,2,1,0:T(8,128)(2,1)S(1)} %bitcast.8, ...), custom_call_target="tpu_custom_call" | custom-call | tf_op jit(solution)/shard_map/taps/pallas_call | solution.py:134
  45.3 7.1 %forward.1 = (bf16[3,10,64,160]{3,2,1,0:T(8,128)(2,1)S(1)}, bf16[3,10,64,160]{3,2,1,0:T(8,128)(2,1)S(1)}, bf16[3,8,64,160]{3,2,1,0:T(8,128)(2,1)S(1)}, bf16[3,8,64,160]{3,2,1,0:T(8,128)(2,1)S(1)}) custom-call(bf16[512,1024]{1,0:T(8,128)(2,1)S(1)} %join.1.w_ref, bf16[8,384,1024]{2,1,0:T(8,128)(2,1)S(1)} %get-tuple-element.20.x_ref, ...), custom_call_target="tpu_custom_call" | custom-call | tf_op jit(solution)/shard_map/forward/pallas_call | solution.py:373
  52.4 0.5 collective-permute-start.13
  52.9 1.8 %backward_own.1.y_ref = f32[3,512,1024]{2,1,0:T(8,128)S(1)} custom-call(bf16[512,1024]{1,0:T(8,128)(2,1)S(1)} %join.1.w_ref, bf16[3,10,64,160]{3,2,1,0:T(8,128)(2,1)S(1)} %get-tuple-element.27.g_ref), custom_call_target="tpu_custom_call" | custom-call | tf_op jit(solution)/shard_map/backward_own/pallas_call | solution.py:402
  54.8 1.4 %collective-permute-done.14.rs_ref = bf16[3,8,64,160]{3,2,1,0:T(8,128)(2,1)S(1)} collective-permute-done((bf16[3,8,64,160]{3,2,1,0:T(8,128)(2,1)S(1)}, bf16[3,8,64,160]{3,2,1,0:T(8,128)(2,1)S(1)}, u32[]{:S(2)}, u32[]{:S(2)}) %collective-permute-start.14) | collective-permute-done | bytes 491552 | tf_op jit(solution)/shard_map/ppermute | solution.py:438
  56.2 3.9 %backward.1 = (f32[3,8,64,320]{3,2,1,0:T(8,128)}, bf16[3,8,64,320]{3,2,1,0:T(8,128)(2,1)}) custom-call(bf16[512,1024]{1,0:T(8,128)(2,1)S(1)} %collective-permute-done.8.w_ref, bf16[3,10,64,160]{3,2,1,0:T(8,128)(2,1)S(1)} %collective-permute-done.13.g_ref, f32[3,512,1024]{2,1,0:T(8,128)S(1)} %backward_own.1.y_ref, bf16[3,8,64,320]{3,2,1,0:T(8,128)(2,1)S(1)} %bitcast.9, ...), custom_call_target="tpu_custom_call" | custom-call | tf_op jit(solution)/shard_map/backward/pallas_call | solution.py:426
  (31 shorter events, 0.9 us)
Async XLA Ops:
  0.6 39.5 %collective-permute-start.10 = (bf16[3,8,64,320]{3,2,1,0:T(8,128)(2,1)}, bf16[3,8,64,320]{3,2,1,0:T(8,128)(2,1)S(1)}, u32[]{:S(2)}, u32[]{:S(2)}) collective-permute-start(bf16[3,8,64,320]{3,2,1,0:T(8,128)(2,1)} %bitcast.6), channel_id=1, source_target_pairs={{0,2},{2,0},{1,3},{3,1},{4,6},{6,4},{5,7},{7,5},{8,10},{10,8},{9,1... | collective-permute-start | bytes 2949128 | tf_op jit(solution)/shard_map/ppermute | solution.py:438
  1.4 38.7 %collective-permute-start.9 = (bf16[3,8,64,320]{3,2,1,0:T(8,128)(2,1)}, bf16[3,8,64,320]{3,2,1,0:T(8,128)(2,1)S(1)}, u32[]{:S(2)}, u32[]{:S(2)}) collective-permute-start(bf16[3,8,64,320]{3,2,1,0:T(8,128)(2,1)} %bitcast.10), channel_id=1, source_target_pairs={{0,2},{2,0},{1,3},{3,1},{4,6},{6,4},{5,7},{7,5},{8,10},{10,8},{9,1... | collective-permute-start | bytes 2949128 | tf_op jit(solution)/shard_map/ppermute | solution.py:438
  1.5 1.3 %copy-start = (bf16[1,3,8,64,320]{4,3,2,1,0:T(8,128)(2,1)S(1)}, bf16[1,3,8,64,320]{4,3,2,1,0:T(8,128)(2,1)}, u32[]{:S(2)}) copy-start(bf16[1,3,8,64,320]{4,3,2,1,0:T(8,128)(2,1)} %param.7) | copy-start | bytes 2949124
  2.7 1.3 %copy-start.2 = (bf16[1,3,8,64,320]{4,3,2,1,0:T(8,128)(2,1)S(1)}, bf16[1,3,8,64,320]{4,3,2,1,0:T(8,128)(2,1)}, u32[]{:S(2)}) copy-start(bf16[1,3,8,64,320]{4,3,2,1,0:T(8,128)(2,1)} %param.6) | copy-start | bytes 2949124
  4.0 1.2 %copy-start.4 = (s32[3,3,320,80]{2,3,1,0:T(8,128)S(1)}, s32[3,3,320,80]{2,3,1,0:T(8,128)}, u32[]{:S(2)}) copy-start(s32[3,3,320,80]{2,3,1,0:T(8,128)} %param.8) | copy-start | bytes 2764804
  5.2 0.8 %copy-start.5 = (s32[3,3,10,80]{3,1,2,0:T(4,128)S(1)}, s32[3,3,10,80]{3,1,2,0:T(4,128)}, u32[]{:S(2)}) copy-start(s32[3,3,10,80]{3,1,2,0:T(4,128)} %param.9) | copy-start | bytes 86404
  7.2 29.4 %copy-start.6 = (f32[320]{0:T(512)S(1)}, f32[320]{0:T(512)}, u32[]{:S(2)}) copy-start(f32[320]{0:T(512)} %param.10) | copy-start | bytes 3844
  7.2 29.4 %copy-start.7 = (f32[320]{0:T(512)S(1)}, f32[320]{0:T(512)}, u32[]{:S(2)}) copy-start(f32[320]{0:T(512)} %param.11) | copy-start | bytes 3844
  7.2 1.6 %collective-permute-start = (bf16[240,256]{1,0:T(8,128)(2,1)S(1)}, bf16[240,256]{1,0:T(8,128)(2,1)S(1)}, u32[]{:S(2)}, u32[]{:S(2)}) collective-permute-start(bf16[240,256]{1,0:T(8,128)(2,1)S(1)} %get-tuple-element.18), channel_id=1, source_target_pairs={{8,2},{12,6},{2,8},{6,12},{9,3},{13,7},{3,9},{7,13},{24,18},{28,22... | collective-permute-start | bytes 368648 | tf_op jit(solution)/shard_map/ppermute | solution.py:224
  7.9 3.8 %collective-permute-start.4 = (bf16[240,256]{1,0:T(8,128)(2,1)S(1)}, bf16[240,256]{1,0:T(8,128)(2,1)S(1)}, u32[]{:S(2)}, u32[]{:S(2)}) collective-permute-start(bf16[240,256]{1,0:T(8,128)(2,1)S(1)} %get-tuple-element.18), channel_id=1, source_target_pairs={{4,0},{12,2},{0,4},{8,6},{6,8},{14,10},{2,12},{10,14},{5,1},{13,3}... | collective-permute-start | bytes 368648 | tf_op jit(solution)/shard_map/ppermute | solution.py:224
  8.1 4.8 %collective-permute-start.1 = (bf16[240,256]{1,0:T(8,128)(2,1)S(1)}, bf16[240,256]{1,0:T(8,128)(2,1)S(1)}, u32[]{:S(2)}, u32[]{:S(2)}) collective-permute-start(bf16[240,256]{1,0:T(8,128)(2,1)S(1)} %get-tuple-element.19), channel_id=1, source_target_pairs={{8,2},{12,6},{2,8},{6,12},{9,3},{13,7},{3,9},{7,13},{24,18},{28,22... | collective-permute-start | bytes 368648 | tf_op jit(solution)/shard_map/ppermute | solution.py:225
  8.8 4.8 %collective-permute-start.5 = (bf16[240,256]{1,0:T(8,128)(2,1)S(1)}, bf16[240,256]{1,0:T(8,128)(2,1)S(1)}, u32[]{:S(2)}, u32[]{:S(2)}) collective-permute-start(bf16[240,256]{1,0:T(8,128)(2,1)S(1)} %get-tuple-element.19), channel_id=1, source_target_pairs={{4,0},{12,2},{0,4},{8,6},{6,8},{14,10},{2,12},{10,14},{5,1},{13,3}... | collective-permute-start | bytes 368648 | tf_op jit(solution)/shard_map/ppermute | solution.py:225
  11.6 24.9 %collective-permute-start.11 = (bf16[3,3,64,320]{3,2,1,0:T(8,128)(2,1)S(1)}, bf16[3,3,64,320]{3,2,1,0:T(8,128)(2,1)S(1)}, u32[]{:S(2)}, u32[]{:S(2)}) collective-permute-start(bf16[3,3,64,320]{3,2,1,0:T(8,128)(2,1)S(1)} %get-tuple-element.23), channel_id=1, source_target_pairs={{0,1},{1,0},{2,3},{3,2},{4,5},{5,4},{6,7},{7,6},{8,9},{9,8},{10,11... | collective-permute-start | bytes 1105928 | tf_op jit(solution)/shard_map/ppermute | solution.py:443
  12.9 1.4 %collective-permute-start.2 = (bf16[240,256]{1,0:T(8,128)(2,1)S(1)}, bf16[240,256]{1,0:T(8,128)(2,1)S(1)}, u32[]{:S(2)}, u32[]{:S(2)}) collective-permute-start(bf16[240,256]{1,0:T(8,128)(2,1)S(1)} %collective-permute-done.refs_0_), channel_id=1, source_target_pairs={{2,3},{3,2},{6,7},{7,6},{8,9},{9,8},{12,13},{13,12},{18,19},{19,18... | collective-permute-start | bytes 368648 | tf_op jit(solution)/shard_map/ppermute | solution.py:231
  13.5 1.9 %collective-permute-start.3 = (bf16[240,256]{1,0:T(8,128)(2,1)S(1)}, bf16[240,256]{1,0:T(8,128)(2,1)S(1)}, u32[]{:S(2)}, u32[]{:S(2)}) collective-permute-start(bf16[240,256]{1,0:T(8,128)(2,1)S(1)} %collective-permute-done.refs_0_), channel_id=1, source_target_pairs={{2,18},{18,2},{6,22},{22,6},{8,24},{24,8},{12,28},{28,12},{3,19},{... | collective-permute-start | bytes 368648 | tf_op jit(solution)/shard_map/ppermute | solution.py:232
  14.2 6.2 %collective-permute-start.6 = (bf16[240,256]{1,0:T(8,128)(2,1)S(1)}, bf16[240,256]{1,0:T(8,128)(2,1)S(1)}, u32[]{:S(2)}, u32[]{:S(2)}) collective-permute-start(bf16[240,256]{1,0:T(8,128)(2,1)S(1)} %collective-permute-done.4.refs_4_), channel_id=1, source_target_pairs={{0,1},{1,0},{2,3},{3,2},{4,5},{5,4},{6,7},{7,6},{8,9},{9,8},{10,11... | collective-permute-start | bytes 368648 | tf_op jit(solution)/shard_map/ppermute | solution.py:231
  15.5 4.9 %collective-permute-start.7 = (bf16[240,256]{1,0:T(8,128)(2,1)S(1)}, bf16[240,256]{1,0:T(8,128)(2,1)S(1)}, u32[]{:S(2)}, u32[]{:S(2)}) collective-permute-start(bf16[240,256]{1,0:T(8,128)(2,1)S(1)} %collective-permute-done.4.refs_4_), channel_id=1, source_target_pairs={{0,16},{16,0},{2,18},{18,2},{4,20},{20,4},{6,22},{22,6},{8,24},{24... | collective-permute-start | bytes 368648 | tf_op jit(solution)/shard_map/ppermute | solution.py:232
  20.4 19.7 %copy-start.1 = (bf16[1,3,8,64,320]{4,3,2,1,0:T(8,128)(2,1)S(1)}, bf16[1,3,8,64,320]{4,3,2,1,0:T(8,128)(2,1)}, u32[]{:S(2)}) copy-start(bf16[1,3,8,64,320]{4,3,2,1,0:T(8,128)(2,1)} %param.7) | copy-start | bytes 2949124
  20.4 19.7 %copy-start.3 = (bf16[1,3,8,64,320]{4,3,2,1,0:T(8,128)(2,1)S(1)}, bf16[1,3,8,64,320]{4,3,2,1,0:T(8,128)(2,1)}, u32[]{:S(2)}) copy-start(bf16[1,3,8,64,320]{4,3,2,1,0:T(8,128)(2,1)} %param.6) | copy-start | bytes 2949124
  20.6 34.2 %collective-permute-start.8 = (bf16[512,1024]{1,0:T(8,128)(2,1)S(1)}, bf16[512,1024]{1,0:T(8,128)(2,1)S(1)}, u32[]{:S(2)}, u32[]{:S(2)}) collective-permute-start(bf16[512,1024]{1,0:T(8,128)(2,1)S(1)} %join.1.w_ref), channel_id=1, source_target_pairs={{0,2},{2,0},{1,3},{3,1},{4,6},{6,4},{5,7},{7,5},{8,10},{10,8},{9,1... | collective-permute-start | bytes 3145736 | tf_op jit(solution)/shard_map/ppermute | solution.py:438
  36.5 2.9 %collective-permute-start.12 = (bf16[3,3,64,320]{3,2,1,0:T(8,128)(2,1)S(1)}, bf16[3,3,64,320]{3,2,1,0:T(8,128)(2,1)S(1)}, u32[]{:S(2)}, u32[]{:S(2)}) collective-permute-start(bf16[3,3,64,320]{3,2,1,0:T(8,128)(2,1)S(1)} %collective-permute-done.11.halo_ref), channel_id=1, source_target_pairs={{0,2},{2,0},{1,3},{3,1},{4,6},{6,4},{5,7},{7,5},{8,10},{10,8},{9,1... | collective-permute-start | bytes 1105928 | tf_op jit(solution)/shard_map/ppermute | solution.py:438
  52.4 3.8 %collective-permute-start.13 = (bf16[3,10,64,160]{3,2,1,0:T(8,128)(2,1)S(1)}, bf16[3,10,64,160]{3,2,1,0:T(8,128)(2,1)S(1)}, u32[]{:S(2)}, u32[]{:S(2)}) collective-permute-start(bf16[3,10,64,160]{3,2,1,0:T(8,128)(2,1)S(1)} %get-tuple-element.26), channel_id=1, source_target_pairs={{0,2},{2,0},{1,3},{3,1},{4,6},{6,4},{5,7},{7,5},{8,10},{10,8},{9,1... | collective-permute-start | bytes 1843208 | tf_op jit(solution)/shard_map/ppermute | solution.py:438
  52.8 3.3 %collective-permute-start.14 = (bf16[3,8,64,160]{3,2,1,0:T(8,128)(2,1)S(1)}, bf16[3,8,64,160]{3,2,1,0:T(8,128)(2,1)S(1)}, u32[]{:S(2)}, u32[]{:S(2)}) collective-permute-start(bf16[3,8,64,160]{3,2,1,0:T(8,128)(2,1)S(1)} %get-tuple-element.29), channel_id=1, source_target_pairs={{0,2},{2,0},{1,3},{3,1},{4,6},{6,4},{5,7},{7,5},{8,10},{10,8},{9,1... | collective-permute-start | bytes 1474568 | tf_op jit(solution)/shard_map/ppermute | solution.py:438

commit v3 on v2

--- a/solution.py
+++ b/solution.py
@@ -12,11 +12,11 @@
 F32 = jnp.float32
 BF16 = jnp.bfloat16
 VMEM_SPEC = pl.BlockSpec(memory_space=pltpu.VMEM)
-ANY_SPEC = pl.BlockSpec(memory_space=pl.ANY)
+HBM_SPEC = pl.BlockSpec(memory_space=pltpu.HBM)
 QUARTERS = 4
 
 
-def call(body, out_shape, in_specs, mib, name, scratch=(), grid=(), out_specs=None):
+def call(body, out_shape, in_specs, mib, name, scratch=(), grid=(), out_specs=None, cost=0):
     return pl.pallas_call(
         body,
         out_shape=out_shape,
@@ -25,10 +25,15 @@
         out_specs=out_specs or jax.tree.map(lambda _: VMEM_SPEC, out_shape),
         scratch_shapes=list(scratch),
         compiler_params=pltpu.CompilerParams(vmem_limit_bytes=mib << 20),
+        cost_estimate=pl.CostEstimate(flops=0, transcendentals=0, bytes_accessed=cost) if cost else None,
         name=name,
     )
 
 
+def in_hbm(x):
+    return pltpu.with_memory_space_constraint(x, pltpu.HBM)
+
+
 def shape(dims, dtype=BF16):
     return jax.ShapeDtypeStruct(dims, dtype)
 
@@ -41,14 +46,19 @@
     return lax.axis_index("groups") * 2 + lax.rem(lax.axis_index("rows"), 2)
 
 
-def prepare_kernel(two, codes_ref, exps_ref, spikes_ref, cot_ref, *refs):
+def prepare_kernel(two, codes_hbm, exps_hbm, spikes_ref, cot_ref, *refs):
+    w_ref, wq_ref, wd_ref = refs[:3]
+    halo_refs, (codes_ref, exps_ref, sems, code_sems) = refs[3:-4], refs[-4:]
     if two:
-        w_ref, wq_ref, wd_ref, halo_ref, sems = refs
-        halos = [(halo_ref, 1 - lax.axis_index("rows"))]
+        halos = [(halo_refs[0], 1 - lax.axis_index("rows"))]
     else:
-        w_ref, wq_ref, wd_ref, head_ref, tail_ref, sems = refs
-        halos = [(head_ref, 0), (tail_ref, 1)]
+        halos = [(halo_refs[0], 0), (halo_refs[1], 1)]
     steps, rows = spikes_ref.shape[:2]
+    scales = pltpu.make_async_copy(exps_hbm, exps_ref, code_sems.at[TAPS])
+    codes = [pltpu.make_async_copy(codes_hbm.at[dy], codes_ref.at[dy], code_sems.at[dy]) for dy in range(TAPS)]
+    scales.start()
+    for copy in codes:
+        copy.start()
     copies = []
     for n, (ref, end) in enumerate(halos):
         for t in range(steps):
@@ -63,7 +73,9 @@
     width = w_ref.shape[2]
     spread = lax.broadcasted_iota(jnp.int32, (blocks, ins), 1) // MX_BLOCK
     spread = (spread == lax.broadcasted_iota(jnp.int32, (blocks, ins), 0)).astype(F32).astype(BF16)
+    scales.wait()
     for dy in range(TAPS):
+        codes[dy].wait()
         parts = []
         for dx in range(TAPS):
             scale = 1.0 / lax.shift_left(jnp.int32(1), -exps_ref[dy, :, dx, :]).astype(F32)
@@ -90,11 +102,17 @@
     return call(
         functools.partial(prepare_kernel, two),
         out,
-        [VMEM_SPEC] * 2 + [ANY_SPEC] * 2,
+        [HBM_SPEC] * 4,
         16,
         "prepare",
-        [pltpu.SemaphoreType.DMA((2 * steps * n_halo,))],
-    )(weight_codes.transpose(0, 1, 3, 2), block_exponents.transpose(0, 2, 1, 3), spikes, cot)
+        [
+            pltpu.VMEM((TAPS, TAPS, outs, ch), jnp.int32),
+            pltpu.VMEM((TAPS, block_exponents.shape[2], TAPS, outs), jnp.int32),
+            pltpu.SemaphoreType.DMA((2 * steps * n_halo,)),
+            pltpu.SemaphoreType.DMA((TAPS + 1,)),
+        ],
+        cost=2 << 20,
+    )(*map(in_hbm, (weight_codes.transpose(0, 1, 3, 2), block_exponents.transpose(0, 2, 1, 3), spikes, cot)))
 
 
 def put_taps(x_ref, x, s, t):
@@ -131,7 +149,7 @@
     steps, rows, cols, ch = spikes.shape
     half = shape((rows, 2 * steps, cols, ch // 2))
     out = (shape((rows, 2 * steps * cols, lanes)), half, half)
-    return call(taps_kernel, out, [VMEM_SPEC] * 4, 16, "taps")(spikes, spikes2, cot, cot2)
+    return call(taps_kernel, out, [VMEM_SPEC] * 4, 16, "taps", cost=18 << 20)(spikes, spikes2, cot, cot2)
 
 
 def halo_taps_kernel(halo_ref, halo2_ref, x_ref, c_ref):
@@ -150,7 +168,7 @@
 def build_halo_taps(halo, halo2, lanes):
     steps, _, cols, ch = halo.shape
     out = (shape((2, 2 * steps * cols, lanes)), shape((2 * steps, cols, ch // 2)))
-    return call(halo_taps_kernel, out, [VMEM_SPEC] * 2, 16, "halo_taps")(halo, halo2)
+    return call(halo_taps_kernel, out, [VMEM_SPEC] * 2, 16, "halo_taps", cost=2 << 20)(halo, halo2)
 
 
 def split_half(half):
@@ -159,7 +177,9 @@
 
 
 def join_kernel(w_ref, *refs):
-    rounds, out_ref = (refs[:QUARTERS], refs[QUARTERS : 2 * QUARTERS]), refs[-1]
+    first, last, (x_ref, y_ref), out_ref = refs[:2], refs[2:4], refs[4:6], refs[-1]
+    size = w_ref.shape[1]
+    rounds = [(first[k], last[k], x_ref.at[k * size : (k + 1) * size], y_ref.at[k * size : (k + 1) * size]) for k in range(2)]
     outs = w_ref.shape[1] // TAPS
     width = w_ref.shape[2]
     main, tail, _ = split_half(2 * outs)
@@ -203,7 +223,7 @@
     out_ref[TAPS * 2 * outs :, :] = jnp.zeros((rest, out_ref.shape[1]), BF16)
 
 
-def fetch_weights(w, wq, wd):
+def fetch_weights(w, wq, wd, after):
     count = lax.axis_size("dp")
     n_rows = lax.axis_size("rows")
     h = count // 2
@@ -223,20 +243,18 @@
         moved = [[(a, b) for a, b in pairs(k) if a != b] for k in range(h)]
         first = [lax.ppermute(wq, ("dp", "tm"), moved[k]) for k in range(h)]
         last = [lax.ppermute(wd, ("dp", "tm"), moved[k]) for k in range(h)]
-        args = []
-        for k in range(h):
-            takes = [b for _, b in moved[k]]
-            rows = [(d * n_rows + r, d * n_rows + (r ^ 1)) for d in takes for r in range(n_rows)]
-            groups = [(g * 2 * count + d, (1 - g) * 2 * count + d) for d in takes for g in range(2)]
-            x = lax.ppermute(first[k], ("dp", "tm", "rows"), rows)
-            y = lax.ppermute(first[k], ("groups", "dp", "tm"), groups)
-            args += [first[k], last[k], x, y]
-        return call(join_kernel, shape((padded, lanes)), [VMEM_SPEC] * 9, 8, "join")(w, *args)
+        both, after = lax.optimization_barrier((first, after))
+        both = jnp.concatenate(both)
+        x = lax.ppermute(both, "rows", [(r, r ^ 1) for r in range(n_rows)])
+        y = lax.ppermute(both, "groups", [(0, 1), (1, 0)])
+        parts = first + last + [x, y]
+        return lambda w: call(join_kernel, shape((padded, lanes)), [VMEM_SPEC] * 7, 8, "join")(w, *parts), after
     w = w.reshape(QUARTERS, TAPS, outs, -1).transpose(1, 2, 0, 3).reshape(TAPS, outs, lanes)
     stack = jnp.stack([lax.ppermute(w, ("dp", "tm"), pairs(k)) for k in range(h)], axis=1)
     stack = jnp.roll(stack, lax.axis_index("dp") % h, axis=1).reshape(TAPS, h * outs, lanes)
     rest = jnp.zeros((padded - TAPS * h * outs, lanes), BF16)
-    return jnp.concatenate([stack[:, :main].reshape(-1, lanes), stack[:, main:].reshape(-1, lanes), rest])
+    joined = jnp.concatenate([stack[:, :main].reshape(-1, lanes), stack[:, main:].reshape(-1, lanes), rest])
+    return lambda w: joined, after
 
 
 def forward_kernel(two, w_ref, x_ref, s_ref, c_ref, *refs):
@@ -253,7 +271,8 @@
     chunk = 16
 
     def half_row(ref):
-        return jnp.where(core == 0, ref[:, :half], ref[:, half:])
+        x = ref[...].reshape(1, 2 * half)
+        return jnp.where(core == 0, x[:, :half], x[:, half:])
 
     thr = half_row(thr_ref)
     shift = half_row(bias_ref) - thr
@@ -377,6 +396,7 @@
         16,
         "forward",
         [pltpu.VMEM((rows + (3 if two else 4), times * cols, weights.shape[0]), F32)],
+        cost=24 << 20,
     )(*args)
 
 
@@ -399,7 +419,7 @@
 def backward_own(weights, grads):
     steps, rows2, cols, _ = grads.shape
     out = shape((steps, (rows2 - 2) * cols, weights.shape[1]), F32)
-    return call(backward_own_kernel, out, [VMEM_SPEC] * 2, 12, "backward_own")(weights, grads)
+    return call(backward_own_kernel, out, [VMEM_SPEC] * 2, 12, "backward_own", cost=6 << 20)(weights, grads)
 
 
 def backward_kernel(w_ref, g_ref, y_ref, cot_ref, rk_ref, rs_ref, out_ref, res_ref):
@@ -455,11 +475,13 @@
     w, wq, wd, *halos = prepare(two, weight_codes, block_exponents, spikes, cot)
     lanes = QUARTERS * w.shape[2]
     halos = fetch_halos(two, halos)
-    weights = fetch_weights(w, wq, wd)
-    taps = build_taps(spikes, cot, swap_cores(spikes), swap_cores(cot), lanes)
+    join, inputs = fetch_weights(w, wq, wd, (spikes, cot, swap_cores(spikes), swap_cores(cot)))
+    taps, halos = lax.optimization_barrier((build_taps(*inputs, lanes), halos))
     halo_taps = [build_halo_taps(x, swap_cores(x), lanes) for x in halos]
+    w, taps, halo_taps = lax.optimization_barrier((w, taps, halo_taps))
+    weights = join(w)
     weights2 = swap_cores(weights)
-    keep, send, res_keep, res_send = forward(two, weights, taps, halo_taps, current_bias[None], threshold[None])
+    keep, send, res_keep, res_send = forward(two, weights, taps, halo_taps, current_bias, threshold)
     arrived = swap_cores(send)
     res_arrived = swap_cores(res_send)
     y = backward_own(weights, keep)

time: 60.5 us -> 49.1 us (0.81)
  the two profiles are of different devices: /device:TPU:29 before, /device:TPU:0 now
where the time goes in v3:
time: 49.1 us; the launch traced here: 48.9 us
  Pallas kernels  21.2 us (43%)
  starting transfers between devices  17.1 us (35%)
  waiting for transfers between devices  9.91 us (20%)
  between operations  0.74 us (2%)
    ppermute x6, starting transfers between devices, swap_cores(): return lax.ppermute(x, 'tm', [(0, 1), (1, 0)])  8.94 us
    pallas_call x1, Pallas kernels, forward(): call(functools.partial(forward_kernel, two), (grad, grad, res, res), [VME...  7.08 us
    pallas_call x1, Pallas kernels, build_taps(): call(taps_kernel, out, [VMEM_SPEC] * 4, 16, 'taps', cost=18 << 20)  5.17 us
    ppermute x2, waiting for transfers between devices, fetch_weights(): last = [lax.ppermute(wd, ('dp', 'tm'), moved[k]) for k in range(h)]  4.72 us
    pallas_call x1, Pallas kernels, backward(): call(backward_kernel, (shape(cot.shape, F32), shape(cot.shape)), [VMEM_SP...  3.97 us
    ppermute x1, starting transfers between devices, fetch_halos(): return [lax.ppermute(halos[0], 'rows', [(0, 1), (1, 0)])]  2.99 us
    ppermute x2, waiting for transfers between devices, fetch_weights(): first = [lax.ppermute(wq, ('dp', 'tm'), moved[k]) for k in range(h)]  2.64 us
    pallas_call x1, Pallas kernels, prepare(): call(functools.partial(prepare_kernel, two), out, [HBM_SPEC] * 4, 16, 'pr...  2.35 us
  transfers between devices with their start and end apart: 13, of which 5 were waited for; matrix products, arithmetic and copies ran while one was open for 0% of the time, Pallas kernels for 35%

profile of v3, /device:TPU:0, one launch (start us, length us, event | category | flops | bytes accessed | tf_op | source)
XLA Modules:
  0.0 48.9 jit_solution(15787876226960108141)
XLA Ops:
  0.6 0.5 %collective-permute-start.2 = (bf16[3,8,64,320]{3,2,1,0:T(8,128)(2,1)}, bf16[3,8,64,320]{3,2,1,0:T(8,128)(2,1)S(1)}, u32[]{:S(2)}, u32[]{:S(2)}) collective-permute-start(bf16[3,8,64,320]{3,2,1,0:T(8,128)(2,1)} %bitcast.10), channel_id=1, source_target_pairs={{0,2},{2,0},{1,3},{3,1},{4,6},{6,4},{5,7},{7,5},{8,10},{10,8},{9,1... | collective-permute-start | bytes 2949128 | tf_op jit(solution)/shard_map/ppermute | solution.py:458
  1.1 0.1 collective-permute-start.3
  1.2 2.3 %prepare.1 = (bf16[4,240,256]{2,1,0:T(8,128)(2,1)S(1)}, bf16[240,256]{1,0:T(8,128)(2,1)S(1)}, bf16[240,256]{1,0:T(8,128)(2,1)S(1)}, bf16[3,3,64,320]{3,2,1,0:T(8,128)(2,1)S(1)}) custom-call(s32[3,3,80,320]{3,2,1,0:T(8,128)} %bitcast.13, s32[3,10,3,80]{3,2,1,0:T(4,128)} %bitcast.14, bf16[3,8,64,320]{3,2,1,0:T(8,128)(2,1)} %bitcast.11, ...), custom_call_target="tpu_custom_call" | custom-call | bytes 2097152 | tf_op jit(solution)/shard_map/prepare/pallas_call | solution.py:102
  3.6 3.0 %collective-permute-start.4 = (bf16[3,3,64,320]{3,2,1,0:T(8,128)(2,1)S(1)}, bf16[3,3,64,320]{3,2,1,0:T(8,128)(2,1)S(1)}, u32[]{:S(2)}, u32[]{:S(2)}) collective-permute-start(bf16[3,3,64,320]{3,2,1,0:T(8,128)(2,1)S(1)} %get-tuple-element.42), channel_id=1, source_target_pairs={{0,1},{1,0},{2,3},{3,2},{4,5},{5,4},{6,7},{7,6},{8,9},{9,8},{10,11... | collective-permute-start | bytes 1105928 | tf_op jit(solution)/shard_map/ppermute | solution.py:463
  6.6 1.6 %collective-permute-start.1 = (bf16[240,256]{1,0:T(8,128)(2,1)S(1)}, bf16[240,256]{1,0:T(8,128)(2,1)S(1)}, u32[]{:S(2)}, u32[]{:S(2)}) collective-permute-start(bf16[240,256]{1,0:T(8,128)(2,1)S(1)} %get-tuple-element.34), channel_id=1, source_target_pairs={{4,0},{12,2},{0,4},{8,6},{6,8},{14,10},{2,12},{10,14},{5,1},{13,3}... | collective-permute-start | bytes 368648 | tf_op jit(solution)/shard_map/ppermute | solution.py:244
  8.2 0.7 %collective-permute-start = (bf16[240,256]{1,0:T(8,128)(2,1)S(1)}, bf16[240,256]{1,0:T(8,128)(2,1)S(1)}, u32[]{:S(2)}, u32[]{:S(2)}) collective-permute-start(bf16[240,256]{1,0:T(8,128)(2,1)S(1)} %get-tuple-element.34), channel_id=1, source_target_pairs={{8,2},{12,6},{2,8},{6,12},{9,3},{13,7},{3,9},{7,13},{24,18},{28,22... | collective-permute-start | bytes 368648 | tf_op jit(solution)/shard_map/ppermute | solution.py:244
  8.8 2.6 %collective-permute-done.1.refs_1_ = bf16[240,256]{1,0:T(8,128)(2,1)S(1)} collective-permute-done((bf16[240,256]{1,0:T(8,128)(2,1)S(1)}, bf16[240,256]{1,0:T(8,128)(2,1)S(1)}, u32[]{:S(2)}, u32[]{:S(2)}) %collective-permute-start.1) | collective-permute-done | bytes 122912 | tf_op jit(solution)/shard_map/ppermute | solution.py:244
  11.5 5.2 %taps.1 = (bf16[8,384,1024]{2,1,0:T(8,128)(2,1)S(1)}, bf16[8,6,64,160]{3,2,1,0:T(8,128)(2,1)S(1)}, bf16[8,6,64,160]{3,2,1,0:T(8,128)(2,1)S(1)}) custom-call(bf16[3,8,64,320]{3,2,1,0:T(8,128)(2,1)S(1)} %bitcast.12, bf16[3,8,64,320]{3,2,1,0:T(8,128)(2,1)S(1)} %collective-permute-done.2.spikes2_ref, bf16[3,8,64,320]{3,2,1,0:T(8,128)(2,1)S(1)} %bitcast.8, ...), custom_call_target="tpu_custom_call" | custom-call | bytes 18874368 | tf_op jit(solution)/shard_map/taps/pallas_call | solution.py:152
  16.7 0.3 collective-permute-done.4.halo_ref
  17.0 6.0 %collective-permute-start.5 = (bf16[3,3,64,320]{3,2,1,0:T(8,128)(2,1)S(1)}, bf16[3,3,64,320]{3,2,1,0:T(8,128)(2,1)S(1)}, u32[]{:S(2)}, u32[]{:S(2)}) collective-permute-start(bf16[3,3,64,320]{3,2,1,0:T(8,128)(2,1)S(1)} %collective-permute-done.4.halo_ref), channel_id=1, source_target_pairs={{0,2},{2,0},{1,3},{3,1},{4,6},{6,4},{5,7},{7,5},{8,10},{10,8},{9,1... | collective-permute-start | bytes 1105928 | tf_op jit(solution)/shard_map/ppermute | solution.py:458
  23.0 1.6 %collective-permute-start.9 = (bf16[480,256]{1,0:T(8,128)(2,1)S(1)}, bf16[480,256]{1,0:T(8,128)(2,1)S(1)}, u32[]{:S(2)}, u32[]{:S(2)}) collective-permute-start(bf16[480,256]{1,0:T(8,128)(2,1)S(1)} %constant_dynamic-update-slice_fusion), channel_id=1, source_target_pairs={{0,16},{16,0},{1,17},{17,1},{2,18},{18,2},{3,19},{19,3},{4,20},{20... | collective-permute-start | bytes 737288 | tf_op jit(solution)/shard_map/ppermute | solution.py:249
  24.6 0.5 %collective-permute-start.8 = (bf16[480,256]{1,0:T(8,128)(2,1)S(1)}, bf16[480,256]{1,0:T(8,128)(2,1)S(1)}, u32[]{:S(2)}, u32[]{:S(2)}) collective-permute-start(bf16[480,256]{1,0:T(8,128)(2,1)S(1)} %constant_dynamic-update-slice_fusion), channel_id=1, source_target_pairs={{0,1},{1,0},{2,3},{3,2},{4,5},{5,4},{6,7},{7,6},{8,9},{9,8},{10,11... | collective-permute-start | bytes 737288 | tf_op jit(solution)/shard_map/ppermute | solution.py:248
  25.1 0.8 %collective-permute-start.6 = (bf16[240,256]{1,0:T(8,128)(2,1)S(1)}, bf16[240,256]{1,0:T(8,128)(2,1)S(1)}, u32[]{:S(2)}, u32[]{:S(2)}) collective-permute-start(bf16[240,256]{1,0:T(8,128)(2,1)S(1)} %get-tuple-element.50), channel_id=1, source_target_pairs={{8,2},{12,6},{2,8},{6,12},{9,3},{13,7},{3,9},{7,13},{24,18},{28,22... | collective-permute-start | bytes 368648 | tf_op jit(solution)/shard_map/ppermute | solution.py:245
  25.9 0.7 %halo_taps.1 = (bf16[2,384,1024]{2,1,0:T(8,128)(2,1)S(1)}, bf16[6,64,160]{2,1,0:T(8,128)(2,1)S(1)}) custom-call(bf16[3,3,64,320]{3,2,1,0:T(8,128)(2,1)S(1)} %collective-permute-done.4.halo_ref, bf16[3,3,64,320]{3,2,1,0:T(8,128)(2,1)S(1)} %collective-permute-done.5.halo2_ref), custom_call_target="tpu_custom_call" | custom-call | bytes 2097152 | tf_op jit(solution)/shard_map/halo_taps/pallas_call | solution.py:171
  26.6 4.7 %collective-permute-done.7.refs_3_ = bf16[240,256]{1,0:T(8,128)(2,1)S(1)} collective-permute-done((bf16[240,256]{1,0:T(8,128)(2,1)S(1)}, bf16[240,256]{1,0:T(8,128)(2,1)S(1)}, u32[]{:S(2)}, u32[]{:S(2)}) %collective-permute-start.7) | collective-permute-done | bytes 122912 | tf_op jit(solution)/shard_map/ppermute | solution.py:245
  31.3 0.8 %collective-permute-done.8.refs_4_ = bf16[480,256]{1,0:T(8,128)(2,1)S(1)} collective-permute-done((bf16[480,256]{1,0:T(8,128)(2,1)S(1)}, bf16[480,256]{1,0:T(8,128)(2,1)S(1)}, u32[]{:S(2)}, u32[]{:S(2)}) %collective-permute-start.8) | collective-permute-done | bytes 245792 | tf_op jit(solution)/shard_map/ppermute | solution.py:248
  32.2 0.1 join.1.w_ref
  32.3 1.8 %collective-permute-start.10 = (bf16[512,1024]{1,0:T(8,128)(2,1)S(1)}, bf16[512,1024]{1,0:T(8,128)(2,1)S(1)}, u32[]{:S(2)}, u32[]{:S(2)}) collective-permute-start(bf16[512,1024]{1,0:T(8,128)(2,1)S(1)} %join.1.w_ref), channel_id=1, source_target_pairs={{0,2},{2,0},{1,3},{3,1},{4,6},{6,4},{5,7},{7,5},{8,10},{10,8},{9,1... | collective-permute-start | bytes 3145736 | tf_op jit(solution)/shard_map/ppermute | solution.py:458
  34.1 7.1 %forward.1 = (bf16[3,10,64,160]{3,2,1,0:T(8,128)(2,1)S(1)}, bf16[3,10,64,160]{3,2,1,0:T(8,128)(2,1)S(1)}, bf16[3,8,64,160]{3,2,1,0:T(8,128)(2,1)S(1)}, bf16[3,8,64,160]{3,2,1,0:T(8,128)(2,1)S(1)}) custom-call(bf16[512,1024]{1,0:T(8,128)(2,1)S(1)} %join.1.w_ref, bf16[8,384,1024]{2,1,0:T(8,128)(2,1)S(1)} %get-tuple-element.53.x_ref, ...), custom_call_target="tpu_custom_call" | custom-call | bytes 25165824 | tf_op jit(solution)/shard_map/forward/pallas_call | solution.py:392
  41.2 0.1 collective-permute-start.11
  41.3 0.5 collective-permute-start.12
  41.8 1.8 %backward_own.1.y_ref = f32[3,512,1024]{2,1,0:T(8,128)S(1)} custom-call(bf16[512,1024]{1,0:T(8,128)(2,1)S(1)} %join.1.w_ref, bf16[3,10,64,160]{3,2,1,0:T(8,128)(2,1)S(1)} %get-tuple-element.59.g_ref), custom_call_target="tpu_custom_call" | custom-call | bytes 6291456 | tf_op jit(solution)/shard_map/backward_own/pallas_call | solution.py:422
  43.6 1.4 %collective-permute-done.12.rs_ref = bf16[3,8,64,160]{3,2,1,0:T(8,128)(2,1)S(1)} collective-permute-done((bf16[3,8,64,160]{3,2,1,0:T(8,128)(2,1)S(1)}, bf16[3,8,64,160]{3,2,1,0:T(8,128)(2,1)S(1)}, u32[]{:S(2)}, u32[]{:S(2)}) %collective-permute-start.12) | collective-permute-done | bytes 491552 | tf_op jit(solution)/shard_map/ppermute | solution.py:458
  44.9 4.0 %backward.1 = (f32[3,8,64,320]{3,2,1,0:T(8,128)}, bf16[3,8,64,320]{3,2,1,0:T(8,128)(2,1)}) custom-call(bf16[512,1024]{1,0:T(8,128)(2,1)S(1)} %collective-permute-done.10.w_ref, bf16[3,10,64,160]{3,2,1,0:T(8,128)(2,1)S(1)} %collective-permute-done.11.g_ref, f32[3,512,1024]{2,1,0:T(8,128)S(1)} %backward_own.1.y_ref, bf16[3,8,64,320]{3,2,1,0:T(8,128)(2,1)S(1)} %bitcast.9, ...), custom_call_target="tpu_custom_call" | custom-call | tf_op jit(solution)/shard_map/backward/pallas_call | solution.py:446
  (19 shorter events, 0.1 us)
Async XLA Ops:
  0.6 10.8 %collective-permute-start.2 = (bf16[3,8,64,320]{3,2,1,0:T(8,128)(2,1)}, bf16[3,8,64,320]{3,2,1,0:T(8,128)(2,1)S(1)}, u32[]{:S(2)}, u32[]{:S(2)}) collective-permute-start(bf16[3,8,64,320]{3,2,1,0:T(8,128)(2,1)} %bitcast.10), channel_id=1, source_target_pairs={{0,2},{2,0},{1,3},{3,1},{4,6},{6,4},{5,7},{7,5},{8,10},{10,8},{9,1... | collective-permute-start | bytes 2949128 | tf_op jit(solution)/shard_map/ppermute | solution.py:458
  1.1 10.3 %collective-permute-start.3 = (bf16[3,8,64,320]{3,2,1,0:T(8,128)(2,1)}, bf16[3,8,64,320]{3,2,1,0:T(8,128)(2,1)S(1)}, u32[]{:S(2)}, u32[]{:S(2)}) collective-permute-start(bf16[3,8,64,320]{3,2,1,0:T(8,128)(2,1)} %bitcast.6), channel_id=1, source_target_pairs={{0,2},{2,0},{1,3},{3,1},{4,6},{6,4},{5,7},{7,5},{8,10},{10,8},{9,1... | collective-permute-start | bytes 2949128 | tf_op jit(solution)/shard_map/ppermute | solution.py:458
  1.2 10.2 %copy-start = (bf16[1,3,8,64,320]{4,3,2,1,0:T(8,128)(2,1)S(1)}, bf16[1,3,8,64,320]{4,3,2,1,0:T(8,128)(2,1)}, u32[]{:S(2)}) copy-start(bf16[1,3,8,64,320]{4,3,2,1,0:T(8,128)(2,1)} %param.7) | copy-start | bytes 2949124
  1.2 10.2 %copy-start.1 = (bf16[1,3,8,64,320]{4,3,2,1,0:T(8,128)(2,1)S(1)}, bf16[1,3,8,64,320]{4,3,2,1,0:T(8,128)(2,1)}, u32[]{:S(2)}) copy-start(bf16[1,3,8,64,320]{4,3,2,1,0:T(8,128)(2,1)} %param.6) | copy-start | bytes 2949124
  3.6 13.4 %collective-permute-start.4 = (bf16[3,3,64,320]{3,2,1,0:T(8,128)(2,1)S(1)}, bf16[3,3,64,320]{3,2,1,0:T(8,128)(2,1)S(1)}, u32[]{:S(2)}, u32[]{:S(2)}) collective-permute-start(bf16[3,3,64,320]{3,2,1,0:T(8,128)(2,1)S(1)} %get-tuple-element.42), channel_id=1, source_target_pairs={{0,1},{1,0},{2,3},{3,2},{4,5},{5,4},{6,7},{7,6},{8,9},{9,8},{10,11... | collective-permute-start | bytes 1105928 | tf_op jit(solution)/shard_map/ppermute | solution.py:463
  6.6 4.9 %collective-permute-start.1 = (bf16[240,256]{1,0:T(8,128)(2,1)S(1)}, bf16[240,256]{1,0:T(8,128)(2,1)S(1)}, u32[]{:S(2)}, u32[]{:S(2)}) collective-permute-start(bf16[240,256]{1,0:T(8,128)(2,1)S(1)} %get-tuple-element.34), channel_id=1, source_target_pairs={{4,0},{12,2},{0,4},{8,6},{6,8},{14,10},{2,12},{10,14},{5,1},{13,3}... | collective-permute-start | bytes 368648 | tf_op jit(solution)/shard_map/ppermute | solution.py:244
  8.2 3.3 %collective-permute-start = (bf16[240,256]{1,0:T(8,128)(2,1)S(1)}, bf16[240,256]{1,0:T(8,128)(2,1)S(1)}, u32[]{:S(2)}, u32[]{:S(2)}) collective-permute-start(bf16[240,256]{1,0:T(8,128)(2,1)S(1)} %get-tuple-element.34), channel_id=1, source_target_pairs={{8,2},{12,6},{2,8},{6,12},{9,3},{13,7},{3,9},{7,13},{24,18},{28,22... | collective-permute-start | bytes 368648 | tf_op jit(solution)/shard_map/ppermute | solution.py:244
  17.0 8.9 %collective-permute-start.5 = (bf16[3,3,64,320]{3,2,1,0:T(8,128)(2,1)S(1)}, bf16[3,3,64,320]{3,2,1,0:T(8,128)(2,1)S(1)}, u32[]{:S(2)}, u32[]{:S(2)}) collective-permute-start(bf16[3,3,64,320]{3,2,1,0:T(8,128)(2,1)S(1)} %collective-permute-done.4.halo_ref), channel_id=1, source_target_pairs={{0,2},{2,0},{1,3},{3,1},{4,6},{6,4},{5,7},{7,5},{8,10},{10,8},{9,1... | collective-permute-start | bytes 1105928 | tf_op jit(solution)/shard_map/ppermute | solution.py:458
  23.0 8.3 %collective-permute-start.9 = (bf16[480,256]{1,0:T(8,128)(2,1)S(1)}, bf16[480,256]{1,0:T(8,128)(2,1)S(1)}, u32[]{:S(2)}, u32[]{:S(2)}) collective-permute-start(bf16[480,256]{1,0:T(8,128)(2,1)S(1)} %constant_dynamic-update-slice_fusion), channel_id=1, source_target_pairs={{0,16},{16,0},{1,17},{17,1},{2,18},{18,2},{3,19},{19,3},{4,20},{20... | collective-permute-start | bytes 737288 | tf_op jit(solution)/shard_map/ppermute | solution.py:249
  24.6 7.6 %collective-permute-start.8 = (bf16[480,256]{1,0:T(8,128)(2,1)S(1)}, bf16[480,256]{1,0:T(8,128)(2,1)S(1)}, u32[]{:S(2)}, u32[]{:S(2)}) collective-permute-start(bf16[480,256]{1,0:T(8,128)(2,1)S(1)} %constant_dynamic-update-slice_fusion), channel_id=1, source_target_pairs={{0,1},{1,0},{2,3},{3,2},{4,5},{5,4},{6,7},{7,6},{8,9},{9,8},{10,11... | collective-permute-start | bytes 737288 | tf_op jit(solution)/shard_map/ppermute | solution.py:248
  25.1 9.0 %copy-start.2 = (f32[320]{0:T(512)S(1)}, f32[320]{0:T(512)}, u32[]{:S(2)}) copy-start(f32[320]{0:T(512)} %refs_2_.1) | copy-start | bytes 3844
  25.1 9.0 %copy-start.3 = (f32[320]{0:T(512)S(1)}, f32[320]{0:T(512)}, u32[]{:S(2)}) copy-start(f32[320]{0:T(512)} %refs_3_.1) | copy-start | bytes 3844
  25.1 6.2 %collective-permute-start.7 = (bf16[240,256]{1,0:T(8,128)(2,1)S(1)}, bf16[240,256]{1,0:T(8,128)(2,1)S(1)}, u32[]{:S(2)}, u32[]{:S(2)}) collective-permute-start(bf16[240,256]{1,0:T(8,128)(2,1)S(1)} %get-tuple-element.50), channel_id=1, source_target_pairs={{4,0},{12,2},{0,4},{8,6},{6,8},{14,10},{2,12},{10,14},{5,1},{13,3}... | collective-permute-start | bytes 368648 | tf_op jit(solution)/shard_map/ppermute | solution.py:245
  25.1 6.2 %collective-permute-start.6 = (bf16[240,256]{1,0:T(8,128)(2,1)S(1)}, bf16[240,256]{1,0:T(8,128)(2,1)S(1)}, u32[]{:S(2)}, u32[]{:S(2)}) collective-permute-start(bf16[240,256]{1,0:T(8,128)(2,1)S(1)} %get-tuple-element.50), channel_id=1, source_target_pairs={{8,2},{12,6},{2,8},{6,12},{9,3},{13,7},{3,9},{7,13},{24,18},{28,22... | collective-permute-start | bytes 368648 | tf_op jit(solution)/shard_map/ppermute | solution.py:245
  32.3 12.7 %collective-permute-start.10 = (bf16[512,1024]{1,0:T(8,128)(2,1)S(1)}, bf16[512,1024]{1,0:T(8,128)(2,1)S(1)}, u32[]{:S(2)}, u32[]{:S(2)}) collective-permute-start(bf16[512,1024]{1,0:T(8,128)(2,1)S(1)} %join.1.w_ref), channel_id=1, source_target_pairs={{0,2},{2,0},{1,3},{3,1},{4,6},{6,4},{5,7},{7,5},{8,10},{10,8},{9,1... | collective-permute-start | bytes 3145736 | tf_op jit(solution)/shard_map/ppermute | solution.py:458
  41.2 3.8 %collective-permute-start.11 = (bf16[3,10,64,160]{3,2,1,0:T(8,128)(2,1)S(1)}, bf16[3,10,64,160]{3,2,1,0:T(8,128)(2,1)S(1)}, u32[]{:S(2)}, u32[]{:S(2)}) collective-permute-start(bf16[3,10,64,160]{3,2,1,0:T(8,128)(2,1)S(1)} %get-tuple-element.58), channel_id=1, source_target_pairs={{0,2},{2,0},{1,3},{3,1},{4,6},{6,4},{5,7},{7,5},{8,10},{10,8},{9,1... | collective-permute-start | bytes 1843208 | tf_op jit(solution)/shard_map/ppermute | solution.py:458
  41.3 3.7 %collective-permute-start.12 = (bf16[3,8,64,160]{3,2,1,0:T(8,128)(2,1)S(1)}, bf16[3,8,64,160]{3,2,1,0:T(8,128)(2,1)S(1)}, u32[]{:S(2)}, u32[]{:S(2)}) collective-permute-start(bf16[3,8,64,160]{3,2,1,0:T(8,128)(2,1)S(1)} %get-tuple-element.61), channel_id=1, source_target_pairs={{0,2},{2,0},{1,3},{3,1},{4,6},{6,4},{5,7},{7,5},{8,10},{10,8},{9,1... | collective-permute-start | bytes 1474568 | tf_op jit(solution)/shard_map/ppermute | solution.py:458

commit v4 on v3

--- a/solution.py
+++ b/solution.py
@@ -243,8 +243,10 @@
         moved = [[(a, b) for a, b in pairs(k) if a != b] for k in range(h)]
         first = [lax.ppermute(wq, ("dp", "tm"), moved[k]) for k in range(h)]
         last = [lax.ppermute(wd, ("dp", "tm"), moved[k]) for k in range(h)]
-        both, after = lax.optimization_barrier((first, after))
-        both = jnp.concatenate(both)
+        first, (taps, halos) = lax.optimization_barrier((first, (after[0], after[1])))
+        both = jnp.concatenate(first)
+        held, halos = lax.optimization_barrier((both, halos))
+        after = taps, halos
         x = lax.ppermute(both, "rows", [(r, r ^ 1) for r in range(n_rows)])
         y = lax.ppermute(both, "groups", [(0, 1), (1, 0)])
         parts = first + last + [x, y]
@@ -475,8 +477,8 @@
     w, wq, wd, *halos = prepare(two, weight_codes, block_exponents, spikes, cot)
     lanes = QUARTERS * w.shape[2]
     halos = fetch_halos(two, halos)
-    join, inputs = fetch_weights(w, wq, wd, (spikes, cot, swap_cores(spikes), swap_cores(cot)))
-    taps, halos = lax.optimization_barrier((build_taps(*inputs, lanes), halos))
+    taps = build_taps(spikes, cot, swap_cores(spikes), swap_cores(cot), lanes)
+    join, (taps, halos) = fetch_weights(w, wq, wd, (taps, halos))
     halo_taps = [build_halo_taps(x, swap_cores(x), lanes) for x in halos]
     w, taps, halo_taps = lax.optimization_barrier((w, taps, halo_taps))
     weights = join(w)

time: 49.1 us -> 46.7 us (0.951)
  waiting for transfers between devices: 9.91 us -> 7.93 us
    ppermute x2, waiting for transfers between devices: 4.72 us -> 1.96 us  [fetch_weights(): last = [lax.ppermute(wd, ('dp', 'tm'), moved[k]) for k in range(h)]]
    ppermute x2, waiting for transfers between devices: 2.64 us -> 0.01 us  [fetch_weights(): first = [lax.ppermute(wq, ('dp', 'tm'), moved[k]) for k in range(h)]]
    ppermute x1, waiting for transfers between devices: 0.32 us -> 2.93 us  [fetch_halos(): return [lax.ppermute(halos[0], 'rows', [(0, 1), (1, 0)])]]
    ppermute x6, starting transfers between devices: 8.94 us -> 6.58 us  [swap_cores(): return lax.ppermute(x, 'tm', [(0, 1), (1, 0)])]
    ppermute x2, starting transfers between devices: 0.79 us -> 2.23 us  [fetch_weights(): last = [lax.ppermute(wd, ('dp', 'tm'), moved[k]) for k in range(h)]]
    ppermute x1, starting transfers between devices: 0.55 us -> 1.12 us  [fetch_weights(): x = lax.ppermute(both, 'rows', [(r, r ^ 1) for r in range(n_rows)])]
  transfers between devices with their start and end apart: 13 -> 13, of which waited for: 5 -> 5; matrix products, arithmetic and copies ran while one was open for 0% -> 0% of each run, Pallas kernels for 35% -> 37%
where the time goes in v4:
time: 46.7 us; the launch traced here: 46.5 us
  Pallas kernels  21.1 us (45%)
  starting transfers between devices  16.7 us (36%)
  waiting for transfers between devices  7.93 us (17%)
  between operations  0.76 us (2%)
    pallas_call x1, Pallas kernels, forward(): call(functools.partial(forward_kernel, two), (grad, grad, res, res), [VME...  7.08 us
    ppermute x6, starting transfers between devices, swap_cores(): return lax.ppermute(x, 'tm', [(0, 1), (1, 0)])  6.58 us
    pallas_call x1, Pallas kernels, build_taps(): call(taps_kernel, out, [VMEM_SPEC] * 4, 16, 'taps', cost=18 << 20)  5.17 us
    pallas_call x1, Pallas kernels, backward(): call(backward_kernel, (shape(cot.shape, F32), shape(cot.shape)), [VMEM_SP...  3.97 us
    ppermute x1, starting transfers between devices, fetch_halos(): return [lax.ppermute(halos[0], 'rows', [(0, 1), (1, 0)])]  2.99 us
    ppermute x1, waiting for transfers between devices, fetch_halos(): return [lax.ppermute(halos[0], 'rows', [(0, 1), (1, 0)])]  2.93 us
    pallas_call x1, Pallas kernels, prepare(): call(functools.partial(prepare_kernel, two), out, [HBM_SPEC] * 4, 16, 'pr...  2.35 us
    ppermute x2, starting transfers between devices, fetch_weights(): last = [lax.ppermute(wd, ('dp', 'tm'), moved[k]) for k in range(h)]  2.23 us
  transfers between devices with their start and end apart: 13, of which 5 were waited for; matrix products, arithmetic and copies ran while one was open for 0% of the time, Pallas kernels for 37%

profile of v4, /device:TPU:0, one launch (start us, length us, event | category | flops | bytes accessed | tf_op | source)
XLA Modules:
  0.0 46.5 jit_solution(10213759850321296554)
XLA Ops:
  0.6 0.5 %collective-permute-start.2 = (bf16[3,8,64,320]{3,2,1,0:T(8,128)(2,1)}, bf16[3,8,64,320]{3,2,1,0:T(8,128)(2,1)S(1)}, u32[]{:S(2)}, u32[]{:S(2)}) collective-permute-start(bf16[3,8,64,320]{3,2,1,0:T(8,128)(2,1)} %bitcast.10), channel_id=1, source_target_pairs={{0,2},{2,0},{1,3},{3,1},{4,6},{6,4},{5,7},{7,5},{8,10},{10,8},{9,1... | collective-permute-start | bytes 2949128 | tf_op jit(solution)/shard_map/ppermute | solution.py:460
  1.2 2.3 %prepare.1 = (bf16[4,240,256]{2,1,0:T(8,128)(2,1)S(1)}, bf16[240,256]{1,0:T(8,128)(2,1)S(1)}, bf16[240,256]{1,0:T(8,128)(2,1)S(1)}, bf16[3,3,64,320]{3,2,1,0:T(8,128)(2,1)S(1)}) custom-call(s32[3,3,80,320]{3,2,1,0:T(8,128)} %bitcast.13, s32[3,10,3,80]{3,2,1,0:T(4,128)} %bitcast.14, bf16[3,8,64,320]{3,2,1,0:T(8,128)(2,1)} %bitcast.11, ...), custom_call_target="tpu_custom_call" | custom-call | bytes 2097152 | tf_op jit(solution)/shard_map/prepare/pallas_call | solution.py:102
  3.6 3.0 %collective-permute-start.4 = (bf16[3,3,64,320]{3,2,1,0:T(8,128)(2,1)S(1)}, bf16[3,3,64,320]{3,2,1,0:T(8,128)(2,1)S(1)}, u32[]{:S(2)}, u32[]{:S(2)}) collective-permute-start(bf16[3,3,64,320]{3,2,1,0:T(8,128)(2,1)S(1)} %get-tuple-element.35), channel_id=1, source_target_pairs={{0,1},{1,0},{2,3},{3,2},{4,5},{5,4},{6,7},{7,6},{8,9},{9,8},{10,11... | collective-permute-start | bytes 1105928 | tf_op jit(solution)/shard_map/ppermute | solution.py:465
  6.6 1.6 %collective-permute-start.1 = (bf16[240,256]{1,0:T(8,128)(2,1)S(1)}, bf16[240,256]{1,0:T(8,128)(2,1)S(1)}, u32[]{:S(2)}, u32[]{:S(2)}) collective-permute-start(bf16[240,256]{1,0:T(8,128)(2,1)S(1)} %get-tuple-element.31), channel_id=1, source_target_pairs={{4,0},{12,2},{0,4},{8,6},{6,8},{14,10},{2,12},{10,14},{5,1},{13,3}... | collective-permute-start | bytes 368648 | tf_op jit(solution)/shard_map/ppermute | solution.py:244
  8.2 0.7 %collective-permute-start = (bf16[240,256]{1,0:T(8,128)(2,1)S(1)}, bf16[240,256]{1,0:T(8,128)(2,1)S(1)}, u32[]{:S(2)}, u32[]{:S(2)}) collective-permute-start(bf16[240,256]{1,0:T(8,128)(2,1)S(1)} %get-tuple-element.31), channel_id=1, source_target_pairs={{8,2},{12,6},{2,8},{6,12},{9,3},{13,7},{3,9},{7,13},{24,18},{28,22... | collective-permute-start | bytes 368648 | tf_op jit(solution)/shard_map/ppermute | solution.py:244
  8.9 5.2 %taps.1 = (bf16[8,384,1024]{2,1,0:T(8,128)(2,1)S(1)}, bf16[8,6,64,160]{3,2,1,0:T(8,128)(2,1)S(1)}, bf16[8,6,64,160]{3,2,1,0:T(8,128)(2,1)S(1)}) custom-call(bf16[3,8,64,320]{3,2,1,0:T(8,128)(2,1)S(1)} %bitcast.12, bf16[3,8,64,320]{3,2,1,0:T(8,128)(2,1)S(1)} %collective-permute-done.2.spikes2_ref, bf16[3,8,64,320]{3,2,1,0:T(8,128)(2,1)S(1)} %bitcast.8, ...), custom_call_target="tpu_custom_call" | custom-call | bytes 18874368 | tf_op jit(solution)/shard_map/taps/pallas_call | solution.py:152
  14.1 2.9 %collective-permute-done.4.halo_ref = bf16[3,3,64,320]{3,2,1,0:T(8,128)(2,1)S(1)} collective-permute-done((bf16[3,3,64,320]{3,2,1,0:T(8,128)(2,1)S(1)}, bf16[3,3,64,320]{3,2,1,0:T(8,128)(2,1)S(1)}, u32[]{:S(2)}, u32[]{:S(2)}) %collective-permute-start.4) | collective-permute-done | bytes 368672 | tf_op jit(solution)/shard_map/ppermute | solution.py:465
  17.0 0.8 %collective-permute-start.5 = (bf16[3,3,64,320]{3,2,1,0:T(8,128)(2,1)S(1)}, bf16[3,3,64,320]{3,2,1,0:T(8,128)(2,1)S(1)}, u32[]{:S(2)}, u32[]{:S(2)}) collective-permute-start(bf16[3,3,64,320]{3,2,1,0:T(8,128)(2,1)S(1)} %collective-permute-done.4.halo_ref), channel_id=1, source_target_pairs={{0,2},{2,0},{1,3},{3,1},{4,6},{6,4},{5,7},{7,5},{8,10},{10,8},{9,1... | collective-permute-start | bytes 1105928 | tf_op jit(solution)/shard_map/ppermute | solution.py:460
  17.8 1.5 %collective-permute-start.9 = (bf16[480,256]{1,0:T(8,128)(2,1)S(1)}, bf16[480,256]{1,0:T(8,128)(2,1)S(1)}, u32[]{:S(2)}, u32[]{:S(2)}) collective-permute-start(bf16[480,256]{1,0:T(8,128)(2,1)S(1)} %constant_dynamic-update-slice_fusion), channel_id=1, source_target_pairs={{0,16},{16,0},{1,17},{17,1},{2,18},{18,2},{3,19},{19,3},{4,20},{20... | collective-permute-start | bytes 737288 | tf_op jit(solution)/shard_map/ppermute | solution.py:251
  19.3 1.1 %collective-permute-start.8 = (bf16[480,256]{1,0:T(8,128)(2,1)S(1)}, bf16[480,256]{1,0:T(8,128)(2,1)S(1)}, u32[]{:S(2)}, u32[]{:S(2)}) collective-permute-start(bf16[480,256]{1,0:T(8,128)(2,1)S(1)} %constant_dynamic-update-slice_fusion), channel_id=1, source_target_pairs={{0,1},{1,0},{2,3},{3,2},{4,5},{5,4},{6,7},{7,6},{8,9},{9,8},{10,11... | collective-permute-start | bytes 737288 | tf_op jit(solution)/shard_map/ppermute | solution.py:250
  20.4 1.6 %collective-permute-start.7 = (bf16[240,256]{1,0:T(8,128)(2,1)S(1)}, bf16[240,256]{1,0:T(8,128)(2,1)S(1)}, u32[]{:S(2)}, u32[]{:S(2)}) collective-permute-start(bf16[240,256]{1,0:T(8,128)(2,1)S(1)} %get-tuple-element.46), channel_id=1, source_target_pairs={{4,0},{12,2},{0,4},{8,6},{6,8},{14,10},{2,12},{10,14},{5,1},{13,3}... | collective-permute-start | bytes 368648 | tf_op jit(solution)/shard_map/ppermute | solution.py:245
  22.0 0.7 %collective-permute-start.6 = (bf16[240,256]{1,0:T(8,128)(2,1)S(1)}, bf16[240,256]{1,0:T(8,128)(2,1)S(1)}, u32[]{:S(2)}, u32[]{:S(2)}) collective-permute-start(bf16[240,256]{1,0:T(8,128)(2,1)S(1)} %get-tuple-element.46), channel_id=1, source_target_pairs={{8,2},{12,6},{2,8},{6,12},{9,3},{13,7},{3,9},{7,13},{24,18},{28,22... | collective-permute-start | bytes 368648 | tf_op jit(solution)/shard_map/ppermute | solution.py:245
  22.7 0.7 %halo_taps.1 = (bf16[2,384,1024]{2,1,0:T(8,128)(2,1)S(1)}, bf16[6,64,160]{2,1,0:T(8,128)(2,1)S(1)}) custom-call(bf16[3,3,64,320]{3,2,1,0:T(8,128)(2,1)S(1)} %collective-permute-done.4.halo_ref, bf16[3,3,64,320]{3,2,1,0:T(8,128)(2,1)S(1)} %collective-permute-done.5.halo2_ref), custom_call_target="tpu_custom_call" | custom-call | bytes 2097152 | tf_op jit(solution)/shard_map/halo_taps/pallas_call | solution.py:171
  23.3 2.0 %collective-permute-done.7.refs_3_ = bf16[240,256]{1,0:T(8,128)(2,1)S(1)} collective-permute-done((bf16[240,256]{1,0:T(8,128)(2,1)S(1)}, bf16[240,256]{1,0:T(8,128)(2,1)S(1)}, u32[]{:S(2)}, u32[]{:S(2)}) %collective-permute-start.7) | collective-permute-done | bytes 122912 | tf_op jit(solution)/shard_map/ppermute | solution.py:245
  25.3 0.4 collective-permute-done.9.refs_5_
  25.7 1.2 %collective-permute-done.8.refs_4_ = bf16[480,256]{1,0:T(8,128)(2,1)S(1)} collective-permute-done((bf16[480,256]{1,0:T(8,128)(2,1)S(1)}, bf16[480,256]{1,0:T(8,128)(2,1)S(1)}, u32[]{:S(2)}, u32[]{:S(2)}) %collective-permute-start.8) | collective-permute-done | bytes 245792 | tf_op jit(solution)/shard_map/ppermute | solution.py:250
  27.0 0.1 join.1.w_ref
  27.1 4.6 %collective-permute-start.10 = (bf16[512,1024]{1,0:T(8,128)(2,1)S(1)}, bf16[512,1024]{1,0:T(8,128)(2,1)S(1)}, u32[]{:S(2)}, u32[]{:S(2)}) collective-permute-start(bf16[512,1024]{1,0:T(8,128)(2,1)S(1)} %join.1.w_ref), channel_id=1, source_target_pairs={{0,2},{2,0},{1,3},{3,1},{4,6},{6,4},{5,7},{7,5},{8,10},{10,8},{9,1... | collective-permute-start | bytes 3145736 | tf_op jit(solution)/shard_map/ppermute | solution.py:460
  31.7 7.1 %forward.1 = (bf16[3,10,64,160]{3,2,1,0:T(8,128)(2,1)S(1)}, bf16[3,10,64,160]{3,2,1,0:T(8,128)(2,1)S(1)}, bf16[3,8,64,160]{3,2,1,0:T(8,128)(2,1)S(1)}, bf16[3,8,64,160]{3,2,1,0:T(8,128)(2,1)S(1)}) custom-call(bf16[512,1024]{1,0:T(8,128)(2,1)S(1)} %join.1.w_ref, bf16[8,384,1024]{2,1,0:T(8,128)(2,1)S(1)} %get-tuple-element.47.x_ref, ...), custom_call_target="tpu_custom_call" | custom-call | bytes 25165824 | tf_op jit(solution)/shard_map/forward/pallas_call | solution.py:394
  38.8 0.1 collective-permute-start.11
  38.9 0.5 %collective-permute-start.12 = (bf16[3,8,64,160]{3,2,1,0:T(8,128)(2,1)S(1)}, bf16[3,8,64,160]{3,2,1,0:T(8,128)(2,1)S(1)}, u32[]{:S(2)}, u32[]{:S(2)}) collective-permute-start(bf16[3,8,64,160]{3,2,1,0:T(8,128)(2,1)S(1)} %get-tuple-element.55), channel_id=1, source_target_pairs={{0,2},{2,0},{1,3},{3,1},{4,6},{6,4},{5,7},{7,5},{8,10},{10,8},{9,1... | collective-permute-start | bytes 1474568 | tf_op jit(solution)/shard_map/ppermute | solution.py:460
  39.4 1.8 %backward_own.1.y_ref = f32[3,512,1024]{2,1,0:T(8,128)S(1)} custom-call(bf16[512,1024]{1,0:T(8,128)(2,1)S(1)} %join.1.w_ref, bf16[3,10,64,160]{3,2,1,0:T(8,128)(2,1)S(1)} %get-tuple-element.53.g_ref), custom_call_target="tpu_custom_call" | custom-call | bytes 6291456 | tf_op jit(solution)/shard_map/backward_own/pallas_call | solution.py:424
  41.2 1.4 %collective-permute-done.12.rs_ref = bf16[3,8,64,160]{3,2,1,0:T(8,128)(2,1)S(1)} collective-permute-done((bf16[3,8,64,160]{3,2,1,0:T(8,128)(2,1)S(1)}, bf16[3,8,64,160]{3,2,1,0:T(8,128)(2,1)S(1)}, u32[]{:S(2)}, u32[]{:S(2)}) %collective-permute-start.12) | collective-permute-done | bytes 491552 | tf_op jit(solution)/shard_map/ppermute | solution.py:460
  42.6 4.0 %backward.1 = (f32[3,8,64,320]{3,2,1,0:T(8,128)}, bf16[3,8,64,320]{3,2,1,0:T(8,128)(2,1)}) custom-call(bf16[512,1024]{1,0:T(8,128)(2,1)S(1)} %collective-permute-done.10.w_ref, bf16[3,10,64,160]{3,2,1,0:T(8,128)(2,1)S(1)} %collective-permute-done.11.g_ref, f32[3,512,1024]{2,1,0:T(8,128)S(1)} %backward_own.1.y_ref, bf16[3,8,64,320]{3,2,1,0:T(8,128)(2,1)S(1)} %bitcast.9, ...), custom_call_target="tpu_custom_call" | custom-call | tf_op jit(solution)/shard_map/backward/pallas_call | solution.py:448
  (19 shorter events, 0.1 us)
Async XLA Ops:
  0.6 8.2 %collective-permute-start.2 = (bf16[3,8,64,320]{3,2,1,0:T(8,128)(2,1)}, bf16[3,8,64,320]{3,2,1,0:T(8,128)(2,1)S(1)}, u32[]{:S(2)}, u32[]{:S(2)}) collective-permute-start(bf16[3,8,64,320]{3,2,1,0:T(8,128)(2,1)} %bitcast.10), channel_id=1, source_target_pairs={{0,2},{2,0},{1,3},{3,1},{4,6},{6,4},{5,7},{7,5},{8,10},{10,8},{9,1... | collective-permute-start | bytes 2949128 | tf_op jit(solution)/shard_map/ppermute | solution.py:460
  1.1 7.7 %collective-permute-start.3 = (bf16[3,8,64,320]{3,2,1,0:T(8,128)(2,1)}, bf16[3,8,64,320]{3,2,1,0:T(8,128)(2,1)S(1)}, u32[]{:S(2)}, u32[]{:S(2)}) collective-permute-start(bf16[3,8,64,320]{3,2,1,0:T(8,128)(2,1)} %bitcast.6), channel_id=1, source_target_pairs={{0,2},{2,0},{1,3},{3,1},{4,6},{6,4},{5,7},{7,5},{8,10},{10,8},{9,1... | collective-permute-start | bytes 2949128 | tf_op jit(solution)/shard_map/ppermute | solution.py:460
  1.2 7.6 %copy-start = (bf16[1,3,8,64,320]{4,3,2,1,0:T(8,128)(2,1)S(1)}, bf16[1,3,8,64,320]{4,3,2,1,0:T(8,128)(2,1)}, u32[]{:S(2)}) copy-start(bf16[1,3,8,64,320]{4,3,2,1,0:T(8,128)(2,1)} %param.7) | copy-start | bytes 2949124
  1.2 7.6 %copy-start.1 = (bf16[1,3,8,64,320]{4,3,2,1,0:T(8,128)(2,1)S(1)}, bf16[1,3,8,64,320]{4,3,2,1,0:T(8,128)(2,1)}, u32[]{:S(2)}) copy-start(bf16[1,3,8,64,320]{4,3,2,1,0:T(8,128)(2,1)} %param.6) | copy-start | bytes 2949124
  3.6 13.4 %collective-permute-start.4 = (bf16[3,3,64,320]{3,2,1,0:T(8,128)(2,1)S(1)}, bf16[3,3,64,320]{3,2,1,0:T(8,128)(2,1)S(1)}, u32[]{:S(2)}, u32[]{:S(2)}) collective-permute-start(bf16[3,3,64,320]{3,2,1,0:T(8,128)(2,1)S(1)} %get-tuple-element.35), channel_id=1, source_target_pairs={{0,1},{1,0},{2,3},{3,2},{4,5},{5,4},{6,7},{7,6},{8,9},{9,8},{10,11... | collective-permute-start | bytes 1105928 | tf_op jit(solution)/shard_map/ppermute | solution.py:465
  6.6 7.5 %collective-permute-start.1 = (bf16[240,256]{1,0:T(8,128)(2,1)S(1)}, bf16[240,256]{1,0:T(8,128)(2,1)S(1)}, u32[]{:S(2)}, u32[]{:S(2)}) collective-permute-start(bf16[240,256]{1,0:T(8,128)(2,1)S(1)} %get-tuple-element.31), channel_id=1, source_target_pairs={{4,0},{12,2},{0,4},{8,6},{6,8},{14,10},{2,12},{10,14},{5,1},{13,3}... | collective-permute-start | bytes 368648 | tf_op jit(solution)/shard_map/ppermute | solution.py:244
  8.2 5.9 %collective-permute-start = (bf16[240,256]{1,0:T(8,128)(2,1)S(1)}, bf16[240,256]{1,0:T(8,128)(2,1)S(1)}, u32[]{:S(2)}, u32[]{:S(2)}) collective-permute-start(bf16[240,256]{1,0:T(8,128)(2,1)S(1)} %get-tuple-element.31), channel_id=1, source_target_pairs={{8,2},{12,6},{2,8},{6,12},{9,3},{13,7},{3,9},{7,13},{24,18},{28,22... | collective-permute-start | bytes 368648 | tf_op jit(solution)/shard_map/ppermute | solution.py:244
  17.0 5.6 %collective-permute-start.5 = (bf16[3,3,64,320]{3,2,1,0:T(8,128)(2,1)S(1)}, bf16[3,3,64,320]{3,2,1,0:T(8,128)(2,1)S(1)}, u32[]{:S(2)}, u32[]{:S(2)}) collective-permute-start(bf16[3,3,64,320]{3,2,1,0:T(8,128)(2,1)S(1)} %collective-permute-done.4.halo_ref), channel_id=1, source_target_pairs={{0,2},{2,0},{1,3},{3,1},{4,6},{6,4},{5,7},{7,5},{8,10},{10,8},{9,1... | collective-permute-start | bytes 1105928 | tf_op jit(solution)/shard_map/ppermute | solution.py:460
  17.8 7.9 %collective-permute-start.9 = (bf16[480,256]{1,0:T(8,128)(2,1)S(1)}, bf16[480,256]{1,0:T(8,128)(2,1)S(1)}, u32[]{:S(2)}, u32[]{:S(2)}) collective-permute-start(bf16[480,256]{1,0:T(8,128)(2,1)S(1)} %constant_dynamic-update-slice_fusion), channel_id=1, source_target_pairs={{0,16},{16,0},{1,17},{17,1},{2,18},{18,2},{3,19},{19,3},{4,20},{20... | collective-permute-start | bytes 737288 | tf_op jit(solution)/shard_map/ppermute | solution.py:251
  19.3 7.7 %collective-permute-start.8 = (bf16[480,256]{1,0:T(8,128)(2,1)S(1)}, bf16[480,256]{1,0:T(8,128)(2,1)S(1)}, u32[]{:S(2)}, u32[]{:S(2)}) collective-permute-start(bf16[480,256]{1,0:T(8,128)(2,1)S(1)} %constant_dynamic-update-slice_fusion), channel_id=1, source_target_pairs={{0,1},{1,0},{2,3},{3,2},{4,5},{5,4},{6,7},{7,6},{8,9},{9,8},{10,11... | collective-permute-start | bytes 737288 | tf_op jit(solution)/shard_map/ppermute | solution.py:250
  20.4 11.3 %copy-start.2 = (f32[320]{0:T(512)S(1)}, f32[320]{0:T(512)}, u32[]{:S(2)}) copy-start(f32[320]{0:T(512)} %refs_2_.1) | copy-start | bytes 3844
  20.4 11.3 %copy-start.3 = (f32[320]{0:T(512)S(1)}, f32[320]{0:T(512)}, u32[]{:S(2)}) copy-start(f32[320]{0:T(512)} %refs_3_.1) | copy-start | bytes 3844
  20.4 4.9 %collective-permute-start.7 = (bf16[240,256]{1,0:T(8,128)(2,1)S(1)}, bf16[240,256]{1,0:T(8,128)(2,1)S(1)}, u32[]{:S(2)}, u32[]{:S(2)}) collective-permute-start(bf16[240,256]{1,0:T(8,128)(2,1)S(1)} %get-tuple-element.46), channel_id=1, source_target_pairs={{4,0},{12,2},{0,4},{8,6},{6,8},{14,10},{2,12},{10,14},{5,1},{13,3}... | collective-permute-start | bytes 368648 | tf_op jit(solution)/shard_map/ppermute | solution.py:245
  22.0 3.3 %collective-permute-start.6 = (bf16[240,256]{1,0:T(8,128)(2,1)S(1)}, bf16[240,256]{1,0:T(8,128)(2,1)S(1)}, u32[]{:S(2)}, u32[]{:S(2)}) collective-permute-start(bf16[240,256]{1,0:T(8,128)(2,1)S(1)} %get-tuple-element.46), channel_id=1, source_target_pairs={{8,2},{12,6},{2,8},{6,12},{9,3},{13,7},{3,9},{7,13},{24,18},{28,22... | collective-permute-start | bytes 368648 | tf_op jit(solution)/shard_map/ppermute | solution.py:245
  27.1 15.5 %collective-permute-start.10 = (bf16[512,1024]{1,0:T(8,128)(2,1)S(1)}, bf16[512,1024]{1,0:T(8,128)(2,1)S(1)}, u32[]{:S(2)}, u32[]{:S(2)}) collective-permute-start(bf16[512,1024]{1,0:T(8,128)(2,1)S(1)} %join.1.w_ref), channel_id=1, source_target_pairs={{0,2},{2,0},{1,3},{3,1},{4,6},{6,4},{5,7},{7,5},{8,10},{10,8},{9,1... | collective-permute-start | bytes 3145736 | tf_op jit(solution)/shard_map/ppermute | solution.py:460
  38.8 3.8 %collective-permute-start.11 = (bf16[3,10,64,160]{3,2,1,0:T(8,128)(2,1)S(1)}, bf16[3,10,64,160]{3,2,1,0:T(8,128)(2,1)S(1)}, u32[]{:S(2)}, u32[]{:S(2)}) collective-permute-start(bf16[3,10,64,160]{3,2,1,0:T(8,128)(2,1)S(1)} %get-tuple-element.52), channel_id=1, source_target_pairs={{0,2},{2,0},{1,3},{3,1},{4,6},{6,4},{5,7},{7,5},{8,10},{10,8},{9,1... | collective-permute-start | bytes 1843208 | tf_op jit(solution)/shard_map/ppermute | solution.py:460
  38.9 3.7 %collective-permute-start.12 = (bf16[3,8,64,160]{3,2,1,0:T(8,128)(2,1)S(1)}, bf16[3,8,64,160]{3,2,1,0:T(8,128)(2,1)S(1)}, u32[]{:S(2)}, u32[]{:S(2)}) collective-permute-start(bf16[3,8,64,160]{3,2,1,0:T(8,128)(2,1)S(1)} %get-tuple-element.55), channel_id=1, source_target_pairs={{0,2},{2,0},{1,3},{3,1},{4,6},{6,4},{5,7},{7,5},{8,10},{10,8},{9,1... | collective-permute-start | bytes 1474568 | tf_op jit(solution)/shard_map/ppermute | solution.py:460

commit v5 on v4

--- a/solution.py
+++ b/solution.py
@@ -47,8 +47,8 @@
 
 
 def prepare_kernel(two, codes_hbm, exps_hbm, spikes_ref, cot_ref, *refs):
-    w_ref, wq_ref, wd_ref = refs[:3]
-    halo_refs, (codes_ref, exps_ref, sems, code_sems) = refs[3:-4], refs[-4:]
+    w_ref, send_ref = refs[:2]
+    halo_refs, (codes_ref, exps_ref, sems, code_sems) = refs[2:-4], refs[-4:]
     if two:
         halos = [(halo_refs[0], 1 - lax.axis_index("rows"))]
     else:
@@ -86,8 +86,8 @@
         for q in range(QUARTERS):
             w_ref[q, dy * outs : (dy + 1) * outs, :] = tap[:, q * width : (q + 1) * width]
     q = quarter_here()
-    wq_ref[...] = w_ref[q]
-    wd_ref[...] = w_ref[QUARTERS - 1 - q]
+    send_ref[: TAPS * outs] = w_ref[q]
+    send_ref[TAPS * outs :] = w_ref[QUARTERS - 1 - q]
     for copy in copies:
         copy.wait()
 
@@ -97,8 +97,7 @@
     steps, rows, cols, ch = spikes.shape
     width = -(-TAPS * ch // (QUARTERS * 128)) * 128
     n_halo = 1 if two else 2
-    w = shape((TAPS * outs, width))
-    out = (shape((QUARTERS, TAPS * outs, width)), w, w) + (shape((steps, 3, cols, ch)),) * n_halo
+    out = (shape((QUARTERS, TAPS * outs, width)), shape((2 * TAPS * outs, width))) + (shape((steps, 3, cols, ch)),) * n_halo
     return call(
         functools.partial(prepare_kernel, two),
         out,
@@ -177,9 +176,10 @@
 
 
 def join_kernel(w_ref, *refs):
-    first, last, (x_ref, y_ref), out_ref = refs[:2], refs[2:4], refs[4:6], refs[-1]
+    rounds, x_ref, y_ref, out_ref = refs[:2], refs[2], refs[3], refs[4]
     size = w_ref.shape[1]
-    rounds = [(first[k], last[k], x_ref.at[k * size : (k + 1) * size], y_ref.at[k * size : (k + 1) * size]) for k in range(2)]
+    halves = [pl.ds(k * size, size) for k in range(2)]
+    rounds = [(rounds[k].at[halves[0]], rounds[k].at[halves[1]], x_ref.at[halves[k]], y_ref.at[halves[k]]) for k in range(2)]
     outs = w_ref.shape[1] // TAPS
     width = w_ref.shape[2]
     main, tail, _ = split_half(2 * outs)
@@ -223,7 +223,7 @@
     out_ref[TAPS * 2 * outs :, :] = jnp.zeros((rest, out_ref.shape[1]), BF16)
 
 
-def fetch_weights(w, wq, wd, after):
+def fetch_weights(w, send, after):
     count = lax.axis_size("dp")
     n_rows = lax.axis_size("rows")
     h = count // 2
@@ -241,16 +241,12 @@
     main, tail, padded = split_half(h * outs)
     if h == 2 and outs % 16 == 0 and n_rows % 2 == 0 and lax.axis_size("groups") == 2:
         moved = [[(a, b) for a, b in pairs(k) if a != b] for k in range(h)]
-        first = [lax.ppermute(wq, ("dp", "tm"), moved[k]) for k in range(h)]
-        last = [lax.ppermute(wd, ("dp", "tm"), moved[k]) for k in range(h)]
-        first, (taps, halos) = lax.optimization_barrier((first, (after[0], after[1])))
-        both = jnp.concatenate(first)
-        held, halos = lax.optimization_barrier((both, halos))
-        after = taps, halos
+        rounds = [lax.ppermute(send, ("dp", "tm"), moved[k]) for k in range(h)]
+        rounds, after = lax.optimization_barrier((rounds, after))
+        both = jnp.concatenate([r[: TAPS * outs] for r in rounds])
         x = lax.ppermute(both, "rows", [(r, r ^ 1) for r in range(n_rows)])
         y = lax.ppermute(both, "groups", [(0, 1), (1, 0)])
-        parts = first + last + [x, y]
-        return lambda w: call(join_kernel, shape((padded, lanes)), [VMEM_SPEC] * 7, 8, "join")(w, *parts), after
+        return lambda w: call(join_kernel, shape((padded, lanes)), [VMEM_SPEC] * 5, 8, "join")(w, *rounds, x, y), after
     w = w.reshape(QUARTERS, TAPS, outs, -1).transpose(1, 2, 0, 3).reshape(TAPS, outs, lanes)
     stack = jnp.stack([lax.ppermute(w, ("dp", "tm"), pairs(k)) for k in range(h)], axis=1)
     stack = jnp.roll(stack, lax.axis_index("dp") % h, axis=1).reshape(TAPS, h * outs, lanes)
@@ -474,11 +470,12 @@
 def on_device(spikes, cotangent, weight_codes, block_exponents, current_bias, threshold):
     two = lax.axis_size("rows") == 2
     spikes, cot = spikes[0], cotangent[0]
-    w, wq, wd, *halos = prepare(two, weight_codes, block_exponents, spikes, cot)
+    w, send, *halos = prepare(two, weight_codes, block_exponents, spikes, cot)
     lanes = QUARTERS * w.shape[2]
     halos = fetch_halos(two, halos)
     taps = build_taps(spikes, cot, swap_cores(spikes), swap_cores(cot), lanes)
-    join, (taps, halos) = fetch_weights(w, wq, wd, (taps, halos))
+    taps, halos = lax.optimization_barrier((taps, halos))
+    join, taps = fetch_weights(w, send, taps)
     halo_taps = [build_halo_taps(x, swap_cores(x), lanes) for x in halos]
     w, taps, halo_taps = lax.optimization_barrier((w, taps, halo_taps))
     weights = join(w)

time: 46.7 us -> 43 us (0.921)
  starting transfers between devices: 16.7 us -> 12.2 us
  waiting for transfers between devices: 7.93 us -> 8.63 us
    ppermute x6, starting transfers between devices: 6.58 us -> 4.2 us  [swap_cores(): return lax.ppermute(x, 'tm', [(0, 1), (1, 0)])]
    ppermute x1, waiting for transfers between devices: 0.42 us -> 2.78 us  [fetch_weights(): y = lax.ppermute(both, 'groups', [(0, 1), (1, 0)])]
    ppermute x4 -> x2, starting transfers between devices: 4.47 us -> 2.24 us  [fetch_weights(): rounds = [lax.ppermute(send, ('dp', 'tm'), moved[k]) for k in range(h)]]
    ppermute x4 -> x2, waiting for transfers between devices: 1.96 us -> 0.01 us  [fetch_weights(): rounds = [lax.ppermute(send, ('dp', 'tm'), moved[k]) for k in range(h)]]
  transfers between devices with their start and end apart: 13 -> 11, of which waited for: 5 -> 4; matrix products, arithmetic and copies ran while one was open for 0% -> 0% of each run, Pallas kernels for 37% -> 40%
where the time goes in v5:
time: 43 us; the launch traced here: 42.8 us
  Pallas kernels  21.1 us (49%)
  starting transfers between devices  12.2 us (28%)
  waiting for transfers between devices  8.63 us (20%)
  between operations  0.76 us (2%)
    pallas_call x1, Pallas kernels, forward(): call(functools.partial(forward_kernel, two), (grad, grad, res, res), [VME...  7.08 us
    pallas_call x1, Pallas kernels, build_taps(): call(taps_kernel, out, [VMEM_SPEC] * 4, 16, 'taps', cost=18 << 20)  5.17 us
    ppermute x6, starting transfers between devices, swap_cores(): return lax.ppermute(x, 'tm', [(0, 1), (1, 0)])  4.2 us
    pallas_call x1, Pallas kernels, backward(): call(backward_kernel, (shape(cot.shape, F32), shape(cot.shape)), [VMEM_SP...  3.96 us
    ppermute x1, starting transfers between devices, fetch_halos(): return [lax.ppermute(halos[0], 'rows', [(0, 1), (1, 0)])]  2.99 us
    ppermute x1, waiting for transfers between devices, fetch_halos(): return [lax.ppermute(halos[0], 'rows', [(0, 1), (1, 0)])]  2.94 us
    ppermute x1, waiting for transfers between devices, fetch_weights(): y = lax.ppermute(both, 'groups', [(0, 1), (1, 0)])  2.78 us
    pallas_call x1, Pallas kernels, prepare(): call(functools.partial(prepare_kernel, two), out, [HBM_SPEC] * 4, 16, 'pr...  2.35 us
  transfers between devices with their start and end apart: 11, of which 4 were waited for; matrix products, arithmetic and copies ran while one was open for 0% of the time, Pallas kernels for 40%

profile of v5, /device:TPU:0, one launch (start us, length us, event | category | flops | bytes accessed | tf_op | source)
XLA Modules:
  0.0 42.8 jit_solution(17058909150303513983)
XLA Ops:
  0.6 0.5 %collective-permute-start.2 = (bf16[3,8,64,320]{3,2,1,0:T(8,128)(2,1)}, bf16[3,8,64,320]{3,2,1,0:T(8,128)(2,1)S(1)}, u32[]{:S(2)}, u32[]{:S(2)}) collective-permute-start(bf16[3,8,64,320]{3,2,1,0:T(8,128)(2,1)} %bitcast.10), channel_id=1, source_target_pairs={{0,2},{2,0},{1,3},{3,1},{4,6},{6,4},{5,7},{7,5},{8,10},{10,8},{9,1... | collective-permute-start | bytes 2949128 | tf_op jit(solution)/shard_map/ppermute | solution.py:456
  1.1 0.1 collective-permute-start.3
  1.2 2.3 %prepare.1 = (bf16[4,240,256]{2,1,0:T(8,128)(2,1)S(1)}, bf16[480,256]{1,0:T(8,128)(2,1)S(1)}, bf16[3,3,64,320]{3,2,1,0:T(8,128)(2,1)S(1)}) custom-call(s32[3,3,80,320]{3,2,1,0:T(8,128)} %bitcast.13, s32[3,10,3,80]{3,2,1,0:T(4,128)} %bitcast.14, bf16[3,8,64,320]{3,2,1,0:T(8,128)(2,1)} %bitcast.11, bf16[3,8,64,320]{3,2,1,0:T(8,128)(2,1)} %bitcast.7), custom_call_target="tpu_custom_call" | custom-call | bytes 2097152 | tf_op jit(solution)/shard_map/prepare/pallas_call | solution.py:101
  3.6 3.0 %collective-permute-start.4 = (bf16[3,3,64,320]{3,2,1,0:T(8,128)(2,1)S(1)}, bf16[3,3,64,320]{3,2,1,0:T(8,128)(2,1)S(1)}, u32[]{:S(2)}, u32[]{:S(2)}) collective-permute-start(bf16[3,3,64,320]{3,2,1,0:T(8,128)(2,1)S(1)} %get-tuple-element.36), channel_id=1, source_target_pairs={{0,1},{1,0},{2,3},{3,2},{4,5},{5,4},{6,7},{7,6},{8,9},{9,8},{10,11... | collective-permute-start | bytes 1105928 | tf_op jit(solution)/shard_map/ppermute | solution.py:461
  6.6 1.6 %collective-permute-start.1 = (bf16[480,256]{1,0:T(8,128)(2,1)S(1)}, bf16[480,256]{1,0:T(8,128)(2,1)S(1)}, u32[]{:S(2)}, u32[]{:S(2)}) collective-permute-start(bf16[480,256]{1,0:T(8,128)(2,1)S(1)} %get-tuple-element.32), channel_id=1, source_target_pairs={{4,0},{12,2},{0,4},{8,6},{6,8},{14,10},{2,12},{10,14},{5,1},{13,3}... | collective-permute-start | bytes 737288 | tf_op jit(solution)/shard_map/ppermute | solution.py:244
  8.2 0.7 %collective-permute-start = (bf16[480,256]{1,0:T(8,128)(2,1)S(1)}, bf16[480,256]{1,0:T(8,128)(2,1)S(1)}, u32[]{:S(2)}, u32[]{:S(2)}) collective-permute-start(bf16[480,256]{1,0:T(8,128)(2,1)S(1)} %get-tuple-element.32), channel_id=1, source_target_pairs={{8,2},{12,6},{2,8},{6,12},{9,3},{13,7},{3,9},{7,13},{24,18},{28,22... | collective-permute-start | bytes 737288 | tf_op jit(solution)/shard_map/ppermute | solution.py:244
  8.9 5.2 %taps.1 = (bf16[8,384,1024]{2,1,0:T(8,128)(2,1)S(1)}, bf16[8,6,64,160]{3,2,1,0:T(8,128)(2,1)S(1)}, bf16[8,6,64,160]{3,2,1,0:T(8,128)(2,1)S(1)}) custom-call(bf16[3,8,64,320]{3,2,1,0:T(8,128)(2,1)S(1)} %bitcast.12, bf16[3,8,64,320]{3,2,1,0:T(8,128)(2,1)S(1)} %collective-permute-done.2.spikes2_ref, bf16[3,8,64,320]{3,2,1,0:T(8,128)(2,1)S(1)} %bitcast.8, ...), custom_call_target="tpu_custom_call" | custom-call | bytes 18874368 | tf_op jit(solution)/shard_map/taps/pallas_call | solution.py:151
  14.0 2.9 %collective-permute-done.4.halo_ref = bf16[3,3,64,320]{3,2,1,0:T(8,128)(2,1)S(1)} collective-permute-done((bf16[3,3,64,320]{3,2,1,0:T(8,128)(2,1)S(1)}, bf16[3,3,64,320]{3,2,1,0:T(8,128)(2,1)S(1)}, u32[]{:S(2)}, u32[]{:S(2)}) %collective-permute-start.4) | collective-permute-done | bytes 368672 | tf_op jit(solution)/shard_map/ppermute | solution.py:461
  17.0 0.5 %collective-permute-start.5 = (bf16[3,3,64,320]{3,2,1,0:T(8,128)(2,1)S(1)}, bf16[3,3,64,320]{3,2,1,0:T(8,128)(2,1)S(1)}, u32[]{:S(2)}, u32[]{:S(2)}) collective-permute-start(bf16[3,3,64,320]{3,2,1,0:T(8,128)(2,1)S(1)} %collective-permute-done.4.halo_ref), channel_id=1, source_target_pairs={{0,2},{2,0},{1,3},{3,1},{4,6},{6,4},{5,7},{7,5},{8,10},{10,8},{9,1... | collective-permute-start | bytes 1105928 | tf_op jit(solution)/shard_map/ppermute | solution.py:456
  17.6 0.0 copy-start.2
  17.6 0.0 copy-start.3
  17.6 1.6 %collective-permute-start.7 = (bf16[480,256]{1,0:T(8,128)(2,1)S(1)}, bf16[480,256]{1,0:T(8,128)(2,1)S(1)}, u32[]{:S(2)}, u32[]{:S(2)}) collective-permute-start(bf16[480,256]{1,0:T(8,128)(2,1)S(1)} %pad_maximum_fusion), channel_id=1, source_target_pairs={{0,16},{16,0},{1,17},{17,1},{2,18},{18,2},{3,19},{19,3},{4,20},{20... | collective-permute-start | bytes 737288 | tf_op jit(solution)/shard_map/ppermute | solution.py:248
  19.2 1.2 %collective-permute-start.6 = (bf16[480,256]{1,0:T(8,128)(2,1)S(1)}, bf16[480,256]{1,0:T(8,128)(2,1)S(1)}, u32[]{:S(2)}, u32[]{:S(2)}) collective-permute-start(bf16[480,256]{1,0:T(8,128)(2,1)S(1)} %pad_maximum_fusion), channel_id=1, source_target_pairs={{0,1},{1,0},{2,3},{3,2},{4,5},{5,4},{6,7},{7,6},{8,9},{9,8},{10,11... | collective-permute-start | bytes 737288 | tf_op jit(solution)/shard_map/ppermute | solution.py:247
  20.4 0.7 %halo_taps.1 = (bf16[2,384,1024]{2,1,0:T(8,128)(2,1)S(1)}, bf16[6,64,160]{2,1,0:T(8,128)(2,1)S(1)}) custom-call(bf16[3,3,64,320]{3,2,1,0:T(8,128)(2,1)S(1)} %collective-permute-done.4.halo_ref, bf16[3,3,64,320]{3,2,1,0:T(8,128)(2,1)S(1)} %collective-permute-done.5.halo2_ref), custom_call_target="tpu_custom_call" | custom-call | bytes 2097152 | tf_op jit(solution)/shard_map/halo_taps/pallas_call | solution.py:170
  21.1 2.8 %collective-permute-done.7.refs_3_ = bf16[480,256]{1,0:T(8,128)(2,1)S(1)} collective-permute-done((bf16[480,256]{1,0:T(8,128)(2,1)S(1)}, bf16[480,256]{1,0:T(8,128)(2,1)S(1)}, u32[]{:S(2)}, u32[]{:S(2)}) %collective-permute-start.7) | collective-permute-done | bytes 245792 | tf_op jit(solution)/shard_map/ppermute | solution.py:248
  23.9 1.5 %collective-permute-done.6.refs_2_ = bf16[480,256]{1,0:T(8,128)(2,1)S(1)} collective-permute-done((bf16[480,256]{1,0:T(8,128)(2,1)S(1)}, bf16[480,256]{1,0:T(8,128)(2,1)S(1)}, u32[]{:S(2)}, u32[]{:S(2)}) %collective-permute-start.6) | collective-permute-done | bytes 245792 | tf_op jit(solution)/shard_map/ppermute | solution.py:247
  25.4 0.1 join.1.w_ref
  25.5 2.5 %collective-permute-start.8 = (bf16[512,1024]{1,0:T(8,128)(2,1)S(1)}, bf16[512,1024]{1,0:T(8,128)(2,1)S(1)}, u32[]{:S(2)}, u32[]{:S(2)}) collective-permute-start(bf16[512,1024]{1,0:T(8,128)(2,1)S(1)} %join.1.w_ref), channel_id=1, source_target_pairs={{0,2},{2,0},{1,3},{3,1},{4,6},{6,4},{5,7},{7,5},{8,10},{10,8},{9,1... | collective-permute-start | bytes 3145736 | tf_op jit(solution)/shard_map/ppermute | solution.py:456
  28.0 7.1 %forward.1 = (bf16[3,10,64,160]{3,2,1,0:T(8,128)(2,1)S(1)}, bf16[3,10,64,160]{3,2,1,0:T(8,128)(2,1)S(1)}, bf16[3,8,64,160]{3,2,1,0:T(8,128)(2,1)S(1)}, bf16[3,8,64,160]{3,2,1,0:T(8,128)(2,1)S(1)}) custom-call(bf16[512,1024]{1,0:T(8,128)(2,1)S(1)} %join.1.w_ref, bf16[8,384,1024]{2,1,0:T(8,128)(2,1)S(1)} %get-tuple-element.49.x_ref, ...), custom_call_target="tpu_custom_call" | custom-call | bytes 25165824 | tf_op jit(solution)/shard_map/forward/pallas_call | solution.py:390
  35.1 0.1 collective-permute-start.9
  35.2 0.5 %collective-permute-start.10 = (bf16[3,8,64,160]{3,2,1,0:T(8,128)(2,1)S(1)}, bf16[3,8,64,160]{3,2,1,0:T(8,128)(2,1)S(1)}, u32[]{:S(2)}, u32[]{:S(2)}) collective-permute-start(bf16[3,8,64,160]{3,2,1,0:T(8,128)(2,1)S(1)} %get-tuple-element.57), channel_id=1, source_target_pairs={{0,2},{2,0},{1,3},{3,1},{4,6},{6,4},{5,7},{7,5},{8,10},{10,8},{9,1... | collective-permute-start | bytes 1474568 | tf_op jit(solution)/shard_map/ppermute | solution.py:456
  35.7 1.8 %backward_own.1.y_ref = f32[3,512,1024]{2,1,0:T(8,128)S(1)} custom-call(bf16[512,1024]{1,0:T(8,128)(2,1)S(1)} %join.1.w_ref, bf16[3,10,64,160]{3,2,1,0:T(8,128)(2,1)S(1)} %get-tuple-element.55.g_ref), custom_call_target="tpu_custom_call" | custom-call | bytes 6291456 | tf_op jit(solution)/shard_map/backward_own/pallas_call | solution.py:420
  37.5 1.4 %collective-permute-done.10.rs_ref = bf16[3,8,64,160]{3,2,1,0:T(8,128)(2,1)S(1)} collective-permute-done((bf16[3,8,64,160]{3,2,1,0:T(8,128)(2,1)S(1)}, bf16[3,8,64,160]{3,2,1,0:T(8,128)(2,1)S(1)}, u32[]{:S(2)}, u32[]{:S(2)}) %collective-permute-start.10) | collective-permute-done | bytes 491552 | tf_op jit(solution)/shard_map/ppermute | solution.py:456
  38.9 4.0 %backward.1 = (f32[3,8,64,320]{3,2,1,0:T(8,128)}, bf16[3,8,64,320]{3,2,1,0:T(8,128)(2,1)}) custom-call(bf16[512,1024]{1,0:T(8,128)(2,1)S(1)} %collective-permute-done.8.w_ref, bf16[3,10,64,160]{3,2,1,0:T(8,128)(2,1)S(1)} %collective-permute-done.9.g_ref, f32[3,512,1024]{2,1,0:T(8,128)S(1)} %backward_own.1.y_ref, bf16[3,8,64,320]{3,2,1,0:T(8,128)(2,1)S(1)} %bitcast.9, ...), custom_call_target="tpu_custom_call" | custom-call | tf_op jit(solution)/shard_map/backward/pallas_call | solution.py:444
  (16 shorter events, 0.1 us)
Async XLA Ops:
  0.6 8.2 %collective-permute-start.2 = (bf16[3,8,64,320]{3,2,1,0:T(8,128)(2,1)}, bf16[3,8,64,320]{3,2,1,0:T(8,128)(2,1)S(1)}, u32[]{:S(2)}, u32[]{:S(2)}) collective-permute-start(bf16[3,8,64,320]{3,2,1,0:T(8,128)(2,1)} %bitcast.10), channel_id=1, source_target_pairs={{0,2},{2,0},{1,3},{3,1},{4,6},{6,4},{5,7},{7,5},{8,10},{10,8},{9,1... | collective-permute-start | bytes 2949128 | tf_op jit(solution)/shard_map/ppermute | solution.py:456
  1.1 7.7 %collective-permute-start.3 = (bf16[3,8,64,320]{3,2,1,0:T(8,128)(2,1)}, bf16[3,8,64,320]{3,2,1,0:T(8,128)(2,1)S(1)}, u32[]{:S(2)}, u32[]{:S(2)}) collective-permute-start(bf16[3,8,64,320]{3,2,1,0:T(8,128)(2,1)} %bitcast.6), channel_id=1, source_target_pairs={{0,2},{2,0},{1,3},{3,1},{4,6},{6,4},{5,7},{7,5},{8,10},{10,8},{9,1... | collective-permute-start | bytes 2949128 | tf_op jit(solution)/shard_map/ppermute | solution.py:456
  1.2 7.6 %copy-start = (bf16[1,3,8,64,320]{4,3,2,1,0:T(8,128)(2,1)S(1)}, bf16[1,3,8,64,320]{4,3,2,1,0:T(8,128)(2,1)}, u32[]{:S(2)}) copy-start(bf16[1,3,8,64,320]{4,3,2,1,0:T(8,128)(2,1)} %param.7) | copy-start | bytes 2949124
  1.2 7.6 %copy-start.1 = (bf16[1,3,8,64,320]{4,3,2,1,0:T(8,128)(2,1)S(1)}, bf16[1,3,8,64,320]{4,3,2,1,0:T(8,128)(2,1)}, u32[]{:S(2)}) copy-start(bf16[1,3,8,64,320]{4,3,2,1,0:T(8,128)(2,1)} %param.6) | copy-start | bytes 2949124
  3.6 13.4 %collective-permute-start.4 = (bf16[3,3,64,320]{3,2,1,0:T(8,128)(2,1)S(1)}, bf16[3,3,64,320]{3,2,1,0:T(8,128)(2,1)S(1)}, u32[]{:S(2)}, u32[]{:S(2)}) collective-permute-start(bf16[3,3,64,320]{3,2,1,0:T(8,128)(2,1)S(1)} %get-tuple-element.36), channel_id=1, source_target_pairs={{0,1},{1,0},{2,3},{3,2},{4,5},{5,4},{6,7},{7,6},{8,9},{9,8},{10,11... | collective-permute-start | bytes 1105928 | tf_op jit(solution)/shard_map/ppermute | solution.py:461
  6.6 10.9 %collective-permute-start.1 = (bf16[480,256]{1,0:T(8,128)(2,1)S(1)}, bf16[480,256]{1,0:T(8,128)(2,1)S(1)}, u32[]{:S(2)}, u32[]{:S(2)}) collective-permute-start(bf16[480,256]{1,0:T(8,128)(2,1)S(1)} %get-tuple-element.32), channel_id=1, source_target_pairs={{4,0},{12,2},{0,4},{8,6},{6,8},{14,10},{2,12},{10,14},{5,1},{13,3}... | collective-permute-start | bytes 737288 | tf_op jit(solution)/shard_map/ppermute | solution.py:244
  8.2 9.4 %collective-permute-start = (bf16[480,256]{1,0:T(8,128)(2,1)S(1)}, bf16[480,256]{1,0:T(8,128)(2,1)S(1)}, u32[]{:S(2)}, u32[]{:S(2)}) collective-permute-start(bf16[480,256]{1,0:T(8,128)(2,1)S(1)} %get-tuple-element.32), channel_id=1, source_target_pairs={{8,2},{12,6},{2,8},{6,12},{9,3},{13,7},{3,9},{7,13},{24,18},{28,22... | collective-permute-start | bytes 737288 | tf_op jit(solution)/shard_map/ppermute | solution.py:244
  17.0 3.4 %collective-permute-start.5 = (bf16[3,3,64,320]{3,2,1,0:T(8,128)(2,1)S(1)}, bf16[3,3,64,320]{3,2,1,0:T(8,128)(2,1)S(1)}, u32[]{:S(2)}, u32[]{:S(2)}) collective-permute-start(bf16[3,3,64,320]{3,2,1,0:T(8,128)(2,1)S(1)} %collective-permute-done.4.halo_ref), channel_id=1, source_target_pairs={{0,2},{2,0},{1,3},{3,1},{4,6},{6,4},{5,7},{7,5},{8,10},{10,8},{9,1... | collective-permute-start | bytes 1105928 | tf_op jit(solution)/shard_map/ppermute | solution.py:456
  17.6 10.4 %copy-start.2 = (f32[320]{0:T(512)S(1)}, f32[320]{0:T(512)}, u32[]{:S(2)}) copy-start(f32[320]{0:T(512)} %refs_2_.1) | copy-start | bytes 3844
  17.6 10.4 %copy-start.3 = (f32[320]{0:T(512)S(1)}, f32[320]{0:T(512)}, u32[]{:S(2)}) copy-start(f32[320]{0:T(512)} %refs_3_.1) | copy-start | bytes 3844
  17.6 6.3 %collective-permute-start.7 = (bf16[480,256]{1,0:T(8,128)(2,1)S(1)}, bf16[480,256]{1,0:T(8,128)(2,1)S(1)}, u32[]{:S(2)}, u32[]{:S(2)}) collective-permute-start(bf16[480,256]{1,0:T(8,128)(2,1)S(1)} %pad_maximum_fusion), channel_id=1, source_target_pairs={{0,16},{16,0},{1,17},{17,1},{2,18},{18,2},{3,19},{19,3},{4,20},{20... | collective-permute-start | bytes 737288 | tf_op jit(solution)/shard_map/ppermute | solution.py:248
  19.2 6.2 %collective-permute-start.6 = (bf16[480,256]{1,0:T(8,128)(2,1)S(1)}, bf16[480,256]{1,0:T(8,128)(2,1)S(1)}, u32[]{:S(2)}, u32[]{:S(2)}) collective-permute-start(bf16[480,256]{1,0:T(8,128)(2,1)S(1)} %pad_maximum_fusion), channel_id=1, source_target_pairs={{0,1},{1,0},{2,3},{3,2},{4,5},{5,4},{6,7},{7,6},{8,9},{9,8},{10,11... | collective-permute-start | bytes 737288 | tf_op jit(solution)/shard_map/ppermute | solution.py:247
  25.5 13.4 %collective-permute-start.8 = (bf16[512,1024]{1,0:T(8,128)(2,1)S(1)}, bf16[512,1024]{1,0:T(8,128)(2,1)S(1)}, u32[]{:S(2)}, u32[]{:S(2)}) collective-permute-start(bf16[512,1024]{1,0:T(8,128)(2,1)S(1)} %join.1.w_ref), channel_id=1, source_target_pairs={{0,2},{2,0},{1,3},{3,1},{4,6},{6,4},{5,7},{7,5},{8,10},{10,8},{9,1... | collective-permute-start | bytes 3145736 | tf_op jit(solution)/shard_map/ppermute | solution.py:456
  35.1 3.8 %collective-permute-start.9 = (bf16[3,10,64,160]{3,2,1,0:T(8,128)(2,1)S(1)}, bf16[3,10,64,160]{3,2,1,0:T(8,128)(2,1)S(1)}, u32[]{:S(2)}, u32[]{:S(2)}) collective-permute-start(bf16[3,10,64,160]{3,2,1,0:T(8,128)(2,1)S(1)} %get-tuple-element.54), channel_id=1, source_target_pairs={{0,2},{2,0},{1,3},{3,1},{4,6},{6,4},{5,7},{7,5},{8,10},{10,8},{9,1... | collective-permute-start | bytes 1843208 | tf_op jit(solution)/shard_map/ppermute | solution.py:456
  35.2 3.7 %collective-permute-start.10 = (bf16[3,8,64,160]{3,2,1,0:T(8,128)(2,1)S(1)}, bf16[3,8,64,160]{3,2,1,0:T(8,128)(2,1)S(1)}, u32[]{:S(2)}, u32[]{:S(2)}) collective-permute-start(bf16[3,8,64,160]{3,2,1,0:T(8,128)(2,1)S(1)} %get-tuple-element.57), channel_id=1, source_target_pairs={{0,2},{2,0},{1,3},{3,1},{4,6},{6,4},{5,7},{7,5},{8,10},{10,8},{9,1... | collective-permute-start | bytes 1474568 | tf_op jit(solution)/shard_map/ppermute | solution.py:456

commit v6 on v5

--- a/solution.py
+++ b/solution.py
@@ -175,52 +175,84 @@
     return main, half - main, TAPS * main + -(-TAPS * (half - main) // 128) * 128
 
 
-def join_kernel(w_ref, *refs):
-    rounds, x_ref, y_ref, out_ref = refs[:2], refs[2], refs[3], refs[4]
+def put_rows(out_ref, part, lane, pos):
+    outs, width = part.shape[0] // TAPS, part.shape[1]
+    main, tail, _ = split_half(2 * outs)
+    at = pl.ds(pl.multiple_of(lane * width, width), width)
+    for dy in range(TAPS):
+        for o in range(0, outs, 16):
+            c = pos * outs + o
+            to = dy * main + c if c < main else TAPS * main + dy * tail + c - main
+            out_ref[to : to + 16, at] = part[dy * outs + o : dy * outs + o + 16, :]
+
+
+def put_shards(out_ref, own_parts, rounds):
+    z, core = lax.axis_index("dp"), lax.axis_index("tm")
+    own = core == z // 2
+
+    def put_all(parts, pos):
+        for part, lane in parts:
+            put_rows(out_ref, part, lane, pos)
+
+    for even in range(2):
+
+        @pl.when(lax.rem(z, 2) == even)
+        def _():
+            pl.when(own)(lambda: put_all(own_parts, even))
+            pl.when(jnp.logical_not(own))(lambda: put_all(rounds[0], even))
+            put_all(rounds[1], 1 - even)
+
+    used = 2 * rounds[0][0][0].shape[0]
+    out_ref[used:, :] = jnp.zeros((out_ref.shape[0] - used, out_ref.shape[1]), BF16)
+
+
+def lanes_here():
+    q = quarter_here()
+    return (q, QUARTERS - 1 - q), (jnp.bitwise_xor(q, 1), jnp.bitwise_xor(q, 2))
+
+
+def join_kernel(w_ref, first_ref, second_ref, x_ref, y_ref, out_ref):
     size = w_ref.shape[1]
     halves = [pl.ds(k * size, size) for k in range(2)]
-    rounds = [(rounds[k].at[halves[0]], rounds[k].at[halves[1]], x_ref.at[halves[k]], y_ref.at[halves[k]]) for k in range(2)]
-    outs = w_ref.shape[1] // TAPS
-    width = w_ref.shape[2]
-    main, tail, _ = split_half(2 * outs)
-    z, core, q = lax.axis_index("dp"), lax.axis_index("tm"), quarter_here()
-    place = lax.rem(z, 2)
-    own = core == z // 2
-
-    def put(part, lane, pos):
-        at = pl.ds(pl.multiple_of(lane * width, width), width)
-        for dy in range(TAPS):
-            for o in range(0, outs, 16):
-                c = pos * outs + o
-                to = dy * main + c if c < main else TAPS * main + dy * tail + c - main
-                out_ref[to : to + 16, at] = part[dy * outs + o : dy * outs + o + 16, :]
-
-    def put_round(k, pos):
-        lanes_of = (q, QUARTERS - 1 - q, jnp.bitwise_xor(q, 1), jnp.bitwise_xor(q, 2))
-        if k == 1:
-            for part, lane in zip(rounds[1], lanes_of):
-                put(part, lane, pos)
-            return
-
-        @pl.when(own)
-        def _():
-            for n in range(QUARTERS):
-                put(w_ref[n], n, pos)
-
-        @pl.when(jnp.logical_not(own))
-        def _():
-            for part, lane in zip(rounds[0], lanes_of):
-                put(part, lane, pos)
-
-    for even in range(2):
-
-        @pl.when(place == even)
-        def _():
-            put_round(0, even)
-            put_round(1, 1 - even)
-
-    rest = out_ref.shape[0] - TAPS * 2 * outs
-    out_ref[TAPS * 2 * outs :, :] = jnp.zeros((rest, out_ref.shape[1]), BF16)
+    here, there = lanes_here()
+    rounds = []
+    for k, ref in enumerate((first_ref, second_ref)):
+        parts = ref.at[halves[0]], ref.at[halves[1]], x_ref.at[halves[k]], y_ref.at[halves[k]]
+        rounds.append(list(zip(parts, here + there)))
+    put_shards(out_ref, [(w_ref.at[n], n) for n in range(QUARTERS)], rounds)
+
+
+def partial_kernel(w_ref, first_ref, second_ref, x_ref, halo_ref, p_ref, wh_ref):
+    size, width = w_ref.shape[1:]
+    halves = [pl.ds(k * size, size) for k in range(2)]
+    here, _ = lanes_here()
+    rounds = [[(ref.at[halves[n]], n) for n in range(2)] for ref in (first_ref, second_ref)]
+    put_shards(wh_ref, [(w_ref.at[here[n]], n) for n in range(2)], rounds)
+    for x, h, strip in strips(x_ref, halo_ref):
+        p_ref[pl.ds(strip, 2)] = dot(take_lanes(x, h, here, width), wh_ref[...], ((1,), (1,))).reshape(2, -1, wh_ref.shape[0])
+
+
+def take_lanes(x, h, lanes, width):
+    parts = [x[pl.ds(h, 2), :, pl.ds(pl.multiple_of(n * width, width), width)] for n in lanes]
+    return jnp.concatenate([part.reshape(-1, width) for part in parts], axis=1)
+
+
+def strips(x_ref, halo_ref):
+    rows = x_ref.shape[0]
+    flip = lax.axis_index("rows") == 1
+    todo = []
+    for i in range(0, rows, 2):
+        h = jnp.where(flip, rows - 2 - i, i)
+        todo.append((x_ref, h, jnp.where(flip, h + 2, h + 1)))
+    return todo + [(halo_ref, 0, jnp.where(flip, 0, rows + 1))]
+
+
+def partial_currents(two, w, rounds, taps, halo_taps):
+    x = taps[0]
+    main, tail, padded = split_half(2 * w.shape[1] // TAPS)
+    out = shape((x.shape[0] + 3, x.shape[1], padded), F32)
+    scratch = [pltpu.VMEM((padded, 2 * w.shape[2]), BF16)]
+    return call(partial_kernel, out, [VMEM_SPEC] * 5, 12, "partial", scratch)(w, *rounds, x, halo_taps[0][0])
 
 
 def fetch_weights(w, send, after):
@@ -243,24 +275,25 @@
         moved = [[(a, b) for a, b in pairs(k) if a != b] for k in range(h)]
         rounds = [lax.ppermute(send, ("dp", "tm"), moved[k]) for k in range(h)]
         rounds, after = lax.optimization_barrier((rounds, after))
+        first = functools.partial(partial_currents, True, w, rounds) if n_rows == 2 else None
         both = jnp.concatenate([r[: TAPS * outs] for r in rounds])
         x = lax.ppermute(both, "rows", [(r, r ^ 1) for r in range(n_rows)])
         y = lax.ppermute(both, "groups", [(0, 1), (1, 0)])
-        return lambda w: call(join_kernel, shape((padded, lanes)), [VMEM_SPEC] * 5, 8, "join")(w, *rounds, x, y), after
+        return lambda w: call(join_kernel, shape((padded, lanes)), [VMEM_SPEC] * 5, 8, "join")(w, *rounds, x, y), after, first
     w = w.reshape(QUARTERS, TAPS, outs, -1).transpose(1, 2, 0, 3).reshape(TAPS, outs, lanes)
     stack = jnp.stack([lax.ppermute(w, ("dp", "tm"), pairs(k)) for k in range(h)], axis=1)
     stack = jnp.roll(stack, lax.axis_index("dp") % h, axis=1).reshape(TAPS, h * outs, lanes)
     rest = jnp.zeros((padded - TAPS * h * outs, lanes), BF16)
     joined = jnp.concatenate([stack[:, :main].reshape(-1, lanes), stack[:, main:].reshape(-1, lanes), rest])
-    return lambda w: joined, after
-
-
-def forward_kernel(two, w_ref, x_ref, s_ref, c_ref, *refs):
+    return lambda w: joined, after, None
+
+
+def forward_kernel(two, started, w_ref, x_ref, s_ref, c_ref, *refs):
     if two:
         halos = [refs[:2]]
     else:
         halos = [refs[:2], refs[2:4]]
-    bias_ref, thr_ref, gk_ref, gs_ref, rk_ref, rs_ref, p_ref = refs[2 * len(halos) :]
+    bias_ref, thr_ref, *begun, gk_ref, gs_ref, rk_ref, rs_ref, p_ref = refs[2 * len(halos) :]
     core, row = lax.axis_index("tm"), lax.axis_index("rows")
     rows, times, cols, half = s_ref.shape
     lanes = x_ref.shape[2]
@@ -276,9 +309,18 @@
     shift = half_row(bias_ref) - thr
     at_of = [lax.rem(core + part, 2) * steps + tl for part in range(2) for tl in range(steps)]
 
-    def currents(x, strip):
-        p = dot(x.reshape(-1, lanes), w_ref[...], ((1,), (1,)))
-        p_ref[pl.ds(strip, 2)] = p.reshape(2, times * cols, -1)
+    if started:
+        _, there = lanes_here()
+        width = lanes // QUARTERS
+        w_there = jnp.concatenate([w_ref[:, pl.ds(pl.multiple_of(n * width, width), width)] for n in there], axis=1)
+
+    def currents(x, h, strip):
+        if started:
+            p = dot(take_lanes(x, h, there, width), w_there, ((1,), (1,)))
+            p_ref[pl.ds(strip, 2)] = begun[0][pl.ds(strip, 2)] + p.reshape(2, times * cols, -1)
+        else:
+            p = dot(x[pl.ds(h, 2)].reshape(-1, lanes), w_ref[...], ((1,), (1,)))
+            p_ref[pl.ds(strip, 2)] = p.reshape(2, times * cols, -1)
 
     def scan(strip, cot, spike, g, h, keep=None):
         for w0 in range(0, cols, chunk):
@@ -348,12 +390,8 @@
                 scan_own(h, jnp.where(flip, h + 1, h))
 
         done = 0
-        for i in range(rows // 2 + 1):
-            if i < rows // 2:
-                h = jnp.where(flip, rows - 2 - 2 * i, 2 * i)
-                currents(x_ref[pl.ds(h, 2)], jnp.where(flip, h + 2, h + 1))
-            else:
-                currents(halos[0][0][...], jnp.where(flip, 0, rows + 1))
+        for i, (x, h, strip) in enumerate(strips(x_ref, halos[0][0])):
+            currents(x, h, strip)
             while done <= 2 * i - 2:
                 scan_at(done)
                 done += 1
@@ -362,11 +400,11 @@
             done += 1
     else:
         last = lax.axis_size("rows") - 1
-        currents(halos[0][0][...], 0)
-        currents(halos[1][0][...], rows + 2)
+        currents(halos[0][0], 0, 0)
+        currents(halos[1][0], 0, rows + 2)
 
         def pair(i, carry):
-            currents(x_ref[pl.ds(2 * i, 2)], 2 * i + 2)
+            currents(x_ref, 2 * i, 2 * i + 2)
             return carry
 
         lax.fori_loop(0, rows // 2, pair, 0)
@@ -380,15 +418,15 @@
         scan_halo(1, rows + 1, rows + 1, jnp.where(row == last, 0.0, 1.0))
 
 
-def forward(two, weights, taps, halo_taps, bias, thr):
+def forward(two, weights, taps, halo_taps, bias, thr, begun=()):
     x, s, c = taps
     rows, times, cols, half = s.shape
     steps = times // 2
-    args = [weights, x, s, c] + [a for pair in halo_taps for a in pair] + [bias, thr]
+    args = [weights, x, s, c] + [a for pair in halo_taps for a in pair] + [bias, thr, *begun]
     grad = shape((steps, rows + 2, cols, half))
     res = shape((steps, rows, cols, half))
     return call(
-        functools.partial(forward_kernel, two),
+        functools.partial(forward_kernel, two, bool(begun)),
         (grad, grad, res, res),
         [VMEM_SPEC] * len(args),
         16,
@@ -475,12 +513,13 @@
     halos = fetch_halos(two, halos)
     taps = build_taps(spikes, cot, swap_cores(spikes), swap_cores(cot), lanes)
     taps, halos = lax.optimization_barrier((taps, halos))
-    join, taps = fetch_weights(w, send, taps)
+    join, taps, first = fetch_weights(w, send, taps)
     halo_taps = [build_halo_taps(x, swap_cores(x), lanes) for x in halos]
-    w, taps, halo_taps = lax.optimization_barrier((w, taps, halo_taps))
+    begun = [first(taps, halo_taps)] if first else []
+    w, taps, halo_taps, begun = lax.optimization_barrier((w, taps, halo_taps, begun))
     weights = join(w)
     weights2 = swap_cores(weights)
-    keep, send, res_keep, res_send = forward(two, weights, taps, halo_taps, current_bias, threshold)
+    keep, send, res_keep, res_send = forward(two, weights, taps, halo_taps, current_bias, threshold, begun)
     arrived = swap_cores(send)
     res_arrived = swap_cores(res_send)
     y = backward_own(weights, keep)

time: 43 us -> 41.2 us (0.958)
  waiting for transfers between devices: 8.63 us -> 6.3 us
  Pallas kernels: 21.1 us -> 21.7 us
    ppermute x1, waiting for transfers between devices: 2.78 us -> 0.45 us  [fetch_weights(): y = lax.ppermute(both, 'groups', [(0, 1), (1, 0)])]
    pallas_call x1 -> x2, Pallas kernels: 7.08 us -> 7.59 us  [the longest x1 5.29 us: forward(): call(functools.partial(forward_kernel, two, bool(begun)), (grad, grad, re...]
  transfers between devices with their start and end apart: 11 -> 11, of which waited for: 4 -> 4; matrix products, arithmetic and copies ran while one was open for 0% -> 0% of each run, Pallas kernels for 40% -> 43%
where the time goes in v6:
time: 41.2 us; the launch traced here: 41 us
  Pallas kernels  21.7 us (53%)
  starting transfers between devices  12.2 us (30%)
  waiting for transfers between devices  6.3 us (15%)
  between operations  0.76 us (2%)
    pallas_call x1, Pallas kernels, forward(): call(functools.partial(forward_kernel, two, bool(begun)), (grad, grad, re...  5.29 us
    pallas_call x1, Pallas kernels, build_taps(): call(taps_kernel, out, [VMEM_SPEC] * 4, 16, 'taps', cost=18 << 20)  5.17 us
    ppermute x6, starting transfers between devices, swap_cores(): return lax.ppermute(x, 'tm', [(0, 1), (1, 0)])  4.2 us
    pallas_call x1, Pallas kernels, backward(): call(backward_kernel, (shape(cot.shape, F32), shape(cot.shape)), [VMEM_SP...  3.97 us
    ppermute x1, starting transfers between devices, fetch_halos(): return [lax.ppermute(halos[0], 'rows', [(0, 1), (1, 0)])]  2.99 us
    ppermute x1, waiting for transfers between devices, fetch_halos(): return [lax.ppermute(halos[0], 'rows', [(0, 1), (1, 0)])]  2.94 us
    pallas_call x1, Pallas kernels, prepare(): call(functools.partial(prepare_kernel, two), out, [HBM_SPEC] * 4, 16, 'pr...  2.35 us
    pallas_call x1, Pallas kernels, partial_currents(): call(partial_kernel, out, [VMEM_SPEC] * 5, 12, 'partial', scratch)  2.3 us
  transfers between devices with their start and end apart: 11, of which 4 were waited for; matrix products, arithmetic and copies ran while one was open for 0% of the time, Pallas kernels for 43%

profile of v6, /device:TPU:0, one launch (start us, length us, event | category | flops | bytes accessed | tf_op | source)
XLA Modules:
  0.0 41.0 jit_solution(16244987539464086619)
XLA Ops:
  0.6 0.5 %collective-permute-start.2 = (bf16[3,8,64,320]{3,2,1,0:T(8,128)(2,1)}, bf16[3,8,64,320]{3,2,1,0:T(8,128)(2,1)S(1)}, u32[]{:S(2)}, u32[]{:S(2)}) collective-permute-start(bf16[3,8,64,320]{3,2,1,0:T(8,128)(2,1)} %bitcast.10), channel_id=1, source_target_pairs={{0,2},{2,0},{1,3},{3,1},{4,6},{6,4},{5,7},{7,5},{8,10},{10,8},{9,1... | collective-permute-start | bytes 2949128 | tf_op jit(solution)/shard_map/ppermute | solution.py:494
  1.1 0.1 collective-permute-start.3
  1.2 2.3 %prepare.1 = (bf16[4,240,256]{2,1,0:T(8,128)(2,1)S(1)}, bf16[480,256]{1,0:T(8,128)(2,1)S(1)}, bf16[3,3,64,320]{3,2,1,0:T(8,128)(2,1)S(1)}) custom-call(s32[3,3,80,320]{3,2,1,0:T(8,128)} %bitcast.13, s32[3,10,3,80]{3,2,1,0:T(4,128)} %bitcast.14, bf16[3,8,64,320]{3,2,1,0:T(8,128)(2,1)} %bitcast.11, bf16[3,8,64,320]{3,2,1,0:T(8,128)(2,1)} %bitcast.7), custom_call_target="tpu_custom_call" | custom-call | bytes 2097152 | tf_op jit(solution)/shard_map/prepare/pallas_call | solution.py:101
  3.6 3.0 %collective-permute-start.4 = (bf16[3,3,64,320]{3,2,1,0:T(8,128)(2,1)S(1)}, bf16[3,3,64,320]{3,2,1,0:T(8,128)(2,1)S(1)}, u32[]{:S(2)}, u32[]{:S(2)}) collective-permute-start(bf16[3,3,64,320]{3,2,1,0:T(8,128)(2,1)S(1)} %get-tuple-element.37), channel_id=1, source_target_pairs={{0,1},{1,0},{2,3},{3,2},{4,5},{5,4},{6,7},{7,6},{8,9},{9,8},{10,11... | collective-permute-start | bytes 1105928 | tf_op jit(solution)/shard_map/ppermute | solution.py:499
  6.6 1.6 %collective-permute-start.1 = (bf16[480,256]{1,0:T(8,128)(2,1)S(1)}, bf16[480,256]{1,0:T(8,128)(2,1)S(1)}, u32[]{:S(2)}, u32[]{:S(2)}) collective-permute-start(bf16[480,256]{1,0:T(8,128)(2,1)S(1)} %get-tuple-element.33), channel_id=1, source_target_pairs={{4,0},{12,2},{0,4},{8,6},{6,8},{14,10},{2,12},{10,14},{5,1},{13,3}... | collective-permute-start | bytes 737288 | tf_op jit(solution)/shard_map/ppermute | solution.py:276
  8.2 0.7 %collective-permute-start = (bf16[480,256]{1,0:T(8,128)(2,1)S(1)}, bf16[480,256]{1,0:T(8,128)(2,1)S(1)}, u32[]{:S(2)}, u32[]{:S(2)}) collective-permute-start(bf16[480,256]{1,0:T(8,128)(2,1)S(1)} %get-tuple-element.33), channel_id=1, source_target_pairs={{8,2},{12,6},{2,8},{6,12},{9,3},{13,7},{3,9},{7,13},{24,18},{28,22... | collective-permute-start | bytes 737288 | tf_op jit(solution)/shard_map/ppermute | solution.py:276
  8.9 5.2 %taps.1 = (bf16[8,384,1024]{2,1,0:T(8,128)(2,1)S(1)}, bf16[8,6,64,160]{3,2,1,0:T(8,128)(2,1)S(1)}, bf16[8,6,64,160]{3,2,1,0:T(8,128)(2,1)S(1)}) custom-call(bf16[3,8,64,320]{3,2,1,0:T(8,128)(2,1)S(1)} %bitcast.12, bf16[3,8,64,320]{3,2,1,0:T(8,128)(2,1)S(1)} %collective-permute-done.2.spikes2_ref, bf16[3,8,64,320]{3,2,1,0:T(8,128)(2,1)S(1)} %bitcast.8, ...), custom_call_target="tpu_custom_call" | custom-call | bytes 18874368 | tf_op jit(solution)/shard_map/taps/pallas_call | solution.py:151
  14.0 2.9 %collective-permute-done.4.halo_ref = bf16[3,3,64,320]{3,2,1,0:T(8,128)(2,1)S(1)} collective-permute-done((bf16[3,3,64,320]{3,2,1,0:T(8,128)(2,1)S(1)}, bf16[3,3,64,320]{3,2,1,0:T(8,128)(2,1)S(1)}, u32[]{:S(2)}, u32[]{:S(2)}) %collective-permute-start.4) | collective-permute-done | bytes 368672 | tf_op jit(solution)/shard_map/ppermute | solution.py:499
  17.0 0.5 %collective-permute-start.5 = (bf16[3,3,64,320]{3,2,1,0:T(8,128)(2,1)S(1)}, bf16[3,3,64,320]{3,2,1,0:T(8,128)(2,1)S(1)}, u32[]{:S(2)}, u32[]{:S(2)}) collective-permute-start(bf16[3,3,64,320]{3,2,1,0:T(8,128)(2,1)S(1)} %collective-permute-done.4.halo_ref), channel_id=1, source_target_pairs={{0,2},{2,0},{1,3},{3,1},{4,6},{6,4},{5,7},{7,5},{8,10},{10,8},{9,1... | collective-permute-start | bytes 1105928 | tf_op jit(solution)/shard_map/ppermute | solution.py:494
  17.6 1.6 %collective-permute-start.7 = (bf16[480,256]{1,0:T(8,128)(2,1)S(1)}, bf16[480,256]{1,0:T(8,128)(2,1)S(1)}, u32[]{:S(2)}, u32[]{:S(2)}) collective-permute-start(bf16[480,256]{1,0:T(8,128)(2,1)S(1)} %pad_maximum_fusion), channel_id=1, source_target_pairs={{0,16},{16,0},{1,17},{17,1},{2,18},{18,2},{3,19},{19,3},{4,20},{20... | collective-permute-start | bytes 737288 | tf_op jit(solution)/shard_map/ppermute | solution.py:281
  19.1 1.2 %collective-permute-start.6 = (bf16[480,256]{1,0:T(8,128)(2,1)S(1)}, bf16[480,256]{1,0:T(8,128)(2,1)S(1)}, u32[]{:S(2)}, u32[]{:S(2)}) collective-permute-start(bf16[480,256]{1,0:T(8,128)(2,1)S(1)} %pad_maximum_fusion), channel_id=1, source_target_pairs={{0,1},{1,0},{2,3},{3,2},{4,5},{5,4},{6,7},{7,6},{8,9},{9,8},{10,11... | collective-permute-start | bytes 737288 | tf_op jit(solution)/shard_map/ppermute | solution.py:280
  20.4 0.7 %halo_taps.1 = (bf16[2,384,1024]{2,1,0:T(8,128)(2,1)S(1)}, bf16[6,64,160]{2,1,0:T(8,128)(2,1)S(1)}) custom-call(bf16[3,3,64,320]{3,2,1,0:T(8,128)(2,1)S(1)} %collective-permute-done.4.halo_ref, bf16[3,3,64,320]{3,2,1,0:T(8,128)(2,1)S(1)} %collective-permute-done.5.halo2_ref), custom_call_target="tpu_custom_call" | custom-call | bytes 2097152 | tf_op jit(solution)/shard_map/halo_taps/pallas_call | solution.py:170
  21.0 2.3 %partial.1.refs_4_ = f32[11,384,512]{2,1,0:T(8,128)S(1)} custom-call(bf16[4,240,256]{2,1,0:T(8,128)(2,1)S(1)} %get-tuple-element.49.w_ref, bf16[480,256]{1,0:T(8,128)(2,1)S(1)} %collective-permute-done.first_ref, bf16[480,256]{1,0:T(8,128)(2,1)S(1)} %collective-permute-done.1.second_ref, bf16[8,384,1024]{2,1,0:T(8,128)(2,1)S(1)} %get-tuple-element.50.x_ref, ...), custom_call_target="tpu_custom_call" | custom-call | tf_op jit(solution)/shard_map/partial/pallas_call | solution.py:255
  23.4 0.0 copy-start.2
  23.4 0.5 %collective-permute-done.7.y_ref = bf16[480,256]{1,0:T(8,128)(2,1)S(1)} collective-permute-done((bf16[480,256]{1,0:T(8,128)(2,1)S(1)}, bf16[480,256]{1,0:T(8,128)(2,1)S(1)}, u32[]{:S(2)}, u32[]{:S(2)}) %collective-permute-start.7) | collective-permute-done | bytes 245792 | tf_op jit(solution)/shard_map/ppermute | solution.py:281
  23.8 1.5 %collective-permute-done.6.x_ref = bf16[480,256]{1,0:T(8,128)(2,1)S(1)} collective-permute-done((bf16[480,256]{1,0:T(8,128)(2,1)S(1)}, bf16[480,256]{1,0:T(8,128)(2,1)S(1)}, u32[]{:S(2)}, u32[]{:S(2)}) %collective-permute-start.6) | collective-permute-done | bytes 245792 | tf_op jit(solution)/shard_map/ppermute | solution.py:280
  25.3 0.1 join.1.w_ref
  25.5 2.5 %collective-permute-start.8 = (bf16[512,1024]{1,0:T(8,128)(2,1)S(1)}, bf16[512,1024]{1,0:T(8,128)(2,1)S(1)}, u32[]{:S(2)}, u32[]{:S(2)}) collective-permute-start(bf16[512,1024]{1,0:T(8,128)(2,1)S(1)} %join.1.w_ref), channel_id=1, source_target_pairs={{0,2},{2,0},{1,3},{3,1},{4,6},{6,4},{5,7},{7,5},{8,10},{10,8},{9,1... | collective-permute-start | bytes 3145736 | tf_op jit(solution)/shard_map/ppermute | solution.py:494
  28.0 5.3 %forward.1 = (bf16[3,10,64,160]{3,2,1,0:T(8,128)(2,1)S(1)}, bf16[3,10,64,160]{3,2,1,0:T(8,128)(2,1)S(1)}, bf16[3,8,64,160]{3,2,1,0:T(8,128)(2,1)S(1)}, bf16[3,8,64,160]{3,2,1,0:T(8,128)(2,1)S(1)}) custom-call(bf16[512,1024]{1,0:T(8,128)(2,1)S(1)} %join.1.w_ref, bf16[8,384,1024]{2,1,0:T(8,128)(2,1)S(1)} %get-tuple-element.50.x_ref, ...), custom_call_target="tpu_custom_call" | custom-call | bytes 25165824 | tf_op jit(solution)/shard_map/forward/pallas_call | solution.py:428
  33.3 0.1 collective-permute-start.9
  33.4 0.5 %collective-permute-start.10 = (bf16[3,8,64,160]{3,2,1,0:T(8,128)(2,1)S(1)}, bf16[3,8,64,160]{3,2,1,0:T(8,128)(2,1)S(1)}, u32[]{:S(2)}, u32[]{:S(2)}) collective-permute-start(bf16[3,8,64,160]{3,2,1,0:T(8,128)(2,1)S(1)} %get-tuple-element.59), channel_id=1, source_target_pairs={{0,2},{2,0},{1,3},{3,1},{4,6},{6,4},{5,7},{7,5},{8,10},{10,8},{9,1... | collective-permute-start | bytes 1474568 | tf_op jit(solution)/shard_map/ppermute | solution.py:494
  33.9 1.8 %backward_own.1.y_ref = f32[3,512,1024]{2,1,0:T(8,128)S(1)} custom-call(bf16[512,1024]{1,0:T(8,128)(2,1)S(1)} %join.1.w_ref, bf16[3,10,64,160]{3,2,1,0:T(8,128)(2,1)S(1)} %get-tuple-element.57.g_ref), custom_call_target="tpu_custom_call" | custom-call | bytes 6291456 | tf_op jit(solution)/shard_map/backward_own/pallas_call | solution.py:458
  35.7 1.4 %collective-permute-done.10.rs_ref = bf16[3,8,64,160]{3,2,1,0:T(8,128)(2,1)S(1)} collective-permute-done((bf16[3,8,64,160]{3,2,1,0:T(8,128)(2,1)S(1)}, bf16[3,8,64,160]{3,2,1,0:T(8,128)(2,1)S(1)}, u32[]{:S(2)}, u32[]{:S(2)}) %collective-permute-start.10) | collective-permute-done | bytes 491552 | tf_op jit(solution)/shard_map/ppermute | solution.py:494
  37.0 4.0 %backward.1 = (f32[3,8,64,320]{3,2,1,0:T(8,128)}, bf16[3,8,64,320]{3,2,1,0:T(8,128)(2,1)}) custom-call(bf16[512,1024]{1,0:T(8,128)(2,1)S(1)} %collective-permute-done.8.w_ref, bf16[3,10,64,160]{3,2,1,0:T(8,128)(2,1)S(1)} %collective-permute-done.9.g_ref, f32[3,512,1024]{2,1,0:T(8,128)S(1)} %backward_own.1.y_ref, bf16[3,8,64,320]{3,2,1,0:T(8,128)(2,1)S(1)} %bitcast.9, ...), custom_call_target="tpu_custom_call" | custom-call | tf_op jit(solution)/shard_map/backward/pallas_call | solution.py:482
  (17 shorter events, 0.1 us)
Async XLA Ops:
  0.6 8.2 %collective-permute-start.2 = (bf16[3,8,64,320]{3,2,1,0:T(8,128)(2,1)}, bf16[3,8,64,320]{3,2,1,0:T(8,128)(2,1)S(1)}, u32[]{:S(2)}, u32[]{:S(2)}) collective-permute-start(bf16[3,8,64,320]{3,2,1,0:T(8,128)(2,1)} %bitcast.10), channel_id=1, source_target_pairs={{0,2},{2,0},{1,3},{3,1},{4,6},{6,4},{5,7},{7,5},{8,10},{10,8},{9,1... | collective-permute-start | bytes 2949128 | tf_op jit(solution)/shard_map/ppermute | solution.py:494
  1.1 7.7 %collective-permute-start.3 = (bf16[3,8,64,320]{3,2,1,0:T(8,128)(2,1)}, bf16[3,8,64,320]{3,2,1,0:T(8,128)(2,1)S(1)}, u32[]{:S(2)}, u32[]{:S(2)}) collective-permute-start(bf16[3,8,64,320]{3,2,1,0:T(8,128)(2,1)} %bitcast.6), channel_id=1, source_target_pairs={{0,2},{2,0},{1,3},{3,1},{4,6},{6,4},{5,7},{7,5},{8,10},{10,8},{9,1... | collective-permute-start | bytes 2949128 | tf_op jit(solution)/shard_map/ppermute | solution.py:494
  1.2 7.6 %copy-start = (bf16[1,3,8,64,320]{4,3,2,1,0:T(8,128)(2,1)S(1)}, bf16[1,3,8,64,320]{4,3,2,1,0:T(8,128)(2,1)}, u32[]{:S(2)}) copy-start(bf16[1,3,8,64,320]{4,3,2,1,0:T(8,128)(2,1)} %param.7) | copy-start | bytes 2949124
  1.2 7.6 %copy-start.1 = (bf16[1,3,8,64,320]{4,3,2,1,0:T(8,128)(2,1)S(1)}, bf16[1,3,8,64,320]{4,3,2,1,0:T(8,128)(2,1)}, u32[]{:S(2)}) copy-start(bf16[1,3,8,64,320]{4,3,2,1,0:T(8,128)(2,1)} %param.6) | copy-start | bytes 2949124
  3.6 13.4 %collective-permute-start.4 = (bf16[3,3,64,320]{3,2,1,0:T(8,128)(2,1)S(1)}, bf16[3,3,64,320]{3,2,1,0:T(8,128)(2,1)S(1)}, u32[]{:S(2)}, u32[]{:S(2)}) collective-permute-start(bf16[3,3,64,320]{3,2,1,0:T(8,128)(2,1)S(1)} %get-tuple-element.37), channel_id=1, source_target_pairs={{0,1},{1,0},{2,3},{3,2},{4,5},{5,4},{6,7},{7,6},{8,9},{9,8},{10,11... | collective-permute-start | bytes 1105928 | tf_op jit(solution)/shard_map/ppermute | solution.py:499
  6.6 10.9 %collective-permute-start.1 = (bf16[480,256]{1,0:T(8,128)(2,1)S(1)}, bf16[480,256]{1,0:T(8,128)(2,1)S(1)}, u32[]{:S(2)}, u32[]{:S(2)}) collective-permute-start(bf16[480,256]{1,0:T(8,128)(2,1)S(1)} %get-tuple-element.33), channel_id=1, source_target_pairs={{4,0},{12,2},{0,4},{8,6},{6,8},{14,10},{2,12},{10,14},{5,1},{13,3}... | collective-permute-start | bytes 737288 | tf_op jit(solution)/shard_map/ppermute | solution.py:276
  8.2 9.4 %collective-permute-start = (bf16[480,256]{1,0:T(8,128)(2,1)S(1)}, bf16[480,256]{1,0:T(8,128)(2,1)S(1)}, u32[]{:S(2)}, u32[]{:S(2)}) collective-permute-start(bf16[480,256]{1,0:T(8,128)(2,1)S(1)} %get-tuple-element.33), channel_id=1, source_target_pairs={{8,2},{12,6},{2,8},{6,12},{9,3},{13,7},{3,9},{7,13},{24,18},{28,22... | collective-permute-start | bytes 737288 | tf_op jit(solution)/shard_map/ppermute | solution.py:276
  17.0 3.4 %collective-permute-start.5 = (bf16[3,3,64,320]{3,2,1,0:T(8,128)(2,1)S(1)}, bf16[3,3,64,320]{3,2,1,0:T(8,128)(2,1)S(1)}, u32[]{:S(2)}, u32[]{:S(2)}) collective-permute-start(bf16[3,3,64,320]{3,2,1,0:T(8,128)(2,1)S(1)} %collective-permute-done.4.halo_ref), channel_id=1, source_target_pairs={{0,2},{2,0},{1,3},{3,1},{4,6},{6,4},{5,7},{7,5},{8,10},{10,8},{9,1... | collective-permute-start | bytes 1105928 | tf_op jit(solution)/shard_map/ppermute | solution.py:494
  17.6 6.3 %collective-permute-start.7 = (bf16[480,256]{1,0:T(8,128)(2,1)S(1)}, bf16[480,256]{1,0:T(8,128)(2,1)S(1)}, u32[]{:S(2)}, u32[]{:S(2)}) collective-permute-start(bf16[480,256]{1,0:T(8,128)(2,1)S(1)} %pad_maximum_fusion), channel_id=1, source_target_pairs={{0,16},{16,0},{1,17},{17,1},{2,18},{18,2},{3,19},{19,3},{4,20},{20... | collective-permute-start | bytes 737288 | tf_op jit(solution)/shard_map/ppermute | solution.py:281
  19.1 6.2 %collective-permute-start.6 = (bf16[480,256]{1,0:T(8,128)(2,1)S(1)}, bf16[480,256]{1,0:T(8,128)(2,1)S(1)}, u32[]{:S(2)}, u32[]{:S(2)}) collective-permute-start(bf16[480,256]{1,0:T(8,128)(2,1)S(1)} %pad_maximum_fusion), channel_id=1, source_target_pairs={{0,1},{1,0},{2,3},{3,2},{4,5},{5,4},{6,7},{7,6},{8,9},{9,8},{10,11... | collective-permute-start | bytes 737288 | tf_op jit(solution)/shard_map/ppermute | solution.py:280
  23.4 4.6 %copy-start.2 = (f32[320]{0:T(512)S(1)}, f32[320]{0:T(512)}, u32[]{:S(2)}) copy-start(f32[320]{0:T(512)} %refs_2_.1) | copy-start | bytes 3844
  23.4 4.6 %copy-start.3 = (f32[320]{0:T(512)S(1)}, f32[320]{0:T(512)}, u32[]{:S(2)}) copy-start(f32[320]{0:T(512)} %refs_3_.1) | copy-start | bytes 3844
  25.5 11.6 %collective-permute-start.8 = (bf16[512,1024]{1,0:T(8,128)(2,1)S(1)}, bf16[512,1024]{1,0:T(8,128)(2,1)S(1)}, u32[]{:S(2)}, u32[]{:S(2)}) collective-permute-start(bf16[512,1024]{1,0:T(8,128)(2,1)S(1)} %join.1.w_ref), channel_id=1, source_target_pairs={{0,2},{2,0},{1,3},{3,1},{4,6},{6,4},{5,7},{7,5},{8,10},{10,8},{9,1... | collective-permute-start | bytes 3145736 | tf_op jit(solution)/shard_map/ppermute | solution.py:494
  33.3 3.8 %collective-permute-start.9 = (bf16[3,10,64,160]{3,2,1,0:T(8,128)(2,1)S(1)}, bf16[3,10,64,160]{3,2,1,0:T(8,128)(2,1)S(1)}, u32[]{:S(2)}, u32[]{:S(2)}) collective-permute-start(bf16[3,10,64,160]{3,2,1,0:T(8,128)(2,1)S(1)} %get-tuple-element.56), channel_id=1, source_target_pairs={{0,2},{2,0},{1,3},{3,1},{4,6},{6,4},{5,7},{7,5},{8,10},{10,8},{9,1... | collective-permute-start | bytes 1843208 | tf_op jit(solution)/shard_map/ppermute | solution.py:494
  33.4 3.6 %collective-permute-start.10 = (bf16[3,8,64,160]{3,2,1,0:T(8,128)(2,1)S(1)}, bf16[3,8,64,160]{3,2,1,0:T(8,128)(2,1)S(1)}, u32[]{:S(2)}, u32[]{:S(2)}) collective-permute-start(bf16[3,8,64,160]{3,2,1,0:T(8,128)(2,1)S(1)} %get-tuple-element.59), channel_id=1, source_target_pairs={{0,2},{2,0},{1,3},{3,1},{4,6},{6,4},{5,7},{7,5},{8,10},{10,8},{9,1... | collective-permute-start | bytes 1474568 | tf_op jit(solution)/shard_map/ppermute | solution.py:494

commit v7 on v6

--- a/solution.py
+++ b/solution.py
@@ -74,13 +74,15 @@
     spread = lax.broadcasted_iota(jnp.int32, (blocks, ins), 1) // MX_BLOCK
     spread = (spread == lax.broadcasted_iota(jnp.int32, (blocks, ins), 0)).astype(F32).astype(BF16)
     scales.wait()
+    every = []
+    for n in range(TAPS * TAPS):
+        scale = 1.0 / lax.shift_left(jnp.int32(1), -exps_ref[n // TAPS, :, n % TAPS, :]).astype(F32)
+        every.append(dot(scale.astype(BF16), spread, ((0,), (0,))))
     for dy in range(TAPS):
         codes[dy].wait()
         parts = []
         for dx in range(TAPS):
-            scale = 1.0 / lax.shift_left(jnp.int32(1), -exps_ref[dy, :, dx, :]).astype(F32)
-            scale = dot(scale.astype(BF16), spread, ((0,), (0,)))
-            parts.append(codes_ref[dy, dx].astype(F32) * scale)
+            parts.append(codes_ref[dy, dx].astype(F32) * every[dy * TAPS + dx])
         parts.append(jnp.zeros((outs, QUARTERS * width - TAPS * ins), F32))
         tap = jnp.concatenate(parts, axis=1).astype(BF16)
         for q in range(QUARTERS):
@@ -299,7 +301,7 @@
     lanes = x_ref.shape[2]
     steps = times // 2
     main, tail, _ = split_half(half)
-    chunk = 16
+    chunk = cols * tail // main
 
     def half_row(ref):
         x = ref[...].reshape(1, 2 * half)
@@ -352,14 +354,18 @@
                         fired = 0.5 + 0.5 * tanhs[t]
                         res[t] = (fired + spike(at_of[t], here).astype(F32)).astype(BF16)
                 mine = core == 0
+                if lo == 0:
+                    put = slice(w0, w0 + chunk), slice(None)
+                else:
+                    put = slice(cols, cols + chunk), slice(w0 // chunk * tail, (w0 // chunk + 1) * tail)
                 for tl in range(steps):
                     a, b = grads[tl], grads[steps + tl]
-                    gk_ref[tl, g, w0 : w0 + chunk, lo : lo + width] = jnp.where(mine, a, b)
-                    gs_ref[tl, g, w0 : w0 + chunk, lo : lo + width] = jnp.where(mine, b, a)
+                    gk_ref[tl, g, put[0], put[1]] = jnp.where(mine, a, b)
+                    gs_ref[tl, g, put[0], put[1]] = jnp.where(mine, b, a)
                     if h is not None:
                         a, b = res[tl], res[steps + tl]
-                        rk_ref[tl, h, w0 : w0 + chunk, lo : lo + width] = jnp.where(mine, a, b)
-                        rs_ref[tl, h, w0 : w0 + chunk, lo : lo + width] = jnp.where(mine, b, a)
+                        rk_ref[tl, h, put[0], put[1]] = jnp.where(mine, a, b)
+                        rs_ref[tl, h, put[0], put[1]] = jnp.where(mine, b, a)
 
     def scan_own(h, strip):
         scan(
@@ -380,7 +386,7 @@
         p_ref[edge_strip] = jnp.zeros(p_ref.shape[1:], F32)
         for ref in (gk_ref, gs_ref):
             for tl in range(steps):
-                ref[tl, edge] = jnp.zeros((cols, half), BF16)
+                ref[tl, edge] = jnp.zeros(ref.shape[2:], BF16)
 
         def scan_at(j):
             if j == rows:
@@ -423,8 +429,9 @@
     rows, times, cols, half = s.shape
     steps = times // 2
     args = [weights, x, s, c] + [a for pair in halo_taps for a in pair] + [bias, thr, *begun]
-    grad = shape((steps, rows + 2, cols, half))
-    res = shape((steps, rows, cols, half))
+    main, tail, _ = split_half(half)
+    grad = shape((steps, rows + 2, cols + cols * tail // main, main))
+    res = shape((steps, rows, cols + cols * tail // main, main))
     return call(
         functools.partial(forward_kernel, two, bool(begun)),
         (grad, grad, res, res),
@@ -436,57 +443,75 @@
     )(*args)
 
 
-def rows_of_grads(g_ref, t, h0, count):
-    cols, half = g_ref.shape[2:]
-    main, tail, padded = split_half(half)
-    taps = [g_ref[t, pl.ds(h0 + 2 - dy, count)].reshape(count * cols, half) for dy in range(TAPS)]
-    rest = jnp.zeros((count * cols, padded - TAPS * half), BF16)
-    return jnp.concatenate([x[:, :main] for x in taps] + [x[:, main:] for x in taps] + [rest], axis=1)
+def unpack(x, cols):
+    main = x.shape[2]
+    chunk = x.shape[1] - cols
+    tail = main * chunk // cols
+    parts = [x[:, cols:, k * tail : (k + 1) * tail] for k in range(cols // chunk)]
+    return x[:, :cols], jnp.concatenate(parts, axis=1)
+
+
+def rows_of_grads(g_ref, t, h0, count, cols, padded):
+    taps = [unpack(g_ref[t, pl.ds(h0 + 2 - dy, count)], cols) for dy in range(TAPS)]
+    mains, tails = ([x[k].reshape(count * cols, -1) for x in taps] for k in range(2))
+    rest = jnp.zeros((count * cols, padded - sum(x.shape[1] for x in mains + tails)), BF16)
+    return jnp.concatenate(mains + tails + [rest], axis=1)
 
 
 def backward_own_kernel(w_ref, g_ref, y_ref):
     steps, rows2 = g_ref.shape[:2]
     rows = rows2 - 2
     for t in range(steps):
-        grads = rows_of_grads(g_ref, t, 0, rows)
+        grads = rows_of_grads(g_ref, t, 0, rows, y_ref.shape[1] // rows, w_ref.shape[0])
         y_ref[t] = dot(grads, w_ref[...], ((1,), (0,)))
 
 
-def backward_own(weights, grads):
-    steps, rows2, cols, _ = grads.shape
+def backward_own(weights, grads, cols):
+    steps, rows2 = grads.shape[:2]
     out = shape((steps, (rows2 - 2) * cols, weights.shape[1]), F32)
     return call(backward_own_kernel, out, [VMEM_SPEC] * 2, 12, "backward_own", cost=6 << 20)(weights, grads)
 
 
-def backward_kernel(w_ref, g_ref, y_ref, cot_ref, rk_ref, rs_ref, out_ref, res_ref):
-    t = pl.program_id(0)
-    _, rows, cols, ch = cot_ref.shape
+def backward_kernel(w_ref, g_ref, y_ref, cot_ref, rk_ref, rs_ref, out_hbm, res_hbm, out_ref, res_ref, sems):
+    steps, rows, cols, ch = cot_ref.shape
     core = lax.axis_index("tm")
     edge = lax.broadcasted_iota(jnp.int32, (1, cols, 1), 1)
     block = 4
-    for h0 in range(0, rows, block):
-        total = dot(rows_of_grads(g_ref, t, h0, block), w_ref[...], ((1,), (0,)))
-        total = (total + y_ref[t, h0 * cols : (h0 + block) * cols, :]).reshape(block, cols, -1)
-        left, mid, right = (total[:, :, k * ch : (k + 1) * ch] for k in range(TAPS))
-        left = jnp.where(edge == cols - 1, 0.0, pltpu.roll(left, cols - 1, 1))
-        right = jnp.where(edge == 0, 0.0, pltpu.roll(right, 1, 1))
-        out_ref[0, h0 : h0 + block] = cot_ref[t, h0 : h0 + block].astype(F32) + (left + mid + right)
-        a = rk_ref[t, h0 : h0 + block].astype(F32)
-        b = rs_ref[t, h0 : h0 + block].astype(F32)
-        both = jnp.concatenate([jnp.where(core == 0, a, b), jnp.where(core == 0, b, a)], axis=2)
-        res_ref[0, h0 : h0 + block] = both.astype(BF16)
+    copies = []
+    for t in range(steps):
+        for h0 in range(0, rows, block):
+            total = dot(rows_of_grads(g_ref, t, h0, block, cols, w_ref.shape[0]), w_ref[...], ((1,), (0,)))
+            total = (total + y_ref[t, h0 * cols : (h0 + block) * cols, :]).reshape(block, cols, -1)
+            left, mid, right = (total[:, :, k * ch : (k + 1) * ch] for k in range(TAPS))
+            left = jnp.where(edge == cols - 1, 0.0, pltpu.roll(left, cols - 1, 1))
+            right = jnp.where(edge == 0, 0.0, pltpu.roll(right, 1, 1))
+            here = t, slice(h0, h0 + block)
+            out_ref[here] = cot_ref[here].astype(F32) + (left + mid + right)
+            a, b = (jnp.concatenate(unpack(ref[here].astype(F32), cols), axis=2) for ref in (rk_ref, rs_ref))
+            both = jnp.concatenate([jnp.where(core == 0, a, b), jnp.where(core == 0, b, a)], axis=2)
+            res_ref[here] = both.astype(BF16)
+            for n, (ref, hbm) in enumerate(((out_ref, out_hbm), (res_ref, res_hbm))):
+                window = t, pl.ds(h0, block)
+                copies.append(pltpu.make_async_copy(ref.at[window], hbm.at[window], sems.at[len(copies)]))
+                copies[-1].start()
+    for copy in copies:
+        copy.wait()
 
 
 def backward(weights, grads, y, cot, res_keep, res_arrived):
-    block = pl.BlockSpec((1,) + cot.shape[1:], lambda t: (t, 0, 0, 0))
+    steps, rows = cot.shape[:2]
     return call(
         backward_kernel,
         (shape(cot.shape, F32), shape(cot.shape)),
         [VMEM_SPEC] * 6,
-        16,
+        24,
         "backward",
-        grid=(cot.shape[0],),
-        out_specs=(block, block),
+        [
+            pltpu.VMEM(cot.shape, F32),
+            pltpu.VMEM(cot.shape, BF16),
+            pltpu.SemaphoreType.DMA((2 * steps * (rows // 4),)),
+        ],
+        out_specs=(pl.BlockSpec(memory_space=pltpu.HBM),) * 2,
     )(weights, grads, y, cot, res_keep, res_arrived)
 
 
@@ -522,7 +547,7 @@
     keep, send, res_keep, res_send = forward(two, weights, taps, halo_taps, current_bias, threshold, begun)
     arrived = swap_cores(send)
     res_arrived = swap_cores(res_send)
-    y = backward_own(weights, keep)
+    y = backward_own(weights, keep, cot.shape[2])
     input_grad, residual = backward(weights2, arrived, y, cot, res_keep, res_arrived)
     return residual[None], input_grad[None]
 

time: 41.2 us -> 40.2 us (0.976)
  waiting for transfers between devices: 6.3 us -> 5.25 us
    ppermute x6, waiting for transfers between devices: 1.38 us -> 0.33 us  [swap_cores(): return lax.ppermute(x, 'tm', [(0, 1), (1, 0)])]
    pallas_call x1, Pallas kernels: 2.35 us -> 1.76 us  [prepare(): call(functools.partial(prepare_kernel, two), out, [HBM_SPEC] * 4, 16, 'pr...]
where the time goes in v7:
time: 40.2 us; the launch traced here: 40 us
  Pallas kernels  21.6 us (54%)
  starting transfers between devices  12.2 us (30%)
  waiting for transfers between devices  5.25 us (13%)
  between operations  0.92 us (2%)
    pallas_call x1, Pallas kernels, forward(): call(functools.partial(forward_kernel, two, bool(begun)), (grad, grad, re...  5.48 us
    pallas_call x1, Pallas kernels, build_taps(): call(taps_kernel, out, [VMEM_SPEC] * 4, 16, 'taps', cost=18 << 20)  5.17 us
    ppermute x6, starting transfers between devices, swap_cores(): return lax.ppermute(x, 'tm', [(0, 1), (1, 0)])  4.2 us
    pallas_call x1, Pallas kernels, backward(): call(backward_kernel, (shape(cot.shape, F32), shape(cot.shape)), [VMEM_SP...  4.01 us
    ppermute x1, starting transfers between devices, fetch_halos(): return [lax.ppermute(halos[0], 'rows', [(0, 1), (1, 0)])]  2.99 us
    ppermute x1, waiting for transfers between devices, fetch_halos(): return [lax.ppermute(halos[0], 'rows', [(0, 1), (1, 0)])]  2.94 us
    pallas_call x1, Pallas kernels, partial_currents(): call(partial_kernel, out, [VMEM_SPEC] * 5, 12, 'partial', scratch)  2.3 us
    ppermute x2, starting transfers between devices, fetch_weights(): rounds = [lax.ppermute(send, ('dp', 'tm'), moved[k]) for k in range(h)]  2.24 us
  transfers between devices with their start and end apart: 11, of which 4 were waited for; matrix products, arithmetic and copies ran while one was open for 0% of the time, Pallas kernels for 43%

profile of v7, /device:TPU:0, one launch (start us, length us, event | category | flops | bytes accessed | tf_op | source)
XLA Modules:
  0.0 40.0 jit_solution(7144792054523128585)
XLA Ops:
  0.6 0.5 %collective-permute-start.2 = (bf16[3,8,64,320]{3,2,1,0:T(8,128)(2,1)}, bf16[3,8,64,320]{3,2,1,0:T(8,128)(2,1)S(1)}, u32[]{:S(2)}, u32[]{:S(2)}) collective-permute-start(bf16[3,8,64,320]{3,2,1,0:T(8,128)(2,1)} %bitcast.10), channel_id=1, source_target_pairs={{0,2},{2,0},{1,3},{3,1},{4,6},{6,4},{5,7},{7,5},{8,10},{10,8},{9,1... | collective-permute-start | bytes 2949128 | tf_op jit(solution)/shard_map/ppermute | solution.py:519
  1.1 0.1 collective-permute-start.3
  1.2 1.8 %prepare.1 = (bf16[4,240,256]{2,1,0:T(8,128)(2,1)S(1)}, bf16[480,256]{1,0:T(8,128)(2,1)S(1)}, bf16[3,3,64,320]{3,2,1,0:T(8,128)(2,1)S(1)}) custom-call(s32[3,3,80,320]{3,2,1,0:T(8,128)} %bitcast.13, s32[3,10,3,80]{3,2,1,0:T(4,128)} %bitcast.14, bf16[3,8,64,320]{3,2,1,0:T(8,128)(2,1)} %bitcast.11, bf16[3,8,64,320]{3,2,1,0:T(8,128)(2,1)} %bitcast.7), custom_call_target="tpu_custom_call" | custom-call | bytes 2097152 | tf_op jit(solution)/shard_map/prepare/pallas_call | solution.py:103
  3.0 3.0 %collective-permute-start.4 = (bf16[3,3,64,320]{3,2,1,0:T(8,128)(2,1)S(1)}, bf16[3,3,64,320]{3,2,1,0:T(8,128)(2,1)S(1)}, u32[]{:S(2)}, u32[]{:S(2)}) collective-permute-start(bf16[3,3,64,320]{3,2,1,0:T(8,128)(2,1)S(1)} %get-tuple-element.37), channel_id=1, source_target_pairs={{0,1},{1,0},{2,3},{3,2},{4,5},{5,4},{6,7},{7,6},{8,9},{9,8},{10,11... | collective-permute-start | bytes 1105928 | tf_op jit(solution)/shard_map/ppermute | solution.py:524
  6.0 1.6 %collective-permute-start.1 = (bf16[480,256]{1,0:T(8,128)(2,1)S(1)}, bf16[480,256]{1,0:T(8,128)(2,1)S(1)}, u32[]{:S(2)}, u32[]{:S(2)}) collective-permute-start(bf16[480,256]{1,0:T(8,128)(2,1)S(1)} %get-tuple-element.33), channel_id=1, source_target_pairs={{4,0},{12,2},{0,4},{8,6},{6,8},{14,10},{2,12},{10,14},{5,1},{13,3}... | collective-permute-start | bytes 737288 | tf_op jit(solution)/shard_map/ppermute | solution.py:278
  7.6 0.7 %collective-permute-start = (bf16[480,256]{1,0:T(8,128)(2,1)S(1)}, bf16[480,256]{1,0:T(8,128)(2,1)S(1)}, u32[]{:S(2)}, u32[]{:S(2)}) collective-permute-start(bf16[480,256]{1,0:T(8,128)(2,1)S(1)} %get-tuple-element.33), channel_id=1, source_target_pairs={{8,2},{12,6},{2,8},{6,12},{9,3},{13,7},{3,9},{7,13},{24,18},{28,22... | collective-permute-start | bytes 737288 | tf_op jit(solution)/shard_map/ppermute | solution.py:278
  8.3 5.2 %taps.1 = (bf16[8,384,1024]{2,1,0:T(8,128)(2,1)S(1)}, bf16[8,6,64,160]{3,2,1,0:T(8,128)(2,1)S(1)}, bf16[8,6,64,160]{3,2,1,0:T(8,128)(2,1)S(1)}) custom-call(bf16[3,8,64,320]{3,2,1,0:T(8,128)(2,1)S(1)} %bitcast.12, bf16[3,8,64,320]{3,2,1,0:T(8,128)(2,1)S(1)} %collective-permute-done.2.spikes2_ref, bf16[3,8,64,320]{3,2,1,0:T(8,128)(2,1)S(1)} %bitcast.8, ...), custom_call_target="tpu_custom_call" | custom-call | bytes 18874368 | tf_op jit(solution)/shard_map/taps/pallas_call | solution.py:153
  13.5 2.9 %collective-permute-done.4.halo_ref = bf16[3,3,64,320]{3,2,1,0:T(8,128)(2,1)S(1)} collective-permute-done((bf16[3,3,64,320]{3,2,1,0:T(8,128)(2,1)S(1)}, bf16[3,3,64,320]{3,2,1,0:T(8,128)(2,1)S(1)}, u32[]{:S(2)}, u32[]{:S(2)}) %collective-permute-start.4) | collective-permute-done | bytes 368672 | tf_op jit(solution)/shard_map/ppermute | solution.py:524
  16.4 0.5 %collective-permute-start.5 = (bf16[3,3,64,320]{3,2,1,0:T(8,128)(2,1)S(1)}, bf16[3,3,64,320]{3,2,1,0:T(8,128)(2,1)S(1)}, u32[]{:S(2)}, u32[]{:S(2)}) collective-permute-start(bf16[3,3,64,320]{3,2,1,0:T(8,128)(2,1)S(1)} %collective-permute-done.4.halo_ref), channel_id=1, source_target_pairs={{0,2},{2,0},{1,3},{3,1},{4,6},{6,4},{5,7},{7,5},{8,10},{10,8},{9,1... | collective-permute-start | bytes 1105928 | tf_op jit(solution)/shard_map/ppermute | solution.py:519
  17.0 1.6 %collective-permute-start.7 = (bf16[480,256]{1,0:T(8,128)(2,1)S(1)}, bf16[480,256]{1,0:T(8,128)(2,1)S(1)}, u32[]{:S(2)}, u32[]{:S(2)}) collective-permute-start(bf16[480,256]{1,0:T(8,128)(2,1)S(1)} %pad_maximum_fusion), channel_id=1, source_target_pairs={{0,16},{16,0},{1,17},{17,1},{2,18},{18,2},{3,19},{19,3},{4,20},{20... | collective-permute-start | bytes 737288 | tf_op jit(solution)/shard_map/ppermute | solution.py:283
  18.6 1.2 %collective-permute-start.6 = (bf16[480,256]{1,0:T(8,128)(2,1)S(1)}, bf16[480,256]{1,0:T(8,128)(2,1)S(1)}, u32[]{:S(2)}, u32[]{:S(2)}) collective-permute-start(bf16[480,256]{1,0:T(8,128)(2,1)S(1)} %pad_maximum_fusion), channel_id=1, source_target_pairs={{0,1},{1,0},{2,3},{3,2},{4,5},{5,4},{6,7},{7,6},{8,9},{9,8},{10,11... | collective-permute-start | bytes 737288 | tf_op jit(solution)/shard_map/ppermute | solution.py:282
  19.8 0.7 %halo_taps.1 = (bf16[2,384,1024]{2,1,0:T(8,128)(2,1)S(1)}, bf16[6,64,160]{2,1,0:T(8,128)(2,1)S(1)}) custom-call(bf16[3,3,64,320]{3,2,1,0:T(8,128)(2,1)S(1)} %collective-permute-done.4.halo_ref, bf16[3,3,64,320]{3,2,1,0:T(8,128)(2,1)S(1)} %collective-permute-done.5.halo2_ref), custom_call_target="tpu_custom_call" | custom-call | bytes 2097152 | tf_op jit(solution)/shard_map/halo_taps/pallas_call | solution.py:172
  20.5 2.3 %partial.1.refs_4_ = f32[11,384,512]{2,1,0:T(8,128)S(1)} custom-call(bf16[4,240,256]{2,1,0:T(8,128)(2,1)S(1)} %get-tuple-element.49.w_ref, bf16[480,256]{1,0:T(8,128)(2,1)S(1)} %collective-permute-done.first_ref, bf16[480,256]{1,0:T(8,128)(2,1)S(1)} %collective-permute-done.1.second_ref, bf16[8,384,1024]{2,1,0:T(8,128)(2,1)S(1)} %get-tuple-element.50.x_ref, ...), custom_call_target="tpu_custom_call" | custom-call | tf_op jit(solution)/shard_map/partial/pallas_call | solution.py:257
  22.8 0.0 copy-start.2
  22.8 0.5 %collective-permute-done.7.y_ref = bf16[480,256]{1,0:T(8,128)(2,1)S(1)} collective-permute-done((bf16[480,256]{1,0:T(8,128)(2,1)S(1)}, bf16[480,256]{1,0:T(8,128)(2,1)S(1)}, u32[]{:S(2)}, u32[]{:S(2)}) %collective-permute-start.7) | collective-permute-done | bytes 245792 | tf_op jit(solution)/shard_map/ppermute | solution.py:283
  23.2 1.5 %collective-permute-done.6.x_ref = bf16[480,256]{1,0:T(8,128)(2,1)S(1)} collective-permute-done((bf16[480,256]{1,0:T(8,128)(2,1)S(1)}, bf16[480,256]{1,0:T(8,128)(2,1)S(1)}, u32[]{:S(2)}, u32[]{:S(2)}) %collective-permute-start.6) | collective-permute-done | bytes 245792 | tf_op jit(solution)/shard_map/ppermute | solution.py:282
  24.8 0.3 join.1.w_ref
  25.1 2.5 %collective-permute-start.8 = (bf16[512,1024]{1,0:T(8,128)(2,1)S(1)}, bf16[512,1024]{1,0:T(8,128)(2,1)S(1)}, u32[]{:S(2)}, u32[]{:S(2)}) collective-permute-start(bf16[512,1024]{1,0:T(8,128)(2,1)S(1)} %join.1.w_ref), channel_id=1, source_target_pairs={{0,2},{2,0},{1,3},{3,1},{4,6},{6,4},{5,7},{7,5},{8,10},{10,8},{9,1... | collective-permute-start | bytes 3145736 | tf_op jit(solution)/shard_map/ppermute | solution.py:519
  27.6 5.5 %forward.1 = (bf16[3,10,80,128]{3,2,1,0:T(8,128)(2,1)S(1)}, bf16[3,10,80,128]{3,2,1,0:T(8,128)(2,1)S(1)}, bf16[3,8,80,128]{3,2,1,0:T(8,128)(2,1)S(1)}, bf16[3,8,80,128]{3,2,1,0:T(8,128)(2,1)S(1)}) custom-call(bf16[512,1024]{1,0:T(8,128)(2,1)S(1)} %join.1.w_ref, bf16[8,384,1024]{2,1,0:T(8,128)(2,1)S(1)} %get-tuple-element.50.x_ref, ...), custom_call_target="tpu_custom_call" | custom-call | bytes 25165824 | tf_op jit(solution)/shard_map/forward/pallas_call | solution.py:435
  33.1 0.1 collective-permute-start.9
  33.2 0.5 %collective-permute-start.10 = (bf16[3,8,80,128]{3,2,1,0:T(8,128)(2,1)S(1)}, bf16[3,8,80,128]{3,2,1,0:T(8,128)(2,1)S(1)}, u32[]{:S(2)}, u32[]{:S(2)}) collective-permute-start(bf16[3,8,80,128]{3,2,1,0:T(8,128)(2,1)S(1)} %get-tuple-element.59), channel_id=1, source_target_pairs={{0,2},{2,0},{1,3},{3,1},{4,6},{6,4},{5,7},{7,5},{8,10},{10,8},{9,1... | collective-permute-start | bytes 1474568 | tf_op jit(solution)/shard_map/ppermute | solution.py:519
  33.6 1.9 %backward_own.1.y_ref = f32[3,512,1024]{2,1,0:T(8,128)S(1)} custom-call(bf16[512,1024]{1,0:T(8,128)(2,1)S(1)} %join.1.w_ref, bf16[3,10,80,128]{3,2,1,0:T(8,128)(2,1)S(1)} %get-tuple-element.57.g_ref), custom_call_target="tpu_custom_call" | custom-call | bytes 6291456 | tf_op jit(solution)/shard_map/backward_own/pallas_call | solution.py:472
  35.5 0.3 collective-permute-done.10.rs_ref
  35.9 4.0 %backward.1 = (f32[3,8,64,320]{3,2,1,0:T(8,128)}, bf16[3,8,64,320]{3,2,1,0:T(8,128)(2,1)}) custom-call(bf16[512,1024]{1,0:T(8,128)(2,1)S(1)} %collective-permute-done.8.w_ref, bf16[3,10,80,128]{3,2,1,0:T(8,128)(2,1)S(1)} %collective-permute-done.9.g_ref, f32[3,512,1024]{2,1,0:T(8,128)S(1)} %backward_own.1.y_ref, bf16[3,8,64,320]{3,2,1,0:T(8,128)(2,1)S(1)} %bitcast.9, ...), custom_call_target="tpu_custom_call" | custom-call | tf_op jit(solution)/shard_map/backward/pallas_call | solution.py:503
  (17 shorter events, 0.1 us)
Async XLA Ops:
  0.6 7.6 %collective-permute-start.2 = (bf16[3,8,64,320]{3,2,1,0:T(8,128)(2,1)}, bf16[3,8,64,320]{3,2,1,0:T(8,128)(2,1)S(1)}, u32[]{:S(2)}, u32[]{:S(2)}) collective-permute-start(bf16[3,8,64,320]{3,2,1,0:T(8,128)(2,1)} %bitcast.10), channel_id=1, source_target_pairs={{0,2},{2,0},{1,3},{3,1},{4,6},{6,4},{5,7},{7,5},{8,10},{10,8},{9,1... | collective-permute-start | bytes 2949128 | tf_op jit(solution)/shard_map/ppermute | solution.py:519
  1.1 7.1 %collective-permute-start.3 = (bf16[3,8,64,320]{3,2,1,0:T(8,128)(2,1)}, bf16[3,8,64,320]{3,2,1,0:T(8,128)(2,1)S(1)}, u32[]{:S(2)}, u32[]{:S(2)}) collective-permute-start(bf16[3,8,64,320]{3,2,1,0:T(8,128)(2,1)} %bitcast.6), channel_id=1, source_target_pairs={{0,2},{2,0},{1,3},{3,1},{4,6},{6,4},{5,7},{7,5},{8,10},{10,8},{9,1... | collective-permute-start | bytes 2949128 | tf_op jit(solution)/shard_map/ppermute | solution.py:519
  1.2 7.0 %copy-start = (bf16[1,3,8,64,320]{4,3,2,1,0:T(8,128)(2,1)S(1)}, bf16[1,3,8,64,320]{4,3,2,1,0:T(8,128)(2,1)}, u32[]{:S(2)}) copy-start(bf16[1,3,8,64,320]{4,3,2,1,0:T(8,128)(2,1)} %param.7) | copy-start | bytes 2949124
  1.2 7.0 %copy-start.1 = (bf16[1,3,8,64,320]{4,3,2,1,0:T(8,128)(2,1)S(1)}, bf16[1,3,8,64,320]{4,3,2,1,0:T(8,128)(2,1)}, u32[]{:S(2)}) copy-start(bf16[1,3,8,64,320]{4,3,2,1,0:T(8,128)(2,1)} %param.6) | copy-start | bytes 2949124
  3.0 13.4 %collective-permute-start.4 = (bf16[3,3,64,320]{3,2,1,0:T(8,128)(2,1)S(1)}, bf16[3,3,64,320]{3,2,1,0:T(8,128)(2,1)S(1)}, u32[]{:S(2)}, u32[]{:S(2)}) collective-permute-start(bf16[3,3,64,320]{3,2,1,0:T(8,128)(2,1)S(1)} %get-tuple-element.37), channel_id=1, source_target_pairs={{0,1},{1,0},{2,3},{3,2},{4,5},{5,4},{6,7},{7,6},{8,9},{9,8},{10,11... | collective-permute-start | bytes 1105928 | tf_op jit(solution)/shard_map/ppermute | solution.py:524
  6.0 10.9 %collective-permute-start.1 = (bf16[480,256]{1,0:T(8,128)(2,1)S(1)}, bf16[480,256]{1,0:T(8,128)(2,1)S(1)}, u32[]{:S(2)}, u32[]{:S(2)}) collective-permute-start(bf16[480,256]{1,0:T(8,128)(2,1)S(1)} %get-tuple-element.33), channel_id=1, source_target_pairs={{4,0},{12,2},{0,4},{8,6},{6,8},{14,10},{2,12},{10,14},{5,1},{13,3}... | collective-permute-start | bytes 737288 | tf_op jit(solution)/shard_map/ppermute | solution.py:278
  7.6 9.4 %collective-permute-start = (bf16[480,256]{1,0:T(8,128)(2,1)S(1)}, bf16[480,256]{1,0:T(8,128)(2,1)S(1)}, u32[]{:S(2)}, u32[]{:S(2)}) collective-permute-start(bf16[480,256]{1,0:T(8,128)(2,1)S(1)} %get-tuple-element.33), channel_id=1, source_target_pairs={{8,2},{12,6},{2,8},{6,12},{9,3},{13,7},{3,9},{7,13},{24,18},{28,22... | collective-permute-start | bytes 737288 | tf_op jit(solution)/shard_map/ppermute | solution.py:278
  16.4 3.4 %collective-permute-start.5 = (bf16[3,3,64,320]{3,2,1,0:T(8,128)(2,1)S(1)}, bf16[3,3,64,320]{3,2,1,0:T(8,128)(2,1)S(1)}, u32[]{:S(2)}, u32[]{:S(2)}) collective-permute-start(bf16[3,3,64,320]{3,2,1,0:T(8,128)(2,1)S(1)} %collective-permute-done.4.halo_ref), channel_id=1, source_target_pairs={{0,2},{2,0},{1,3},{3,1},{4,6},{6,4},{5,7},{7,5},{8,10},{10,8},{9,1... | collective-permute-start | bytes 1105928 | tf_op jit(solution)/shard_map/ppermute | solution.py:519
  17.0 6.3 %collective-permute-start.7 = (bf16[480,256]{1,0:T(8,128)(2,1)S(1)}, bf16[480,256]{1,0:T(8,128)(2,1)S(1)}, u32[]{:S(2)}, u32[]{:S(2)}) collective-permute-start(bf16[480,256]{1,0:T(8,128)(2,1)S(1)} %pad_maximum_fusion), channel_id=1, source_target_pairs={{0,16},{16,0},{1,17},{17,1},{2,18},{18,2},{3,19},{19,3},{4,20},{20... | collective-permute-start | bytes 737288 | tf_op jit(solution)/shard_map/ppermute | solution.py:283
  18.6 6.2 %collective-permute-start.6 = (bf16[480,256]{1,0:T(8,128)(2,1)S(1)}, bf16[480,256]{1,0:T(8,128)(2,1)S(1)}, u32[]{:S(2)}, u32[]{:S(2)}) collective-permute-start(bf16[480,256]{1,0:T(8,128)(2,1)S(1)} %pad_maximum_fusion), channel_id=1, source_target_pairs={{0,1},{1,0},{2,3},{3,2},{4,5},{5,4},{6,7},{7,6},{8,9},{9,8},{10,11... | collective-permute-start | bytes 737288 | tf_op jit(solution)/shard_map/ppermute | solution.py:282
  22.8 4.8 %copy-start.2 = (f32[320]{0:T(512)S(1)}, f32[320]{0:T(512)}, u32[]{:S(2)}) copy-start(f32[320]{0:T(512)} %refs_2_.1) | copy-start | bytes 3844
  22.8 4.8 %copy-start.3 = (f32[320]{0:T(512)S(1)}, f32[320]{0:T(512)}, u32[]{:S(2)}) copy-start(f32[320]{0:T(512)} %refs_3_.1) | copy-start | bytes 3844
  25.1 10.8 %collective-permute-start.8 = (bf16[512,1024]{1,0:T(8,128)(2,1)S(1)}, bf16[512,1024]{1,0:T(8,128)(2,1)S(1)}, u32[]{:S(2)}, u32[]{:S(2)}) collective-permute-start(bf16[512,1024]{1,0:T(8,128)(2,1)S(1)} %join.1.w_ref), channel_id=1, source_target_pairs={{0,2},{2,0},{1,3},{3,1},{4,6},{6,4},{5,7},{7,5},{8,10},{10,8},{9,1... | collective-permute-start | bytes 3145736 | tf_op jit(solution)/shard_map/ppermute | solution.py:519
  33.1 2.8 %collective-permute-start.9 = (bf16[3,10,80,128]{3,2,1,0:T(8,128)(2,1)S(1)}, bf16[3,10,80,128]{3,2,1,0:T(8,128)(2,1)S(1)}, u32[]{:S(2)}, u32[]{:S(2)}) collective-permute-start(bf16[3,10,80,128]{3,2,1,0:T(8,128)(2,1)S(1)} %get-tuple-element.56), channel_id=1, source_target_pairs={{0,2},{2,0},{1,3},{3,1},{4,6},{6,4},{5,7},{7,5},{8,10},{10,8},{9,1... | collective-permute-start | bytes 1843208 | tf_op jit(solution)/shard_map/ppermute | solution.py:519
  33.2 2.7 %collective-permute-start.10 = (bf16[3,8,80,128]{3,2,1,0:T(8,128)(2,1)S(1)}, bf16[3,8,80,128]{3,2,1,0:T(8,128)(2,1)S(1)}, u32[]{:S(2)}, u32[]{:S(2)}) collective-permute-start(bf16[3,8,80,128]{3,2,1,0:T(8,128)(2,1)S(1)} %get-tuple-element.59), channel_id=1, source_target_pairs={{0,2},{2,0},{1,3},{3,1},{4,6},{6,4},{5,7},{7,5},{8,10},{10,8},{9,1... | collective-permute-start | bytes 1474568 | tf_op jit(solution)/shard_map/ppermute | solution.py:519

commit v8 on v7

--- a/solution.py
+++ b/solution.py
@@ -297,7 +297,8 @@
         halos = [refs[:2], refs[2:4]]
     bias_ref, thr_ref, *begun, gk_ref, gs_ref, rk_ref, rs_ref, p_ref = refs[2 * len(halos) :]
     core, row = lax.axis_index("tm"), lax.axis_index("rows")
-    rows, times, cols, half = s_ref.shape
+    rows, times = s_ref.shape[:2]
+    cols, half = x_ref.shape[1] // times, bias_ref.shape[0] // 2
     lanes = x_ref.shape[2]
     steps = times // 2
     main, tail, _ = split_half(half)
@@ -325,59 +326,70 @@
             p_ref[pl.ds(strip, 2)] = p.reshape(2, times * cols, -1)
 
     def scan(strip, cot, spike, g, h, keep=None):
-        for w0 in range(0, cols, chunk):
-            for lo, width, first in ((0, main, 0), (main, tail, TAPS * main)):
-                th = thr[:, lo : lo + width]
-                half_th = 0.5 * th
-                sh = shift[:, lo : lo + width]
-                state = jnp.zeros((chunk, width), F32)
-                tanhs = []
-                for t in range(times):
-                    at = pl.ds(pl.multiple_of(at_of[t] * cols + w0, chunk), chunk)
-                    now = sh
-                    for dy in range(TAPS):
-                        now = now + p_ref[strip + dy, at, first + dy * width : first + (dy + 1) * width]
-                    y = state + now
-                    tanh = jnp.tanh(y)
-                    state = (y + half_th) - half_th * tanh
-                    tanhs.append(tanh)
-                adjoint = jnp.zeros((chunk, width), F32)
-                grads, res = [None] * times, [None] * times
-                for t in reversed(range(times)):
-                    here = slice(w0, w0 + chunk), slice(lo, lo + width)
-                    slope = 0.5 - 0.5 * (tanhs[t] * tanhs[t])
-                    up = cot(at_of[t], here).astype(F32)
-                    adjoint = adjoint + slope * (up - th * adjoint)
-                    out = adjoint if keep is None else adjoint * keep
-                    grads[t] = out.astype(BF16)
-                    if h is not None:
-                        fired = 0.5 + 0.5 * tanhs[t]
-                        res[t] = (fired + spike(at_of[t], here).astype(F32)).astype(BF16)
-                mine = core == 0
-                if lo == 0:
-                    put = slice(w0, w0 + chunk), slice(None)
-                else:
-                    put = slice(cols, cols + chunk), slice(w0 // chunk * tail, (w0 // chunk + 1) * tail)
-                for tl in range(steps):
-                    a, b = grads[tl], grads[steps + tl]
-                    gk_ref[tl, g, put[0], put[1]] = jnp.where(mine, a, b)
-                    gs_ref[tl, g, put[0], put[1]] = jnp.where(mine, b, a)
-                    if h is not None:
-                        a, b = res[tl], res[steps + tl]
-                        rk_ref[tl, h, put[0], put[1]] = jnp.where(mine, a, b)
-                        rs_ref[tl, h, put[0], put[1]] = jnp.where(mine, b, a)
+        def row_of(t, w0):
+            return pl.ds(pl.multiple_of(at_of[t] * cols + w0, chunk), chunk)
+
+        def below(t, dy, w0):
+            return p_ref[strip + dy, row_of(t, w0), dy * main : (dy + 1) * main]
+
+        def beyond(t, dy, _):
+            first = TAPS * main + dy * tail
+            parts = [p_ref[strip + dy, row_of(t, w0), first : first + tail] for w0 in range(0, cols, chunk)]
+            return jnp.concatenate(parts, axis=1)
+
+        def packed(read, at, w0):
+            if w0 < cols:
+                return read(at, slice(w0, w0 + chunk), slice(0, main))
+            parts = [read(at, slice(w, w + chunk), slice(main, half)) for w in range(0, cols, chunk)]
+            return jnp.concatenate(parts, axis=1)
+
+        jobs = [(w0, below, thr[:, :main], shift[:, :main]) for w0 in range(0, cols, chunk)]
+        spread = [jnp.concatenate([v[:, main:]] * (cols // chunk), axis=1) for v in (thr, shift)]
+        for w0, part, th, sh in jobs + [(cols, beyond, *spread)]:
+            here = slice(w0, w0 + chunk)
+            half_th = 0.5 * th
+            state = jnp.zeros((chunk, main), F32)
+            tanhs = []
+            for t in range(times):
+                now = sh
+                for dy in range(TAPS):
+                    now = now + part(t, dy, w0)
+                y = state + now
+                tanh = jnp.tanh(y)
+                state = (y + half_th) - half_th * tanh
+                tanhs.append(tanh)
+            adjoint = jnp.zeros((chunk, main), F32)
+            grads, res = [None] * times, [None] * times
+            for t in reversed(range(times)):
+                slope = 0.5 - 0.5 * (tanhs[t] * tanhs[t])
+                up = packed(cot, at_of[t], w0).astype(F32)
+                adjoint = adjoint + slope * (up - th * adjoint)
+                out = adjoint if keep is None else adjoint * keep
+                grads[t] = out.astype(BF16)
+                if h is not None:
+                    fired = 0.5 + 0.5 * tanhs[t]
+                    res[t] = (fired + packed(spike, at_of[t], w0).astype(F32)).astype(BF16)
+            mine = core == 0
+            for tl in range(steps):
+                a, b = grads[tl], grads[steps + tl]
+                gk_ref[tl, g, here] = jnp.where(mine, a, b)
+                gs_ref[tl, g, here] = jnp.where(mine, b, a)
+                if h is not None:
+                    a, b = res[tl], res[steps + tl]
+                    rk_ref[tl, h, here] = jnp.where(mine, a, b)
+                    rs_ref[tl, h, here] = jnp.where(mine, b, a)
 
     def scan_own(h, strip):
         scan(
             strip,
-            lambda at, here: c_ref[h, at, here[0], here[1]],
-            lambda at, here: s_ref[h, at, here[0], here[1]],
+            lambda at, *here: c_ref[h, at, here[0], here[1]],
+            lambda at, *here: s_ref[h, at, here[0], here[1]],
             h + 1,
             h,
         )
 
     def scan_halo(n, strip, g, keep=None):
-        scan(strip, lambda at, here: halos[n][1][at, here[0], here[1]], None, g, None, keep)
+        scan(strip, lambda at, *here: halos[n][1][at, here[0], here[1]], None, g, None, keep)
 
     if two:
         flip = row == 1
@@ -426,7 +438,8 @@
 
 def forward(two, weights, taps, halo_taps, bias, thr, begun=()):
     x, s, c = taps
-    rows, times, cols, half = s.shape
+    rows, times = s.shape[:2]
+    cols, half = x.shape[1] // times, bias.shape[0] // 2
     steps = times // 2
     args = [weights, x, s, c] + [a for pair in halo_taps for a in pair] + [bias, thr, *begun]
     main, tail, _ = split_half(half)

time: 40.2 us -> 39.5 us (0.983)
  Pallas kernels: 21.6 us -> 20.9 us
    pallas_call x1, Pallas kernels: 5.48 us -> 4.76 us  [forward(): call(functools.partial(forward_kernel, two, bool(begun)), (grad, grad, re...]
  transfers between devices with their start and end apart: 11 -> 11, of which waited for: 4 -> 4; matrix products, arithmetic and copies ran while one was open for 0% -> 0% of each run, Pallas kernels for 43% -> 42%
where the time goes in v8:
time: 39.5 us; the launch traced here: 39.4 us
  Pallas kernels  20.9 us (53%)
  starting transfers between devices  12.2 us (31%)
  waiting for transfers between devices  5.25 us (13%)
  between operations  0.92 us (2%)
    pallas_call x1, Pallas kernels, build_taps(): call(taps_kernel, out, [VMEM_SPEC] * 4, 16, 'taps', cost=18 << 20)  5.17 us
    pallas_call x1, Pallas kernels, forward(): call(functools.partial(forward_kernel, two, bool(begun)), (grad, grad, re...  4.76 us
    ppermute x6, starting transfers between devices, swap_cores(): return lax.ppermute(x, 'tm', [(0, 1), (1, 0)])  4.2 us
    pallas_call x1, Pallas kernels, backward(): call(backward_kernel, (shape(cot.shape, F32), shape(cot.shape)), [VMEM_SP...  4.03 us
    ppermute x1, starting transfers between devices, fetch_halos(): return [lax.ppermute(halos[0], 'rows', [(0, 1), (1, 0)])]  2.99 us
    ppermute x1, waiting for transfers between devices, fetch_halos(): return [lax.ppermute(halos[0], 'rows', [(0, 1), (1, 0)])]  2.94 us
    pallas_call x1, Pallas kernels, partial_currents(): call(partial_kernel, out, [VMEM_SPEC] * 5, 12, 'partial', scratch)  2.3 us
    ppermute x2, starting transfers between devices, fetch_weights(): rounds = [lax.ppermute(send, ('dp', 'tm'), moved[k]) for k in range(h)]  2.24 us
  transfers between devices with their start and end apart: 11, of which 4 were waited for; matrix products, arithmetic and copies ran while one was open for 0% of the time, Pallas kernels for 42%

profile of v8, /device:TPU:0, one launch (start us, length us, event | category | flops | bytes accessed | tf_op | source)
XLA Modules:
  0.0 39.4 jit_solution(7238753392509161447)
XLA Ops:
  0.6 0.5 %collective-permute-start.2 = (bf16[3,8,64,320]{3,2,1,0:T(8,128)(2,1)}, bf16[3,8,64,320]{3,2,1,0:T(8,128)(2,1)S(1)}, u32[]{:S(2)}, u32[]{:S(2)}) collective-permute-start(bf16[3,8,64,320]{3,2,1,0:T(8,128)(2,1)} %bitcast.10), channel_id=1, source_target_pairs={{0,2},{2,0},{1,3},{3,1},{4,6},{6,4},{5,7},{7,5},{8,10},{10,8},{9,1... | collective-permute-start | bytes 2949128 | tf_op jit(solution)/shard_map/ppermute | solution.py:532
  1.1 0.1 collective-permute-start.3
  1.2 1.8 %prepare.1 = (bf16[4,240,256]{2,1,0:T(8,128)(2,1)S(1)}, bf16[480,256]{1,0:T(8,128)(2,1)S(1)}, bf16[3,3,64,320]{3,2,1,0:T(8,128)(2,1)S(1)}) custom-call(s32[3,3,80,320]{3,2,1,0:T(8,128)} %bitcast.13, s32[3,10,3,80]{3,2,1,0:T(4,128)} %bitcast.14, bf16[3,8,64,320]{3,2,1,0:T(8,128)(2,1)} %bitcast.11, bf16[3,8,64,320]{3,2,1,0:T(8,128)(2,1)} %bitcast.7), custom_call_target="tpu_custom_call" | custom-call | bytes 2097152 | tf_op jit(solution)/shard_map/prepare/pallas_call | solution.py:103
  3.0 3.0 %collective-permute-start.4 = (bf16[3,3,64,320]{3,2,1,0:T(8,128)(2,1)S(1)}, bf16[3,3,64,320]{3,2,1,0:T(8,128)(2,1)S(1)}, u32[]{:S(2)}, u32[]{:S(2)}) collective-permute-start(bf16[3,3,64,320]{3,2,1,0:T(8,128)(2,1)S(1)} %get-tuple-element.37), channel_id=1, source_target_pairs={{0,1},{1,0},{2,3},{3,2},{4,5},{5,4},{6,7},{7,6},{8,9},{9,8},{10,11... | collective-permute-start | bytes 1105928 | tf_op jit(solution)/shard_map/ppermute | solution.py:537
  6.0 1.6 %collective-permute-start.1 = (bf16[480,256]{1,0:T(8,128)(2,1)S(1)}, bf16[480,256]{1,0:T(8,128)(2,1)S(1)}, u32[]{:S(2)}, u32[]{:S(2)}) collective-permute-start(bf16[480,256]{1,0:T(8,128)(2,1)S(1)} %get-tuple-element.33), channel_id=1, source_target_pairs={{4,0},{12,2},{0,4},{8,6},{6,8},{14,10},{2,12},{10,14},{5,1},{13,3}... | collective-permute-start | bytes 737288 | tf_op jit(solution)/shard_map/ppermute | solution.py:278
  7.6 0.7 %collective-permute-start = (bf16[480,256]{1,0:T(8,128)(2,1)S(1)}, bf16[480,256]{1,0:T(8,128)(2,1)S(1)}, u32[]{:S(2)}, u32[]{:S(2)}) collective-permute-start(bf16[480,256]{1,0:T(8,128)(2,1)S(1)} %get-tuple-element.33), channel_id=1, source_target_pairs={{8,2},{12,6},{2,8},{6,12},{9,3},{13,7},{3,9},{7,13},{24,18},{28,22... | collective-permute-start | bytes 737288 | tf_op jit(solution)/shard_map/ppermute | solution.py:278
  8.3 5.2 %taps.1 = (bf16[8,384,1024]{2,1,0:T(8,128)(2,1)S(1)}, bf16[8,6,64,160]{3,2,1,0:T(8,128)(2,1)S(1)}, bf16[8,6,64,160]{3,2,1,0:T(8,128)(2,1)S(1)}) custom-call(bf16[3,8,64,320]{3,2,1,0:T(8,128)(2,1)S(1)} %bitcast.12, bf16[3,8,64,320]{3,2,1,0:T(8,128)(2,1)S(1)} %collective-permute-done.2.spikes2_ref, bf16[3,8,64,320]{3,2,1,0:T(8,128)(2,1)S(1)} %bitcast.8, ...), custom_call_target="tpu_custom_call" | custom-call | bytes 18874368 | tf_op jit(solution)/shard_map/taps/pallas_call | solution.py:153
  13.5 2.9 %collective-permute-done.4.halo_ref = bf16[3,3,64,320]{3,2,1,0:T(8,128)(2,1)S(1)} collective-permute-done((bf16[3,3,64,320]{3,2,1,0:T(8,128)(2,1)S(1)}, bf16[3,3,64,320]{3,2,1,0:T(8,128)(2,1)S(1)}, u32[]{:S(2)}, u32[]{:S(2)}) %collective-permute-start.4) | collective-permute-done | bytes 368672 | tf_op jit(solution)/shard_map/ppermute | solution.py:537
  16.4 0.5 %collective-permute-start.5 = (bf16[3,3,64,320]{3,2,1,0:T(8,128)(2,1)S(1)}, bf16[3,3,64,320]{3,2,1,0:T(8,128)(2,1)S(1)}, u32[]{:S(2)}, u32[]{:S(2)}) collective-permute-start(bf16[3,3,64,320]{3,2,1,0:T(8,128)(2,1)S(1)} %collective-permute-done.4.halo_ref), channel_id=1, source_target_pairs={{0,2},{2,0},{1,3},{3,1},{4,6},{6,4},{5,7},{7,5},{8,10},{10,8},{9,1... | collective-permute-start | bytes 1105928 | tf_op jit(solution)/shard_map/ppermute | solution.py:532
  17.0 1.6 %collective-permute-start.7 = (bf16[480,256]{1,0:T(8,128)(2,1)S(1)}, bf16[480,256]{1,0:T(8,128)(2,1)S(1)}, u32[]{:S(2)}, u32[]{:S(2)}) collective-permute-start(bf16[480,256]{1,0:T(8,128)(2,1)S(1)} %pad_maximum_fusion), channel_id=1, source_target_pairs={{0,16},{16,0},{1,17},{17,1},{2,18},{18,2},{3,19},{19,3},{4,20},{20... | collective-permute-start | bytes 737288 | tf_op jit(solution)/shard_map/ppermute | solution.py:283
  18.6 1.2 %collective-permute-start.6 = (bf16[480,256]{1,0:T(8,128)(2,1)S(1)}, bf16[480,256]{1,0:T(8,128)(2,1)S(1)}, u32[]{:S(2)}, u32[]{:S(2)}) collective-permute-start(bf16[480,256]{1,0:T(8,128)(2,1)S(1)} %pad_maximum_fusion), channel_id=1, source_target_pairs={{0,1},{1,0},{2,3},{3,2},{4,5},{5,4},{6,7},{7,6},{8,9},{9,8},{10,11... | collective-permute-start | bytes 737288 | tf_op jit(solution)/shard_map/ppermute | solution.py:282
  19.8 0.7 %halo_taps.1 = (bf16[2,384,1024]{2,1,0:T(8,128)(2,1)S(1)}, bf16[6,64,160]{2,1,0:T(8,128)(2,1)S(1)}) custom-call(bf16[3,3,64,320]{3,2,1,0:T(8,128)(2,1)S(1)} %collective-permute-done.4.halo_ref, bf16[3,3,64,320]{3,2,1,0:T(8,128)(2,1)S(1)} %collective-permute-done.5.halo2_ref), custom_call_target="tpu_custom_call" | custom-call | bytes 2097152 | tf_op jit(solution)/shard_map/halo_taps/pallas_call | solution.py:172
  20.5 2.3 %partial.1.refs_4_ = f32[11,384,512]{2,1,0:T(8,128)S(1)} custom-call(bf16[4,240,256]{2,1,0:T(8,128)(2,1)S(1)} %get-tuple-element.49.w_ref, bf16[480,256]{1,0:T(8,128)(2,1)S(1)} %collective-permute-done.first_ref, bf16[480,256]{1,0:T(8,128)(2,1)S(1)} %collective-permute-done.1.second_ref, bf16[8,384,1024]{2,1,0:T(8,128)(2,1)S(1)} %get-tuple-element.50.x_ref, ...), custom_call_target="tpu_custom_call" | custom-call | tf_op jit(solution)/shard_map/partial/pallas_call | solution.py:257
  22.8 0.0 copy-start.2
  22.8 0.5 %collective-permute-done.7.y_ref = bf16[480,256]{1,0:T(8,128)(2,1)S(1)} collective-permute-done((bf16[480,256]{1,0:T(8,128)(2,1)S(1)}, bf16[480,256]{1,0:T(8,128)(2,1)S(1)}, u32[]{:S(2)}, u32[]{:S(2)}) %collective-permute-start.7) | collective-permute-done | bytes 245792 | tf_op jit(solution)/shard_map/ppermute | solution.py:283
  23.2 1.5 %collective-permute-done.6.x_ref = bf16[480,256]{1,0:T(8,128)(2,1)S(1)} collective-permute-done((bf16[480,256]{1,0:T(8,128)(2,1)S(1)}, bf16[480,256]{1,0:T(8,128)(2,1)S(1)}, u32[]{:S(2)}, u32[]{:S(2)}) %collective-permute-start.6) | collective-permute-done | bytes 245792 | tf_op jit(solution)/shard_map/ppermute | solution.py:282
  24.8 0.3 join.1.w_ref
  25.1 2.5 %collective-permute-start.8 = (bf16[512,1024]{1,0:T(8,128)(2,1)S(1)}, bf16[512,1024]{1,0:T(8,128)(2,1)S(1)}, u32[]{:S(2)}, u32[]{:S(2)}) collective-permute-start(bf16[512,1024]{1,0:T(8,128)(2,1)S(1)} %join.1.w_ref), channel_id=1, source_target_pairs={{0,2},{2,0},{1,3},{3,1},{4,6},{6,4},{5,7},{7,5},{8,10},{10,8},{9,1... | collective-permute-start | bytes 3145736 | tf_op jit(solution)/shard_map/ppermute | solution.py:532
  27.6 4.8 %forward.1 = (bf16[3,10,80,128]{3,2,1,0:T(8,128)(2,1)S(1)}, bf16[3,10,80,128]{3,2,1,0:T(8,128)(2,1)S(1)}, bf16[3,8,80,128]{3,2,1,0:T(8,128)(2,1)S(1)}, bf16[3,8,80,128]{3,2,1,0:T(8,128)(2,1)S(1)}) custom-call(bf16[512,1024]{1,0:T(8,128)(2,1)S(1)} %join.1.w_ref, bf16[8,384,1024]{2,1,0:T(8,128)(2,1)S(1)} %get-tuple-element.50.x_ref, ...), custom_call_target="tpu_custom_call" | custom-call | bytes 25165824 | tf_op jit(solution)/shard_map/forward/pallas_call | solution.py:448
  32.3 0.1 collective-permute-start.9
  32.5 0.5 %collective-permute-start.10 = (bf16[3,8,80,128]{3,2,1,0:T(8,128)(2,1)S(1)}, bf16[3,8,80,128]{3,2,1,0:T(8,128)(2,1)S(1)}, u32[]{:S(2)}, u32[]{:S(2)}) collective-permute-start(bf16[3,8,80,128]{3,2,1,0:T(8,128)(2,1)S(1)} %get-tuple-element.59), channel_id=1, source_target_pairs={{0,2},{2,0},{1,3},{3,1},{4,6},{6,4},{5,7},{7,5},{8,10},{10,8},{9,1... | collective-permute-start | bytes 1474568 | tf_op jit(solution)/shard_map/ppermute | solution.py:532
  32.9 1.9 %backward_own.1.y_ref = f32[3,512,1024]{2,1,0:T(8,128)S(1)} custom-call(bf16[512,1024]{1,0:T(8,128)(2,1)S(1)} %join.1.w_ref, bf16[3,10,80,128]{3,2,1,0:T(8,128)(2,1)S(1)} %get-tuple-element.57.g_ref), custom_call_target="tpu_custom_call" | custom-call | bytes 6291456 | tf_op jit(solution)/shard_map/backward_own/pallas_call | solution.py:485
  34.8 0.3 collective-permute-done.10.rs_ref
  35.2 4.0 %backward.1 = (f32[3,8,64,320]{3,2,1,0:T(8,128)}, bf16[3,8,64,320]{3,2,1,0:T(8,128)(2,1)}) custom-call(bf16[512,1024]{1,0:T(8,128)(2,1)S(1)} %collective-permute-done.8.w_ref, bf16[3,10,80,128]{3,2,1,0:T(8,128)(2,1)S(1)} %collective-permute-done.9.g_ref, f32[3,512,1024]{2,1,0:T(8,128)S(1)} %backward_own.1.y_ref, bf16[3,8,64,320]{3,2,1,0:T(8,128)(2,1)S(1)} %bitcast.9, ...), custom_call_target="tpu_custom_call" | custom-call | tf_op jit(solution)/shard_map/backward/pallas_call | solution.py:516
  (17 shorter events, 0.1 us)
Async XLA Ops:
  0.6 7.6 %collective-permute-start.2 = (bf16[3,8,64,320]{3,2,1,0:T(8,128)(2,1)}, bf16[3,8,64,320]{3,2,1,0:T(8,128)(2,1)S(1)}, u32[]{:S(2)}, u32[]{:S(2)}) collective-permute-start(bf16[3,8,64,320]{3,2,1,0:T(8,128)(2,1)} %bitcast.10), channel_id=1, source_target_pairs={{0,2},{2,0},{1,3},{3,1},{4,6},{6,4},{5,7},{7,5},{8,10},{10,8},{9,1... | collective-permute-start | bytes 2949128 | tf_op jit(solution)/shard_map/ppermute | solution.py:532
  1.1 7.1 %collective-permute-start.3 = (bf16[3,8,64,320]{3,2,1,0:T(8,128)(2,1)}, bf16[3,8,64,320]{3,2,1,0:T(8,128)(2,1)S(1)}, u32[]{:S(2)}, u32[]{:S(2)}) collective-permute-start(bf16[3,8,64,320]{3,2,1,0:T(8,128)(2,1)} %bitcast.6), channel_id=1, source_target_pairs={{0,2},{2,0},{1,3},{3,1},{4,6},{6,4},{5,7},{7,5},{8,10},{10,8},{9,1... | collective-permute-start | bytes 2949128 | tf_op jit(solution)/shard_map/ppermute | solution.py:532
  1.2 7.0 %copy-start = (bf16[1,3,8,64,320]{4,3,2,1,0:T(8,128)(2,1)S(1)}, bf16[1,3,8,64,320]{4,3,2,1,0:T(8,128)(2,1)}, u32[]{:S(2)}) copy-start(bf16[1,3,8,64,320]{4,3,2,1,0:T(8,128)(2,1)} %param.7) | copy-start | bytes 2949124
  1.2 7.0 %copy-start.1 = (bf16[1,3,8,64,320]{4,3,2,1,0:T(8,128)(2,1)S(1)}, bf16[1,3,8,64,320]{4,3,2,1,0:T(8,128)(2,1)}, u32[]{:S(2)}) copy-start(bf16[1,3,8,64,320]{4,3,2,1,0:T(8,128)(2,1)} %param.6) | copy-start | bytes 2949124
  3.0 13.4 %collective-permute-start.4 = (bf16[3,3,64,320]{3,2,1,0:T(8,128)(2,1)S(1)}, bf16[3,3,64,320]{3,2,1,0:T(8,128)(2,1)S(1)}, u32[]{:S(2)}, u32[]{:S(2)}) collective-permute-start(bf16[3,3,64,320]{3,2,1,0:T(8,128)(2,1)S(1)} %get-tuple-element.37), channel_id=1, source_target_pairs={{0,1},{1,0},{2,3},{3,2},{4,5},{5,4},{6,7},{7,6},{8,9},{9,8},{10,11... | collective-permute-start | bytes 1105928 | tf_op jit(solution)/shard_map/ppermute | solution.py:537
  6.0 10.9 %collective-permute-start.1 = (bf16[480,256]{1,0:T(8,128)(2,1)S(1)}, bf16[480,256]{1,0:T(8,128)(2,1)S(1)}, u32[]{:S(2)}, u32[]{:S(2)}) collective-permute-start(bf16[480,256]{1,0:T(8,128)(2,1)S(1)} %get-tuple-element.33), channel_id=1, source_target_pairs={{4,0},{12,2},{0,4},{8,6},{6,8},{14,10},{2,12},{10,14},{5,1},{13,3}... | collective-permute-start | bytes 737288 | tf_op jit(solution)/shard_map/ppermute | solution.py:278
  7.6 9.4 %collective-permute-start = (bf16[480,256]{1,0:T(8,128)(2,1)S(1)}, bf16[480,256]{1,0:T(8,128)(2,1)S(1)}, u32[]{:S(2)}, u32[]{:S(2)}) collective-permute-start(bf16[480,256]{1,0:T(8,128)(2,1)S(1)} %get-tuple-element.33), channel_id=1, source_target_pairs={{8,2},{12,6},{2,8},{6,12},{9,3},{13,7},{3,9},{7,13},{24,18},{28,22... | collective-permute-start | bytes 737288 | tf_op jit(solution)/shard_map/ppermute | solution.py:278
  16.4 3.4 %collective-permute-start.5 = (bf16[3,3,64,320]{3,2,1,0:T(8,128)(2,1)S(1)}, bf16[3,3,64,320]{3,2,1,0:T(8,128)(2,1)S(1)}, u32[]{:S(2)}, u32[]{:S(2)}) collective-permute-start(bf16[3,3,64,320]{3,2,1,0:T(8,128)(2,1)S(1)} %collective-permute-done.4.halo_ref), channel_id=1, source_target_pairs={{0,2},{2,0},{1,3},{3,1},{4,6},{6,4},{5,7},{7,5},{8,10},{10,8},{9,1... | collective-permute-start | bytes 1105928 | tf_op jit(solution)/shard_map/ppermute | solution.py:532
  17.0 6.3 %collective-permute-start.7 = (bf16[480,256]{1,0:T(8,128)(2,1)S(1)}, bf16[480,256]{1,0:T(8,128)(2,1)S(1)}, u32[]{:S(2)}, u32[]{:S(2)}) collective-permute-start(bf16[480,256]{1,0:T(8,128)(2,1)S(1)} %pad_maximum_fusion), channel_id=1, source_target_pairs={{0,16},{16,0},{1,17},{17,1},{2,18},{18,2},{3,19},{19,3},{4,20},{20... | collective-permute-start | bytes 737288 | tf_op jit(solution)/shard_map/ppermute | solution.py:283
  18.6 6.2 %collective-permute-start.6 = (bf16[480,256]{1,0:T(8,128)(2,1)S(1)}, bf16[480,256]{1,0:T(8,128)(2,1)S(1)}, u32[]{:S(2)}, u32[]{:S(2)}) collective-permute-start(bf16[480,256]{1,0:T(8,128)(2,1)S(1)} %pad_maximum_fusion), channel_id=1, source_target_pairs={{0,1},{1,0},{2,3},{3,2},{4,5},{5,4},{6,7},{7,6},{8,9},{9,8},{10,11... | collective-permute-start | bytes 737288 | tf_op jit(solution)/shard_map/ppermute | solution.py:282
  22.8 4.8 %copy-start.2 = (f32[320]{0:T(512)S(1)}, f32[320]{0:T(512)}, u32[]{:S(2)}) copy-start(f32[320]{0:T(512)} %refs_2_.1) | copy-start | bytes 3844
  22.8 4.8 %copy-start.3 = (f32[320]{0:T(512)S(1)}, f32[320]{0:T(512)}, u32[]{:S(2)}) copy-start(f32[320]{0:T(512)} %refs_3_.1) | copy-start | bytes 3844
  25.1 10.1 %collective-permute-start.8 = (bf16[512,1024]{1,0:T(8,128)(2,1)S(1)}, bf16[512,1024]{1,0:T(8,128)(2,1)S(1)}, u32[]{:S(2)}, u32[]{:S(2)}) collective-permute-start(bf16[512,1024]{1,0:T(8,128)(2,1)S(1)} %join.1.w_ref), channel_id=1, source_target_pairs={{0,2},{2,0},{1,3},{3,1},{4,6},{6,4},{5,7},{7,5},{8,10},{10,8},{9,1... | collective-permute-start | bytes 3145736 | tf_op jit(solution)/shard_map/ppermute | solution.py:532
  32.3 2.8 %collective-permute-start.9 = (bf16[3,10,80,128]{3,2,1,0:T(8,128)(2,1)S(1)}, bf16[3,10,80,128]{3,2,1,0:T(8,128)(2,1)S(1)}, u32[]{:S(2)}, u32[]{:S(2)}) collective-permute-start(bf16[3,10,80,128]{3,2,1,0:T(8,128)(2,1)S(1)} %get-tuple-element.56), channel_id=1, source_target_pairs={{0,2},{2,0},{1,3},{3,1},{4,6},{6,4},{5,7},{7,5},{8,10},{10,8},{9,1... | collective-permute-start | bytes 1843208 | tf_op jit(solution)/shard_map/ppermute | solution.py:532
  32.5 2.7 %collective-permute-start.10 = (bf16[3,8,80,128]{3,2,1,0:T(8,128)(2,1)S(1)}, bf16[3,8,80,128]{3,2,1,0:T(8,128)(2,1)S(1)}, u32[]{:S(2)}, u32[]{:S(2)}) collective-permute-start(bf16[3,8,80,128]{3,2,1,0:T(8,128)(2,1)S(1)} %get-tuple-element.59), channel_id=1, source_target_pairs={{0,2},{2,0},{1,3},{3,1},{4,6},{6,4},{5,7},{7,5},{8,10},{10,8},{9,1... | collective-permute-start | bytes 1474568 | tf_op jit(solution)/shard_map/ppermute | solution.py:532
